TPU v7x, 256 devices: a whole 4x4x8 slice. The times are simulated.
256 devices in a mesh: dp: 16 (over y, x_lo, core), space: 16 (over z, x_hi).
Axes of the slice: x: 4 (x_hi: 2, x_lo: 2; x = x_hi * 2 + x_lo), y: 4, z: 8, core: 2. Of those that a mesh axis runs over, the one named last changes fastest.
Arguments:
- images: bfloat16 [16, 64, 128, 1024], P('dp', 'space'), may hold values from -18 to 18
- teacher: bfloat16 [16, 64, 128, 1024], P('dp', 'space'), may hold values from 0 to 400
- w_reduce: bfloat16 [1024, 256], replicated, may hold values from -0.1875 to 0.1875
- w_spatial: bfloat16 [3, 3, 256, 256], replicated, may hold values from -0.125 to 0.125
- w_expand: bfloat16 [256, 1024], replicated, may hold values from -0.375 to 0.375
- partners: int32 [2, 16], replicated, may hold values from 0 to 15, as said below
Outputs:
- distill_loss: float32 [], replicated
- grad_images: bfloat16 [16, 64, 128, 1024], P('dp', 'space')
- grad_reduce: float32 [16, 1024, 256], P('dp', 'space')
- grad_spatial: float32 [16, 3, 3, 256, 256], P('dp', None, None, None, 'space')
- grad_expand: float32 [16, 256, 1024], P('dp', None, 'space')
Inputs may be any that keep to these rules, and one draw needn't show every extreme that they name: partners[r, i] = i XOR m_r for a round value m_r of 1 to 15, the m_r distinct over rounds; so each round pairs the images and partners[r, partners[r, i]] = i.
All inputs are finite; a program needn't handle non-finite values.
Results may differ from a plain program's by a relative error of at most 0.019.
The roundings to bfloat16 on the way count: a program that leaves them out, or rounds other values in their place, can miss the bound.
Values may be sent and summed in bfloat16 or wider, within the bound.
No kernel may reach another device: no remote copies, remote signals or barrier semaphores. Data moves between devices by JAX's collectives and lax.ppermute only.
A program may use at most 64 MiB of HBM per device.

v0:
```python
import jax
import jax.numpy as jnp
from jax import lax
from jax.sharding import PartitionSpec as P


def swapped(value, axis, stride):
    mask = 2**stride
    pairs = [(source, source ^ mask) for source in range(lax.axis_size(axis))]
    return lax.ppermute(value, axis, pairs)


def extended(shard, sides, width):
    for axis, dim in sides:
        peers, length = (lax.axis_size(axis), shard.shape[dim])
        up = [(i, (i + 1) % peers) for i in range(peers - 1)]
        down = [(j, i) for i, j in up]
        last = lax.slice_in_dim(shard, length - width, length, axis=dim)
        initial = lax.slice_in_dim(shard, 0, width, axis=dim)
        before = lax.ppermute(last, axis, up)
        after = lax.ppermute(initial, axis, down)
        shard = jnp.concatenate([before, shard, after], axis=dim)
    return shard


def fetch_pair(payload, round_mask, nbits_total):
    for bit_index in range(nbits_total):
        moved = swapped(payload, "dp", bit_index)
        payload = jnp.where((round_mask >> bit_index) % 2 == 1, moved, payload)
    return payload


def inner_product(first, second):
    return jnp.dot(first.reshape(-1), second.reshape(-1), preferred_element_type=jnp.float32)


def body(images, teacher, w_reduce, w_spatial, w_expand, partners):
    _, row_count, col_count, channels = images.shape
    hidden = w_reduce.shape[1]
    rounds_total = partners.shape[0]
    nbits_total = lax.axis_size("dp").bit_length() - 1
    elems_total = row_count * lax.axis_size("space") * col_count * channels
    round_masks = [partners[round_index, 0] for round_index in range(rounds_total)]
    flat_x = images.reshape(-1, channels)
    h_one = jax.nn.relu(jnp.dot(flat_x, w_reduce, preferred_element_type=jnp.float32)).astype(
        jnp.bfloat16
    )
    h_one_img = h_one.reshape(1, row_count, col_count, hidden)
    pad_one = extended(h_one_img, (("space", 1),), 1)
    pad_one = jnp.pad(pad_one, ((0, 0), (0, 0), (1, 1), (0, 0)))
    patches = jnp.concatenate(
        [
            pad_one[:, row_step : row_step + row_count, col_step : col_step + col_count, :]
            for row_step in range(3)
            for col_step in range(3)
        ],
        axis=-1,
    ).reshape(-1, 9 * hidden)
    h_two = jax.nn.relu(
        jnp.dot(patches, w_spatial.reshape(9 * hidden, hidden), preferred_element_type=jnp.float32)
    ).astype(jnp.bfloat16)
    pre_act = jnp.dot(h_two, w_expand, preferred_element_type=jnp.float32) + flat_x.astype(
        jnp.float32
    )
    student = jax.nn.relu(pre_act).astype(jnp.bfloat16)
    student_img = student.reshape(images.shape)
    partner_student = []
    partner_teacher = []
    stacked = jnp.stack([student_img, teacher])
    for round_index in range(rounds_total):
        received = fetch_pair(stacked, round_masks[round_index], nbits_total)
        partner_student.append(received[0])
        partner_teacher.append(received[1])
    self_student = inner_product(student_img, student_img)
    self_teacher = inner_product(teacher, teacher)
    sum_student, sum_teacher = lax.psum((self_student, self_teacher), "space")
    list_student = [sum_student]
    list_teacher = [sum_teacher]
    for round_index in range(rounds_total):
        cross_student, cross_teacher = lax.psum(
            (
                inner_product(student_img, partner_student[round_index]),
                inner_product(teacher, partner_teacher[round_index]),
            ),
            "space",
        )
        list_student.append(cross_student)
        list_teacher.append(cross_teacher)
    v_student = jnp.stack(list_student)
    v_teacher = jnp.stack(list_teacher)
    nu_student = jnp.sqrt(jnp.sum(v_student * v_student) + 1e-06)
    nu_teacher = jnp.sqrt(jnp.sum(v_teacher * v_teacher) + 1e-06)
    n_student = v_student / nu_student
    n_teacher = v_teacher / nu_teacher
    diff = n_student - n_teacher
    loss_term = jnp.sum(diff * diff)
    err_vec = 2.0 * diff
    coefs = (err_vec - jnp.sum(err_vec * n_student) * n_student) / nu_student
    coef_table, loss_terms = (
        lax.all_gather(coefs[None, :], "dp", axis=0, tiled=True),
        lax.all_gather(loss_term[None], "dp", axis=0, tiled=True),
    )
    distill_loss = jnp.sum(loss_terms)
    position = lax.axis_index("dp")
    ranks = jnp.arange(coef_table.shape[0], dtype=jnp.int32)
    summed = 2.0 * coefs[0] * student.astype(jnp.float32)
    for round_index in range(rounds_total):
        partner = jnp.sum(jnp.where(ranks == position, partners[round_index], 0))
        other_coef = jnp.sum(jnp.where(ranks == partner, coef_table[:, round_index + 1], 0.0))
        weight = coefs[round_index + 1] + other_coef
        summed = summed + weight * partner_student[round_index].reshape(-1, channels).astype(
            jnp.float32
        )
    grad_student = (elems_total * summed).astype(jnp.bfloat16)
    g_pre = jnp.where(student > 0, grad_student, jnp.zeros_like(grad_student))
    local_expand = jnp.dot(h_two.T, g_pre, preferred_element_type=jnp.float32)
    back_two = jnp.dot(g_pre, w_expand.T, preferred_element_type=jnp.float32)
    g_two = jnp.where(h_two > 0, back_two, 0.0).astype(jnp.bfloat16)
    local_spatial = jnp.dot(patches.T, g_two, preferred_element_type=jnp.float32).reshape(
        3, 3, hidden, hidden
    )
    pad_grad = extended(g_two.reshape(1, row_count, col_count, hidden), (("space", 1),), 1)
    pad_grad = jnp.pad(pad_grad, ((0, 0), (0, 0), (1, 1), (0, 0)))
    grad_patches = jnp.concatenate(
        [
            pad_grad[
                :,
                2 - row_step : 2 - row_step + row_count,
                2 - col_step : 2 - col_step + col_count,
                :,
            ]
            for row_step in range(3)
            for col_step in range(3)
        ],
        axis=-1,
    ).reshape(-1, 9 * hidden)
    w_back = jnp.concatenate(
        [w_spatial[row_step, col_step].T for row_step in range(3) for col_step in range(3)], axis=0
    )
    back_one = jnp.dot(grad_patches, w_back, preferred_element_type=jnp.float32)
    g_one = jnp.where(h_one > 0, back_one, 0.0).astype(jnp.bfloat16)
    local_reduce = jnp.dot(flat_x.T, g_one, preferred_element_type=jnp.float32)
    grad_images = (
        (g_pre.astype(jnp.float32) + jnp.dot(g_one, w_reduce.T, preferred_element_type=jnp.float32))
        .astype(jnp.bfloat16)
        .reshape(images.shape)
    )
    grad_spatial = lax.psum_scatter(
        local_spatial[None].astype(jnp.bfloat16), "space", scatter_dimension=4, tiled=True
    ).astype(jnp.float32)
    grad_reduce, grad_expand = (
        lax.psum_scatter(
            local_reduce[None].astype(jnp.bfloat16), "space", scatter_dimension=1, tiled=True
        ).astype(jnp.float32),
        lax.psum_scatter(
            local_expand[None].astype(jnp.bfloat16), "space", scatter_dimension=2, tiled=True
        ).astype(jnp.float32),
    )
    return (distill_loss, grad_images, grad_reduce, grad_spatial, grad_expand)


def solution(mesh):
    return jax.shard_map(
        body,
        mesh=mesh,
        in_specs=(P("dp", "space", None, None), P("dp", "space", None, None), P(), P(), P(), P()),
        out_specs=(
            P(),
            P("dp", "space", None, None),
            P("dp", "space", None),
            P("dp", None, None, None, "space"),
            P("dp", None, "space"),
        ),
        check_vma=False,
    )
```

profile of v0, /device:TPU:8, one launch (start us, length us, event | category | flops | bytes accessed | tf_op | source)
XLA Modules:
  0.0 951.0 jit_solution(15935390419554184665)
XLA Ops:
  7.2 1.8 fusion.13
  9.1 4.9 collective-permute-start
  14.0 1.3 collective-permute-start.1
  15.9 5.8 collective-permute-done.1
  22.3 1.3 copy-done.6
  23.6 0.8 fusion.14
  24.8 1.3 fusion.2
  26.1 1.5 pad_maximum_fusion
  29.5 2.6 collective-permute-done.2
  32.1 3.9 broadcast_select_fusion
  36.6 1.4 collective-permute-start.3
  38.7 46.1 %collective-permute-done.6 = bf16[2,1,4,128,1024]{4,3,2,1,0:T(8,128)(2,1)} collective-permute-done((bf16[2,1,4,128,1024]{4,3,2,1,0:T(8,128)(2,1)}, bf16[2,1,4,128,1024]{4,3,2,1,0:T(8,128)(2,1)}, u32[]{:S(2)}, u32[]{:S(2)}) %collective-permute-start.6) | collective-permute-done | bytes 2097184 | tf_op jit(solution)/shard_map/ppermute | solution.py:10
  84.8 3.2 broadcast_select_fusion.1
  89.1 39.8 %collective-permute-done.3 = bf16[2,1,4,128,1024]{4,3,2,1,0:T(8,128)(2,1)} collective-permute-done((bf16[2,1,4,128,1024]{4,3,2,1,0:T(8,128)(2,1)}, bf16[2,1,4,128,1024]{4,3,2,1,0:T(8,128)(2,1)}, u32[]{:S(2)}, u32[]{:S(2)}) %collective-permute-start.3) | collective-permute-done | bytes 2097184 | tf_op jit(solution)/shard_map/ppermute | solution.py:10
  128.9 3.1 broadcast_select_fusion.5
  133.9 1.2 fusion.9
  135.1 1.6 bitcast_dynamic-update-slice_fusion.8
  136.7 1.6 bitcast_dynamic-update-slice_fusion.7
  138.3 3.2 broadcast_select_fusion.2
  141.4 2.6 collective-permute-start.8
  144.0 1.6 bitcast_dynamic-update-slice_fusion.6
  145.6 35.3 %collective-permute-done.4 = bf16[2,1,4,128,1024]{4,3,2,1,0:T(8,128)(2,1)} collective-permute-done((bf16[2,1,4,128,1024]{4,3,2,1,0:T(8,128)(2,1)}, bf16[2,1,4,128,1024]{4,3,2,1,0:T(8,128)(2,1)}, u32[]{:S(2)}, u32[]{:S(2)}) %collective-permute-start.4) | collective-permute-done | bytes 2097184 | tf_op jit(solution)/shard_map/ppermute | solution.py:10
  180.9 3.1 broadcast_select_fusion.6
  184.1 2.3 collective-permute-start.5
  188.6 1.0 copy-done.7
  191.0 0.7 bitcast_dynamic-update-slice_fusion.3
  193.0 0.7 bitcast_dynamic-update-slice_fusion
  194.0 32.9 %collective-permute-done.8 = bf16[2,1,4,128,1024]{4,3,2,1,0:T(8,128)(2,1)} collective-permute-done((bf16[2,1,4,128,1024]{4,3,2,1,0:T(8,128)(2,1)}, bf16[2,1,4,128,1024]{4,3,2,1,0:T(8,128)(2,1)}, u32[]{:S(2)}, u32[]{:S(2)}) %collective-permute-start.8) | collective-permute-done | bytes 2097184 | tf_op jit(solution)/shard_map/ppermute | solution.py:10
  226.9 1.8 broadcast_select_fusion.3
  228.9 1.1 copy-done.2
  230.5 39.6 %collective-permute-done.5 = bf16[2,1,4,128,1024]{4,3,2,1,0:T(8,128)(2,1)} collective-permute-done((bf16[2,1,4,128,1024]{4,3,2,1,0:T(8,128)(2,1)}, bf16[2,1,4,128,1024]{4,3,2,1,0:T(8,128)(2,1)}, u32[]{:S(2)}, u32[]{:S(2)}) %collective-permute-start.5) | collective-permute-done | bytes 2097184 | tf_op jit(solution)/shard_map/ppermute | solution.py:10
  270.1 1.8 broadcast_select_fusion.7
  272.2 1.2 copy-done.3
  273.9 2.0 fusion
  275.9 43.4 %all-reduce.4 = (f32[]{:T(128)}, f32[]{:T(128)}, f32[]{:T(128)}, f32[]{:T(128)}, f32[]{:T(128)}, /*index=5*/f32[]{:T(128)}) all-reduce(f32[]{:T(128)} %get-tuple-element.75, f32[]{:T(128)} %get-tuple-element.76, f32[]{:T(128)} %get-tuple-element.73, f32[]{:T(128)} %get-tuple-element.21, ...), channel_id=1, replica_groups=mesh['dp'=16,'space'=16] {'space'}, use_global_device_ids=true, to_apply=%region_2.3 | all-reduce | flops 6 | bytes 48 | tf_op jit(solution)/shard_map/psum | solution.py:80
  319.3 2.6 multiply_reduce_fusion.3
  322.7 2.6 multiply_reduce_fusion.2
  326.6 4.5 divide_bitcast_fusion
  331.1 16.0 %all-gather = f32[16,1,3]{2,1,0:T(1,128)S(1)} all-gather(f32[1,1,3]{2,1,0:T(1,128)S(1)} %divide_bitcast_fusion), channel_id=1, replica_groups=mesh['dp'=16,'space'=16] {'dp'}, dimensions={0}, use_global_device_ids=true | all-gather | bytes 204 | tf_op jit(solution)/shard_map/all_gather | solution.py:100
  348.3 1.8 fusion.22
  351.4 2.8 convert_multiply_fusion.8
  355.6 1.6 convert_multiply_fusion.7
  359.1 1.3 collective-permute-start.10
  360.4 6.1 collective-permute-start.9
  366.9 2.0 copy.50
  368.9 2.1 copy.62
  371.7 1.0 copy-done.11
  372.7 0.8 fusion.15
  374.4 2.0 copy.48
  376.4 2.1 copy.63
  378.6 4.3 copy.22
  382.9 3.5 fusion.10
  386.4 3.7 copy.23
  392.0 1.4 dynamic-update-slice
  393.3 25.2 %all-reduce.2 = f32[16]{0:T(128)S(1)} all-reduce(f32[16]{0:T(128)S(1)} %dynamic-update-slice), channel_id=1, replica_groups=mesh['dp'=16,'space'=16] {'dp'}, use_global_device_ids=true, to_apply=%add.2 | all-reduce | flops 16 | bytes 128
  419.2 1.4 add_convert_fusion
  420.6 153.3 %reduce-scatter.9.cloned.1.call-done = bf16[64,256]{1,0:T(8,128)(2,1)} async-done(((bf16[1024,256]{1,0:T(8,128)(2,1)}), bf16[64,256]{1,0:T(8,128)(2,1)}) %reduce-scatter.9.cloned.1.call-update) | async-done | bytes 32784
  573.9 0.8 reshape_bitcast_fusion
  574.8 0.7 copy.26
  575.6 202.9 %reduce-scatter.7.cloned.1.call-done = bf16[64,256]{1,0:T(8,128)(2,1)} async-done(((bf16[1024,256]{1,0:T(8,128)(2,1)}), bf16[64,256]{1,0:T(8,128)(2,1)}) %reduce-scatter.7.cloned.1.call-update) | async-done | bytes 32784
  778.5 0.8 reshape_bitcast_fusion.1
  779.4 0.7 copy.24
  780.1 162.7 %all-reduce.7.cloned.1.call-done = bf16[1,3,3,256,256]{3,2,1,0,4:T(4,128)(2,1)} async-done(((bf16[1,3,3,256,256]{3,2,1,0,4:T(4,128)(2,1)}), bf16[1,3,3,256,256]{3,2,1,0,4:T(4,128)(2,1)}) %all-reduce.7.cloned.1.call-update) | async-done | bytes 1179664
  942.8 0.9 dynamic-slice_convert_fusion
  (94 shorter events, 16.6 us)
Async XLA Ops:
  7.2 17.2 %copy-start = (bf16[256,1024]{1,0:T(8,128)(2,1)S(1)}, bf16[256,1024]{1,0:T(8,128)(2,1)}, u32[]{:S(2)}) copy-start(bf16[256,1024]{1,0:T(8,128)(2,1)} %param.10) | copy-start | bytes 1572868
  7.2 566.7 %reduce-scatter.9.cloned.1.call-start = ((), (), s32[]{:S(2)}) async-start(), calls=%async_computation.3 | async-start | bytes 557056
  9.1 6.8 collective-permute-start
  14.0 7.7 collective-permute-start.1
  22.0 1.5 copy-start.6
  22.3 2.1 copy-start.5
  23.6 1.2 copy-start.8
  24.8 1.3 copy-start.1
  26.1 1.5 copy-start.12
  27.6 4.5 collective-permute-start.2
  36.0 48.8 %collective-permute-start.6 = (bf16[2,1,4,128,1024]{4,3,2,1,0:T(8,128)(2,1)}, bf16[2,1,4,128,1024]{4,3,2,1,0:T(8,128)(2,1)}, u32[]{:S(2)}, u32[]{:S(2)}) collective-permute-start(bf16[2,1,4,128,1024]{4,3,2,1,0:T(8,128)(2,1)} %get-tuple-element.42), channel_id=1, source_target_pairs={{0,32},{16,48},{32,0},{48,16},{64,96},{80,112},{96,64},{112,80},{1... | collective-permute-start | bytes 6291464 | tf_op jit(solution)/shard_map/ppermute | solution.py:10
  36.6 92.3 %collective-permute-start.3 = (bf16[2,1,4,128,1024]{4,3,2,1,0:T(8,128)(2,1)}, bf16[2,1,4,128,1024]{4,3,2,1,0:T(8,128)(2,1)}, u32[]{:S(2)}, u32[]{:S(2)}) collective-permute-start(bf16[2,1,4,128,1024]{4,3,2,1,0:T(8,128)(2,1)} %get-tuple-element.43), channel_id=1, source_target_pairs={{0,32},{16,48},{32,0},{48,16},{64,96},{80,112},{96,64},{112,80},{1... | collective-permute-start | bytes 6291464 | tf_op jit(solution)/shard_map/ppermute | solution.py:10
  88.0 50.3 %collective-permute-start.7 = (bf16[2,1,4,128,1024]{4,3,2,1,0:T(8,128)(2,1)}, bf16[2,1,4,128,1024]{4,3,2,1,0:T(8,128)(2,1)}, u32[]{:S(2)}, u32[]{:S(2)}) collective-permute-start(bf16[2,1,4,128,1024]{4,3,2,1,0:T(8,128)(2,1)} %broadcast_select_fusion.1), channel_id=1, source_target_pairs={{0,64},{16,80},{32,96},{48,112},{64,0},{80,16},{96,32},{112,48},{1... | collective-permute-start | bytes 6291464 | tf_op jit(solution)/shard_map/ppermute | solution.py:10
  132.1 48.8 %collective-permute-start.4 = (bf16[2,1,4,128,1024]{4,3,2,1,0:T(8,128)(2,1)}, bf16[2,1,4,128,1024]{4,3,2,1,0:T(8,128)(2,1)}, u32[]{:S(2)}, u32[]{:S(2)}) collective-permute-start(bf16[2,1,4,128,1024]{4,3,2,1,0:T(8,128)(2,1)} %broadcast_select_fusion.5), channel_id=1, source_target_pairs={{0,64},{16,80},{32,96},{48,112},{64,0},{80,16},{96,32},{112,48},{1... | collective-permute-start | bytes 6291464 | tf_op jit(solution)/shard_map/ppermute | solution.py:10
  141.4 85.4 %collective-permute-start.8 = (bf16[2,1,4,128,1024]{4,3,2,1,0:T(8,128)(2,1)}, bf16[2,1,4,128,1024]{4,3,2,1,0:T(8,128)(2,1)}, u32[]{:S(2)}, u32[]{:S(2)}) collective-permute-start(bf16[2,1,4,128,1024]{4,3,2,1,0:T(8,128)(2,1)} %broadcast_select_fusion.2), channel_id=1, source_target_pairs={{0,128},{16,144},{32,160},{48,176},{64,192},{80,208},{96,224},{112... | collective-permute-start | bytes 6291464 | tf_op jit(solution)/shard_map/ppermute | solution.py:10
  184.1 86.1 %collective-permute-start.5 = (bf16[2,1,4,128,1024]{4,3,2,1,0:T(8,128)(2,1)}, bf16[2,1,4,128,1024]{4,3,2,1,0:T(8,128)(2,1)}, u32[]{:S(2)}, u32[]{:S(2)}) collective-permute-start(bf16[2,1,4,128,1024]{4,3,2,1,0:T(8,128)(2,1)} %broadcast_select_fusion.6), channel_id=1, source_target_pairs={{0,128},{16,144},{32,160},{48,176},{64,192},{80,208},{96,224},{112... | collective-permute-start | bytes 6291464 | tf_op jit(solution)/shard_map/ppermute | solution.py:10
  188.3 1.3 copy-start.7
  228.7 1.3 copy-start.2
  272.0 1.3 copy-start.3
  355.6 2.3 copy-start.4
  359.1 12.0 %collective-permute-start.10 = (bf16[1,1,128,256]{3,2,1,0:T(8,128)(2,1)S(1)}, bf16[1,1,128,256]{3,2,1,0:T(8,128)(2,1)S(1)}, u32[]{:S(2)}, u32[]{:S(2)}) collective-permute-start(bf16[1,1,128,256]{3,2,1,0:T(8,128)(2,1)S(1)} %get-tuple-element.63), channel_id=1, source_target_pairs={{1,0},{2,1},{3,2},{4,3},{5,4},{6,5},{7,6},{8,7},{9,8},{10,9},{11,1... | collective-permute-start | bytes 196616 | tf_op jit(solution)/shard_map/ppermute | solution.py:21
  360.4 10.7 %collective-permute-start.9 = (bf16[1,1,128,256]{3,2,1,0:T(8,128)(2,1)S(1)}, bf16[1,1,128,256]{3,2,1,0:T(8,128)(2,1)S(1)}, u32[]{:S(2)}, u32[]{:S(2)}) collective-permute-start(bf16[1,1,128,256]{3,2,1,0:T(8,128)(2,1)S(1)} %get-tuple-element.62), channel_id=1, source_target_pairs={{0,1},{1,2},{2,3},{3,4},{4,5},{5,6},{6,7},{7,8},{8,9},{9,10},{10,1... | collective-permute-start | bytes 196616 | tf_op jit(solution)/shard_map/ppermute | solution.py:20
  371.0 407.5 %reduce-scatter.7.cloned.1.call-start = ((), (), s32[]{:S(2)}) async-start(), calls=%async_computation.2 | async-start | bytes 557056
  371.5 1.3 copy-start.11
  372.7 1.2 copy-start.9
  378.6 564.3 %all-reduce.7.cloned.1.call-start = ((), (), s32[]{:S(2)}) async-start(), calls=%async_computation.4 | async-start | bytes 3145728
  386.4 3.7 copy-start.14
  386.4 5.0 copy-start.13
  386.4 32.8 %copy-start.10 = (bf16[1024,256]{1,0:T(8,128)(2,1)S(1)}, bf16[1024,256]{1,0:T(8,128)(2,1)}, u32[]{:S(2)}) copy-start(bf16[1024,256]{1,0:T(8,128)(2,1)} %param.8) | copy-start | bytes 1572868
Sparse Core Ops, SparseCore 0:
  371.1 202.7 reduce-scatter.8
  577.7 200.7 reduce-scatter.6
  781.1 161.6 all-reduce.6
where the time goes:
time: 952 us; the launch traced here: 951 us
  waiting for transfers between devices  722 us (76%)
  blocking collectives  84.7 us (9%)
  other arithmetic  45.3 us (5%)
  local copies, waits for them, and re-layouts  41.9 us (4%)
  between operations  24.9 us (3%)
  starting transfers between devices  21.5 us (2%)
  matrix products  11.1 us (1%)
    unnamed x6, waiting for transfers between devices  519 us
    ppermute x7, waiting for transfers between devices, swapped(): return lax.ppermute(value, axis, pairs)  196 us
    psum x1, blocking collectives, body(): lax.psum((inner_product(student_img, partner_student[round_index]), inner...  43.4 us
    unnamed x75, local copies, waits for them, and re-layouts  31.3 us
    unnamed x1, blocking collectives  25.2 us
    select_n x7, other arithmetic, fetch_pair(): payload = jnp.where((round_mask >> bit_index) % 2 == 1, moved, payload)  20.2 us
  transfers between devices with their start and end apart: 14, of which 11 were waited for; matrix products, arithmetic and copies ran while one was open for 6% of the time, Pallas kernels for 0%

commit v1 on v0

v1 whole, which is shorter than its diff:
```python
import functools

import jax
import jax.numpy as jnp
from jax import lax
from jax.experimental import pallas as pl
from jax.experimental.pallas import tpu as pltpu
from jax.sharding import PartitionSpec as P

F32 = jnp.float32
BF16 = jnp.bfloat16
ROW_DOT = (((1,), (0,)), ((), ()))
LAST_DOT = (((1,), (1,)), ((), ()))
FIRST_DOT = (((0,), (0,)), ((), ()))


def dot(left, right, dims):
    return lax.dot_general(left, right, dims, preferred_element_type=F32)


def flat(value):
    return value.reshape(-1, value.shape[-1])


def shifted(value, step, cols):
    count = value.shape[0]
    moved = pltpu.roll(value, (-step) % count, 0)
    col = lax.broadcasted_iota(jnp.int32, value.shape, 0) % cols
    edge = cols - 1 if step == 1 else 0
    return jnp.where(col == edge, 0.0, moved)


def reduce_kernel(x_ref, w_ref, h_ref):
    acc = dot(x_ref[0], w_ref[...], ROW_DOT)
    h_ref[0] = jnp.maximum(acc, 0.0).astype(BF16)


def forward_kernel(
    h_ref, above_ref, below_ref, ws_ref, we_ref, x_ref, t_ref, hp_ref, h2_ref, st_ref
):
    rows, cols, mid = h_ref.shape
    devices, _, chunk, channels = st_ref.shape
    hp_ref[0] = above_ref[...]
    hp_ref[rows + 1] = below_ref[...]
    hp_ref[1 : rows + 1] = h_ref[...]
    sums = []
    for b in range(3):
        acc = None
        for a in range(3):
            part = dot(flat(hp_ref[a : a + rows]), ws_ref[a, b], ROW_DOT)
            acc = part if acc is None else acc + part
        sums.append(acc)
    total = sums[1] + shifted(sums[0], -1, cols) + shifted(sums[2], 1, cols)
    h_two = jnp.maximum(total, 0.0).astype(BF16)
    h2_ref[...] = h_two.reshape(rows, cols, mid)
    pre = dot(h_two, we_ref[...], ROW_DOT) + flat(x_ref[...]).astype(F32)
    st_ref[:, 0] = jnp.maximum(pre, 0.0).astype(BF16).reshape(devices, chunk, channels)
    st_ref[:, 1] = t_ref[...].reshape(devices, chunk, channels)


def gram_kernel(masks_ref, st_ref, out_ref):
    images, _, chunk, _ = st_ref.shape
    count = images * chunk
    row = lax.broadcasted_iota(jnp.int32, (count, count), 0)
    col = lax.broadcasted_iota(jnp.int32, (count, count), 1)
    same = (row % chunk) == (col % chunk)
    image = lax.broadcasted_iota(jnp.int32, (images, count), 0)
    other = lax.broadcasted_iota(jnp.int32, (images, count), 1) // chunk
    slot_row = lax.broadcasted_iota(jnp.int32, (images, 128), 0)
    slot = lax.broadcasted_iota(jnp.int32, (images, 128), 1)
    message = jnp.zeros((images, 128), F32)
    for which in range(2):
        value = flat(st_ref[:, which])
        gram = jnp.where(same, dot(value, value, LAST_DOT), 0.0)
        gram = gram.reshape(images, chunk, count).sum(axis=1)
        for k in range(3):
            partner = image if k == 0 else image ^ masks_ref[k - 1]
            column = jnp.where(other == partner, gram, 0.0).sum(axis=1, keepdims=True)
            message = message + jnp.where(slot == 8 * slot_row + 3 * which + k, column, 0.0)
    out_ref[...] = jnp.broadcast_to(message.sum(axis=0, keepdims=True), out_ref.shape)


def grad_kernel(scale, masks_ref, msg_ref, st_ref, g_ref, loss_ref):
    images = st_ref.shape[0]
    total = jnp.broadcast_to(msg_ref[...].sum(axis=0, keepdims=True), (images, 128))
    row = lax.broadcasted_iota(jnp.int32, (images, 128), 0)
    lane = lax.broadcasted_iota(jnp.int32, (images, 128), 1)

    def column(k):
        return jnp.where(lane == 8 * row + k, total, 0.0).sum(axis=1, keepdims=True)

    v_s = [column(k) for k in range(3)]
    v_t = [column(3 + k) for k in range(3)]
    nu_s = jnp.sqrt(v_s[0] * v_s[0] + v_s[1] * v_s[1] + v_s[2] * v_s[2] + 1e-06)
    nu_t = jnp.sqrt(v_t[0] * v_t[0] + v_t[1] * v_t[1] + v_t[2] * v_t[2] + 1e-06)
    n_s = [v / nu_s for v in v_s]
    diff = [a - b / nu_t for a, b in zip(n_s, v_t)]
    terms = diff[0] * diff[0] + diff[1] * diff[1] + diff[2] * diff[2]
    loss_ref[...] = terms.sum(axis=0, keepdims=True)
    err = [2.0 * d for d in diff]
    inner = err[0] * n_s[0] + err[1] * n_s[1] + err[2] * n_s[2]
    coefs = [(e - inner * n) / nu_s for e, n in zip(err, n_s)]
    weights = [2.0 * coefs[0]]
    for k in range(2):
        own = coefs[k + 1]
        as_row = jnp.where(row == lane, own, 0.0).sum(axis=0, keepdims=True)
        partner = row ^ masks_ref[k]
        theirs = jnp.where(lane == partner, as_row, 0.0).sum(axis=1, keepdims=True)
        weights.append(own + theirs)
    for i in range(images):
        own = st_ref[i, 0].astype(F32)
        acc = weights[0][i : i + 1] * own
        for k in range(2):
            acc = acc + weights[k + 1][i : i + 1] * st_ref[i ^ masks_ref[k], 0].astype(F32)
        g_ref[i] = jnp.where(own > 0.0, scale * acc, 0.0).astype(BF16)


def expand_kernel(g_ref, h2_ref, we_ref, g2_ref, ge_ref):
    grads = g_ref[...]
    h_two = flat(h2_ref[...])
    back = dot(grads, we_ref[...], LAST_DOT)
    g_two = jnp.where(h_two > 0, back, 0.0).astype(BF16)
    g2_ref[...] = g_two.reshape(g2_ref.shape)
    ge_ref[...] = dot(grads, h_two, FIRST_DOT).astype(BF16).reshape(ge_ref.shape)


def spatial_kernel(hp_ref, g2_ref, gs_ref):
    rows, cols, mid = g2_ref.shape
    chunks, _, _, width, _ = gs_ref.shape
    g_two = flat(g2_ref[...])
    wide = g_two.astype(F32)
    moved = [shifted(wide, 1, cols).astype(BF16), g_two, shifted(wide, -1, cols).astype(BF16)]
    for a in range(3):
        source = flat(hp_ref[a : a + rows])
        for b in range(3):
            part = dot(moved[b], source, FIRST_DOT).astype(BF16)
            gs_ref[:, a, b] = part.reshape(chunks, width, mid)


def backward_kernel(
    g2_ref, above_ref, below_ref, hp_ref, ws_ref, wr_ref, x_ref, g_ref, gr_ref, gi_ref, gp_ref
):
    rows, cols, mid = g2_ref.shape
    gp_ref[0] = above_ref[...]
    gp_ref[rows + 1] = below_ref[...]
    gp_ref[1 : rows + 1] = g2_ref[...]
    sums = []
    for b in range(3):
        acc = None
        for a in range(3):
            part = dot(flat(gp_ref[2 - a : 2 - a + rows]), ws_ref[a, b], LAST_DOT)
            acc = part if acc is None else acc + part
        sums.append(acc)
    total = sums[1] + shifted(sums[0], 1, cols) + shifted(sums[2], -1, cols)
    g_one = jnp.where(flat(hp_ref[1 : rows + 1]) > 0, total, 0.0).astype(BF16)
    gr_ref[...] = dot(flat(x_ref[...]), g_one, FIRST_DOT).astype(BF16).reshape(gr_ref.shape)
    back = dot(g_one, wr_ref[...], LAST_DOT)
    gi_ref[...] = (g_ref[...].astype(F32) + back).astype(BF16).reshape(gi_ref.shape)


def call(kernel, outs, smem=0, scratch=(), cost=None, name=None):
    def run(*args):
        return pl.pallas_call(
            kernel,
            out_shape=[jax.ShapeDtypeStruct(s, d) for s, d in outs],
            in_specs=[
                pl.BlockSpec(memory_space=pltpu.SMEM if i < smem else pltpu.VMEM)
                for i in range(len(args))
            ],
            out_specs=[pl.BlockSpec(memory_space=pltpu.VMEM) for _ in outs],
            scratch_shapes=list(scratch),
            compiler_params=pltpu.CompilerParams(vmem_limit_bytes=56 * 2**20),
            cost_estimate=cost,
            name=name,
        )(*args)

    return run


def cost(flops, nbytes):
    return pl.CostEstimate(flops=flops, bytes_accessed=nbytes, transcendentals=0)


def edges(value):
    peers = lax.axis_size("space")
    up = [(i, i + 1) for i in range(peers - 1)]
    down = [(i + 1, i) for i in range(peers - 1)]
    above = lax.ppermute(value[-1], "space", up)
    below = lax.ppermute(value[0], "space", down)
    return above, below


def scattered(local):
    peers = lax.axis_size("space")
    depth = peers // 2
    place = lax.axis_index("space")
    z, half = place // 2, place % 2
    ring_up = [(i, (i + 2) % peers) for i in range(peers)]
    ring_down = [(i, (i - 2) % peers) for i in range(peers)]

    def mine(block, side):
        return lax.dynamic_index_in_dim(local, 2 * (block % depth) + side, 0, keepdims=False)

    up = mine(z + depth - 1, 0)
    down = mine(z + 1, 1)
    for step in range(depth - 1):
        got_up = lax.ppermute(up, "space", ring_up)
        got_down = lax.ppermute(down, "space", ring_down)
        up = got_up.astype(F32) + mine(z + 2 * depth - 2 - step, 0).astype(F32)
        down = got_down.astype(F32) + mine(z + 2 + step, 1).astype(F32)
        if step < depth - 2:
            up, down = up.astype(BF16), down.astype(BF16)
    keep = jnp.where(half == 0, up, down)
    give = jnp.where(half == 0, down, up).astype(BF16)
    swap = [(i, i ^ 1) for i in range(peers)]
    return keep + lax.ppermute(give, "space", swap).astype(F32)


def body(images, teacher, w_reduce, w_spatial, w_expand, partners):
    _, rows, cols, channels = images.shape
    mid = w_reduce.shape[1]
    n_dp, n_space = lax.axis_size("dp"), lax.axis_size("space")
    pixels = rows * cols
    chunk = pixels // n_dp
    elems = float(rows * n_space * cols * channels)
    masks = partners[:, 0]
    x = images.reshape(rows, cols, channels)
    t = teacher.reshape(rows, cols, channels)

    h_one = pl.pallas_call(
        reduce_kernel,
        grid=(rows,),
        in_specs=[
            pl.BlockSpec((1, cols, channels), lambda r: (r, 0, 0)),
            pl.BlockSpec((channels, mid), lambda r: (0, 0)),
        ],
        out_specs=pl.BlockSpec((1, cols, mid), lambda r: (r, 0, 0)),
        out_shape=jax.ShapeDtypeStruct((rows, cols, mid), BF16),
        name="reduce",
    )(x, w_reduce)
    above, below = edges(h_one)
    h_pad, h_two, both = call(
        forward_kernel,
        [
            ((rows + 2, cols, mid), BF16),
            ((rows, cols, mid), BF16),
            ((n_dp, 2, chunk, channels), BF16),
        ],
        name="forward",
    )(h_one, above, below, w_spatial, w_expand, x, t)
    both = lax.all_to_all(both, "dp", 0, 0, tiled=True)
    world = n_dp * n_space
    (message,) = call(gram_kernel, [((world, 128), F32)], smem=1, name="gram")(masks, both)
    message = lax.all_to_all(message, ("dp", "space"), 0, 0, tiled=True)
    grads, loss = call(
        functools.partial(grad_kernel, elems),
        [((n_dp, chunk, channels), BF16), ((1, 1), F32)],
        smem=1,
        name="grad",
    )(masks, message, both)
    grads = lax.all_to_all(grads, "dp", 0, 0, tiled=True).reshape(pixels, channels)
    g_two, g_expand = call(
        expand_kernel,
        [((rows, cols, mid), BF16), ((n_space, channels // n_space, mid), BF16)],
        name="expand",
    )(grads, h_two, w_expand)
    above, below = edges(g_two)
    (g_spatial,) = call(
        spatial_kernel,
        [((n_space, 3, 3, mid // n_space, mid), BF16)],
        cost=cost(2 * 9 * pixels * mid * mid, 4 * pixels * mid),
        name="spatial",
    )(h_pad, g_two)
    g_reduce, g_images = call(
        backward_kernel,
        [((n_space, channels // n_space, mid), BF16), ((1, rows, cols, channels), BF16)],
        scratch=[pltpu.VMEM((rows + 2, cols, mid), BF16)],
        name="backward",
    )(g_two, above, below, h_pad, w_spatial, w_reduce, x, grads)
    part = channels // n_space
    local = jnp.concatenate(
        [g_expand, g_reduce, g_spatial.reshape(n_space, 9 * mid // n_space, mid)], axis=1
    )
    total = scattered(local)
    grad_expand = total[:part].T[None]
    grad_reduce = total[part : 2 * part][None]
    grad_spatial = total[2 * part :].reshape(3, 3, mid // n_space, mid).swapaxes(2, 3)[None]
    return loss[0, 0], g_images, grad_reduce, grad_spatial, grad_expand


def solution(mesh):
    return jax.shard_map(
        body,
        mesh=mesh,
        in_specs=(P("dp", "space", None, None), P("dp", "space", None, None), P(), P(), P(), P()),
        out_specs=(
            P(),
            P("dp", "space", None, None),
            P("dp", "space", None),
            P("dp", None, None, None, "space"),
            P("dp", None, "space"),
        ),
        check_vma=False,
    )
```

time: 952 us -> 194 us (0.20)
  waiting for transfers between devices: 722 us -> 72.7 us
  other arithmetic: 45.3 us -> 1.87 us
  blocking collectives: 84.7 us -> 47.7 us
  local copies, waits for them, and re-layouts: 41.9 us -> 6.38 us
  Pallas kernels: 0 us -> 27.4 us
  between operations: 24.9 us -> 0.83 us
  starting transfers between devices: 21.5 us -> 34.4 us
  matrix products: 11.1 us -> 0 us
    unnamed x6 -> x0, waiting for transfers between devices: 519 us -> none
    ppermute x11 -> x19, waiting for transfers between devices: 203 us -> 47.2 us  [the longest x7 19.6 us: scattered(): got_down = lax.ppermute(down, 'space', ring_down)]
    all_to_all x0 -> x2, blocking collectives: none -> 47.7 us  [the longest x1 28.3 us: body(): message = lax.all_to_all(message, ('dp', 'space'), 0, 0, tiled=True)]
    psum x1 -> x0, blocking collectives: 43.4 us -> none  [body(): lax.psum((inner_product(student_img, partner_student[round_index]), inner...]
    unnamed x75 -> x16, local copies, waits for them, and re-layouts: 31.3 us -> 2.63 us
    pallas_call x0 -> x7, Pallas kernels: none -> 27.4 us  [the longest x6 23.6 us: run(): pl.pallas_call(kernel, out_shape=[jax.ShapeDtypeStruct(s, d) for s, d in...]
    all_to_all x0 -> x1, waiting for transfers between devices: none -> 25.5 us  [body(): both = lax.all_to_all(both, 'dp', 0, 0, tiled=True)]
    unnamed x1 -> x0, blocking collectives: 25.2 us -> none
  transfers between devices with their start and end apart: 14 -> 20, of which waited for: 11 -> 18; matrix products, arithmetic and copies ran while one was open for 6% -> 0% of each run, Pallas kernels for 0% -> 2%
where the time goes in v1:
time: 194 us; the launch traced here: 191 us
  waiting for transfers between devices  72.7 us (37%)
  blocking collectives  47.7 us (25%)
  starting transfers between devices  34.4 us (18%)
  Pallas kernels  27.4 us (14%)
  local copies, waits for them, and re-layouts  6.38 us (3%)
    all_to_all x1, blocking collectives, body(): message = lax.all_to_all(message, ('dp', 'space'), 0, 0, tiled=True)  28.3 us
    all_to_all x1, waiting for transfers between devices, body(): both = lax.all_to_all(both, 'dp', 0, 0, tiled=True)  25.5 us
    pallas_call x6, Pallas kernels, run(): pl.pallas_call(kernel, out_shape=[jax.ShapeDtypeStruct(s, d) for s, d in...  23.6 us
    ppermute x7, waiting for transfers between devices, scattered(): got_down = lax.ppermute(down, 'space', ring_down)  19.6 us
    all_to_all x1, blocking collectives, body(): lax.all_to_all(grads, 'dp', 0, 0, tiled=True).reshape(pixels, channels)  19.4 us
    ppermute x7, waiting for transfers between devices, scattered(): got_up = lax.ppermute(up, 'space', ring_up)  14 us
    ppermute x7, starting transfers between devices, scattered(): got_up = lax.ppermute(up, 'space', ring_up)  9.21 us
    ppermute x2, waiting for transfers between devices, edges(): below = lax.ppermute(value[0], 'space', down)  9.12 us
  transfers between devices with their start and end apart: 20, of which 18 were waited for; matrix products, arithmetic and copies ran while one was open for 0% of the time, Pallas kernels for 2%

profile of v1, /device:TPU:8, one launch (start us, length us, event | category | flops | bytes accessed | tf_op | source)
XLA Modules:
  0.0 191.4 jit_solution(7101946837490162818)
XLA Ops:
  0.6 3.8 %reduce.3.h_ref = bf16[4,128,256]{2,1,0:T(8,128)(2,1)} custom-call(bf16[4,128,1024]{2,1,0:T(8,128)(2,1)} %bitcast.76, bf16[1024,256]{1,0:T(8,128)(2,1)} %wr_ref.1), custom_call_target="tpu_custom_call" | custom-call | tf_op jit(solution)/shard_map/reduce/pallas_call | solution.py:230
  4.5 0.9 slice_bitcast_fusion.2
  5.4 4.9 %collective-permute-start = (bf16[128,256]{1,0:T(8,128)(2,1)S(1)}, bf16[128,256]{1,0:T(8,128)(2,1)S(1)}, u32[]{:S(2)}, u32[]{:S(2)}) collective-permute-start(bf16[128,256]{1,0:T(8,128)(2,1)S(1)} %get-tuple-element.42), channel_id=1, source_target_pairs={{0,1},{1,2},{2,3},{3,4},{4,5},{5,6},{6,7},{7,8},{8,9},{9,10},{10,1... | collective-permute-start | bytes 196616 | tf_op jit(solution)/shard_map/ppermute | solution.py:188
  10.3 1.3 collective-permute-start.1
  11.6 0.6 collective-permute-done.above_ref
  12.2 5.8 %collective-permute-done.1.below_ref = bf16[128,256]{1,0:T(8,128)(2,1)S(1)} collective-permute-done((bf16[128,256]{1,0:T(8,128)(2,1)S(1)}, bf16[128,256]{1,0:T(8,128)(2,1)S(1)}, u32[]{:S(2)}, u32[]{:S(2)}) %collective-permute-start.1) | collective-permute-done | bytes 65568 | tf_op jit(solution)/shard_map/ppermute | solution.py:189
  18.0 0.6 copy-done.6
  18.6 4.9 %forward.1 = (bf16[6,128,256]{2,1,0:T(8,128)(2,1)}, bf16[4,128,256]{2,1,0:T(8,128)(2,1)}, bf16[16,2,32,1024]{3,2,1,0:T(8,128)(2,1)}) custom-call(bf16[4,128,256]{2,1,0:T(8,128)(2,1)} %reduce.3.h_ref, bf16[128,256]{1,0:T(8,128)(2,1)} %copy-done.5, bf16[128,256]{1,0:T(8,128)(2,1)} %copy-done.6, bf16[3,3,256,256]{3,2,1,0:T(8,128)(2,1)} %ws_ref.3, ...), custom_call_target="tpu_custom_call" | custom-call | tf_op jit(solution)/shard_map/forward/pallas_call | solution.py:163
  23.5 5.1 %all-to-all-start = ((bf16[16,2,32,1024]{3,2,1,0:T(8,128)(2,1)}), bf16[16,2,32,1024]{3,2,1,0:T(8,128)(2,1)S(1)}, u32[]{:S(2)}, u32[]{:S(2)}) async-start(bf16[16,2,32,1024]{3,2,1,0:T(8,128)(2,1)} %get-tuple-element.14), calls=%async_computation | async-start | bytes 4194304 | tf_op jit(solution)/shard_map/all_to_all | solution.py:251
  28.6 0.6 slice_reduce_fusion.masks_ref
  29.2 25.5 %all-to-all-done.st_ref = bf16[16,2,32,1024]{3,2,1,0:T(8,128)(2,1)S(1)} async-done(((bf16[16,2,32,1024]{3,2,1,0:T(8,128)(2,1)}), bf16[16,2,32,1024]{3,2,1,0:T(8,128)(2,1)S(1)}, u32[]{:S(2)}, u32[]{:S(2)}) %all-to-all-start) | async-done | bytes 2097184 | tf_op jit(solution)/shard_map/all_to_all | solution.py:251
  54.7 1.4 copy-done
  56.1 3.7 %gram.1 = f32[256,128]{1,0:T(8,128)} custom-call(s32[2]{0:T(128)} %slice_reduce_fusion.masks_ref, bf16[16,2,32,1024]{3,2,1,0:T(8,128)(2,1)} %copy-done), custom_call_target="tpu_custom_call" | custom-call | tf_op jit(solution)/shard_map/gram/pallas_call | solution.py:163
  59.8 28.3 %all_to_all.21 = f32[256,1,128]{2,1,0:T(1,128)} all-to-all(f32[256,1,128]{2,1,0:T(1,128)} %bitcast.84), channel_id=1, replica_groups=mesh['dp'=16,'space'=16] {'dp','space'}, dimensions={0} | all-to-all | bytes 262144 | tf_op jit(solution)/shard_map/all_to_all | solution.py:254
  88.1 3.9 %grad.1 = (bf16[16,32,1024]{2,1,0:T(8,128)(2,1)}, f32[1,1]{1,0:T(1,128)}) custom-call(s32[2]{0:T(128)} %slice_reduce_fusion.masks_ref, f32[256,128]{1,0:T(8,128)} %bitcast.83, bf16[16,2,32,1024]{3,2,1,0:T(8,128)(2,1)} %copy-done), custom_call_target="tpu_custom_call" | custom-call | tf_op jit(solution)/shard_map/grad/pallas_call | solution.py:163
  91.9 19.4 %all_to_all.22 = bf16[16,32,1024]{2,1,0:T(8,128)(2,1)} all-to-all(bf16[16,32,1024]{2,1,0:T(8,128)(2,1)} %get-tuple-element.16), channel_id=1, replica_groups=mesh['dp'=16,'space'=16] {'dp'}, dimensions={0} | all-to-all | bytes 2097152 | tf_op jit(solution)/shard_map/all_to_all | solution.py:261
  111.4 3.1 %expand.1 = (bf16[4,128,256]{2,1,0:T(8,128)(2,1)}, bf16[16,64,256]{2,1,0:T(8,128)(2,1)}) custom-call(bf16[512,1024]{1,0:T(8,128)(2,1)} %bitcast.79, bf16[4,128,256]{2,1,0:T(8,128)(2,1)} %get-tuple-element.17.h2_ref, bf16[256,1024]{1,0:T(8,128)(2,1)} %we_ref.3), custom_call_target="tpu_custom_call" | custom-call | tf_op jit(solution)/shard_map/expand/pallas_call | solution.py:163
  114.4 0.9 slice_bitcast_fusion.4
  115.3 3.0 %collective-permute-start.2 = (bf16[128,256]{1,0:T(8,128)(2,1)S(1)}, bf16[128,256]{1,0:T(8,128)(2,1)S(1)}, u32[]{:S(2)}, u32[]{:S(2)}) collective-permute-start(bf16[128,256]{1,0:T(8,128)(2,1)S(1)} %get-tuple-element.40), channel_id=1, source_target_pairs={{0,1},{1,2},{2,3},{3,4},{4,5},{5,6},{6,7},{7,8},{8,9},{9,10},{10,1... | collective-permute-start | bytes 196616 | tf_op jit(solution)/shard_map/ppermute | solution.py:188
  118.3 1.3 collective-permute-start.3
  119.7 2.9 %spatial.1 = bf16[16,3,3,16,256]{4,3,2,1,0:T(8,128)(2,1)} custom-call(bf16[6,128,256]{2,1,0:T(8,128)(2,1)} %get-tuple-element.19.hp_ref, bf16[4,128,256]{2,1,0:T(8,128)(2,1)} %get-tuple-element.18.g2_ref), custom_call_target="tpu_custom_call" | custom-call | flops 603979776 | bytes 524288 | tf_op jit(solution)/shard_map/spatial/pallas_call | solution.py:163
  122.6 3.3 %collective-permute-done.3.below_ref = bf16[128,256]{1,0:T(8,128)(2,1)S(1)} collective-permute-done((bf16[128,256]{1,0:T(8,128)(2,1)S(1)}, bf16[128,256]{1,0:T(8,128)(2,1)S(1)}, u32[]{:S(2)}, u32[]{:S(2)}) %collective-permute-start.3) | collective-permute-done | bytes 65568 | tf_op jit(solution)/shard_map/ppermute | solution.py:189
  126.0 0.6 copy-done.4
  126.6 5.1 %backward.1 = (bf16[16,64,256]{2,1,0:T(8,128)(2,1)}, bf16[1,4,128,1024]{3,2,1,0:T(8,128)(2,1)}) custom-call(bf16[4,128,256]{2,1,0:T(8,128)(2,1)} %get-tuple-element.18.g2_ref, bf16[128,256]{1,0:T(8,128)(2,1)} %copy-done.3, bf16[128,256]{1,0:T(8,128)(2,1)} %copy-done.4, bf16[6,128,256]{2,1,0:T(8,128)(2,1)} %get-tuple-element.19.hp_ref, ...), custom_call_target="tpu_custom_call" | custom-call | tf_op jit(solution)/shard_map/backward/pallas_call | solution.py:163
  131.7 1.2 pad_maximum_fusion
  133.0 1.2 collective-permute-start.11
  134.1 1.1 collective-permute-start.4
  135.2 3.3 %collective-permute-done.11 = bf16[272,256]{1,0:T(8,128)(2,1)S(1)} collective-permute-done((bf16[272,256]{1,0:T(8,128)(2,1)S(1)}, bf16[272,256]{1,0:T(8,128)(2,1)S(1)}, u32[]{:S(2)}, u32[]{:S(2)}) %collective-permute-start.11) | collective-permute-done | bytes 139296 | tf_op jit(solution)/shard_map/ppermute | solution.py:208
  138.5 1.9 collective-permute-done.4
  140.4 0.1 fusion.5
  140.5 0.2 collective-permute-start.12
  140.6 1.9 %collective-permute-start.5 = (bf16[272,256]{1,0:T(8,128)(2,1)S(1)}, bf16[272,256]{1,0:T(8,128)(2,1)S(1)}, u32[]{:S(2)}, u32[]{:S(2)}) collective-permute-start(bf16[272,256]{1,0:T(8,128)(2,1)S(1)} %get-tuple-element.34), channel_id=1, source_target_pairs={{0,2},{1,3},{2,4},{3,5},{4,6},{5,7},{6,8},{7,9},{8,10},{9,11},{10,... | collective-permute-start | bytes 417800 | tf_op jit(solution)/shard_map/ppermute | solution.py:207
  142.6 3.0 %collective-permute-done.12 = bf16[272,256]{1,0:T(8,128)(2,1)S(1)} collective-permute-done((bf16[272,256]{1,0:T(8,128)(2,1)S(1)}, bf16[272,256]{1,0:T(8,128)(2,1)S(1)}, u32[]{:S(2)}, u32[]{:S(2)}) %collective-permute-start.12) | collective-permute-done | bytes 139296 | tf_op jit(solution)/shard_map/ppermute | solution.py:208
  145.6 1.5 collective-permute-done.5
  147.1 0.1 fusion.4
  147.2 0.1 collective-permute-start.13
  147.3 2.0 %collective-permute-start.6 = (bf16[272,256]{1,0:T(8,128)(2,1)S(1)}, bf16[272,256]{1,0:T(8,128)(2,1)S(1)}, u32[]{:S(2)}, u32[]{:S(2)}) collective-permute-start(bf16[272,256]{1,0:T(8,128)(2,1)S(1)} %get-tuple-element.32), channel_id=1, source_target_pairs={{0,2},{1,3},{2,4},{3,5},{4,6},{5,7},{6,8},{7,9},{8,10},{9,11},{10,... | collective-permute-start | bytes 417800 | tf_op jit(solution)/shard_map/ppermute | solution.py:207
  149.3 3.0 %collective-permute-done.13 = bf16[272,256]{1,0:T(8,128)(2,1)S(1)} collective-permute-done((bf16[272,256]{1,0:T(8,128)(2,1)S(1)}, bf16[272,256]{1,0:T(8,128)(2,1)S(1)}, u32[]{:S(2)}, u32[]{:S(2)}) %collective-permute-start.13) | collective-permute-done | bytes 139296 | tf_op jit(solution)/shard_map/ppermute | solution.py:208
  152.3 1.3 collective-permute-done.6
  153.6 0.1 fusion.3
  153.7 1.2 collective-permute-start.14
  154.9 0.9 collective-permute-start.7
  155.8 3.6 %collective-permute-done.14 = bf16[272,256]{1,0:T(8,128)(2,1)S(1)} collective-permute-done((bf16[272,256]{1,0:T(8,128)(2,1)S(1)}, bf16[272,256]{1,0:T(8,128)(2,1)S(1)}, u32[]{:S(2)}, u32[]{:S(2)}) %collective-permute-start.14) | collective-permute-done | bytes 139296 | tf_op jit(solution)/shard_map/ppermute | solution.py:208
  159.4 3.2 %collective-permute-done.7 = bf16[272,256]{1,0:T(8,128)(2,1)S(1)} collective-permute-done((bf16[272,256]{1,0:T(8,128)(2,1)S(1)}, bf16[272,256]{1,0:T(8,128)(2,1)S(1)}, u32[]{:S(2)}, u32[]{:S(2)}) %collective-permute-start.7) | collective-permute-done | bytes 139296 | tf_op jit(solution)/shard_map/ppermute | solution.py:207
  162.6 0.1 fusion.2
  162.7 1.0 collective-permute-start.15
  163.7 1.1 collective-permute-start.8
  164.8 3.7 %collective-permute-done.15 = bf16[272,256]{1,0:T(8,128)(2,1)S(1)} collective-permute-done((bf16[272,256]{1,0:T(8,128)(2,1)S(1)}, bf16[272,256]{1,0:T(8,128)(2,1)S(1)}, u32[]{:S(2)}, u32[]{:S(2)}) %collective-permute-start.15) | collective-permute-done | bytes 139296 | tf_op jit(solution)/shard_map/ppermute | solution.py:208
  168.4 1.5 collective-permute-done.8
  170.0 0.1 fusion.1
  170.1 0.4 collective-permute-start.16
  170.5 1.7 collective-permute-start.9
  172.2 3.0 %collective-permute-done.16 = bf16[272,256]{1,0:T(8,128)(2,1)S(1)} collective-permute-done((bf16[272,256]{1,0:T(8,128)(2,1)S(1)}, bf16[272,256]{1,0:T(8,128)(2,1)S(1)}, u32[]{:S(2)}, u32[]{:S(2)}) %collective-permute-start.16) | collective-permute-done | bytes 139296 | tf_op jit(solution)/shard_map/ppermute | solution.py:208
  175.2 1.6 collective-permute-done.9
  176.8 0.1 fusion
  176.9 0.5 collective-permute-start.10
  177.4 2.8 %collective-permute-start.17 = (bf16[272,256]{1,0:T(8,128)(2,1)S(1)}, bf16[272,256]{1,0:T(8,128)(2,1)S(1)}, u32[]{:S(2)}, u32[]{:S(2)}) collective-permute-start(bf16[272,256]{1,0:T(8,128)(2,1)S(1)} %get-tuple-element.23), channel_id=1, source_target_pairs={{0,14},{1,15},{2,0},{3,1},{4,2},{5,3},{6,4},{7,5},{8,6},{9,7},{10,... | collective-permute-start | bytes 417800 | tf_op jit(solution)/shard_map/ppermute | solution.py:208
  180.2 3.0 %collective-permute-done.10 = bf16[272,256]{1,0:T(8,128)(2,1)S(1)} collective-permute-done((bf16[272,256]{1,0:T(8,128)(2,1)S(1)}, bf16[272,256]{1,0:T(8,128)(2,1)S(1)}, u32[]{:S(2)}, u32[]{:S(2)}) %collective-permute-start.10) | collective-permute-done | bytes 139296 | tf_op jit(solution)/shard_map/ppermute | solution.py:207
  183.2 0.1 select_convert_fusion
  183.3 2.8 %collective-permute-start.18 = (bf16[272,256]{1,0:T(8,128)(2,1)S(1)}, bf16[272,256]{1,0:T(8,128)(2,1)S(1)}, u32[]{:S(2)}, u32[]{:S(2)}) collective-permute-start(bf16[272,256]{1,0:T(8,128)(2,1)S(1)} %select_convert_fusion), channel_id=1, source_target_pairs={{0,1},{1,0},{2,3},{3,2},{4,5},{5,4},{6,7},{7,6},{8,9},{9,8},{10,11... | collective-permute-start | bytes 417800 | tf_op jit(solution)/shard_map/ppermute | solution.py:216
  186.0 3.9 %collective-permute-done.18 = bf16[272,256]{1,0:T(8,128)(2,1)S(1)} collective-permute-done((bf16[272,256]{1,0:T(8,128)(2,1)S(1)}, bf16[272,256]{1,0:T(8,128)(2,1)S(1)}, u32[]{:S(2)}, u32[]{:S(2)}) %collective-permute-start.18) | collective-permute-done | bytes 139296 | tf_op jit(solution)/shard_map/ppermute | solution.py:216
  189.9 0.1 convert_add_fusion.14
  190.0 0.7 slice_bitcast_fusion
  190.7 0.7 slice.35
  (16 shorter events, 0.1 us)
Async XLA Ops:
  5.4 6.8 %collective-permute-start = (bf16[128,256]{1,0:T(8,128)(2,1)S(1)}, bf16[128,256]{1,0:T(8,128)(2,1)S(1)}, u32[]{:S(2)}, u32[]{:S(2)}) collective-permute-start(bf16[128,256]{1,0:T(8,128)(2,1)S(1)} %get-tuple-element.42), channel_id=1, source_target_pairs={{0,1},{1,2},{2,3},{3,4},{4,5},{5,6},{6,7},{7,8},{8,9},{9,10},{10,1... | collective-permute-start | bytes 196616 | tf_op jit(solution)/shard_map/ppermute | solution.py:188
  10.3 7.7 %collective-permute-start.1 = (bf16[128,256]{1,0:T(8,128)(2,1)S(1)}, bf16[128,256]{1,0:T(8,128)(2,1)S(1)}, u32[]{:S(2)}, u32[]{:S(2)}) collective-permute-start(bf16[128,256]{1,0:T(8,128)(2,1)S(1)} %get-tuple-element.41), channel_id=1, source_target_pairs={{1,0},{2,1},{3,2},{4,3},{5,4},{6,5},{7,6},{8,7},{9,8},{10,9},{11,1... | collective-permute-start | bytes 196616 | tf_op jit(solution)/shard_map/ppermute | solution.py:189
  12.2 5.8 %copy-start.5 = (bf16[128,256]{1,0:T(8,128)(2,1)}, bf16[128,256]{1,0:T(8,128)(2,1)S(1)}, u32[]{:S(2)}) copy-start(bf16[128,256]{1,0:T(8,128)(2,1)S(1)} %collective-permute-done.above_ref) | copy-start | bytes 196612
  18.0 0.6 copy-start.6
  23.5 5.1 %copy-start.7 = (s32[2,16]{1,0:T(2,128)S(1)}, s32[2,16]{1,0:T(2,128)}, u32[]{:S(2)}) copy-start(s32[2,16]{1,0:T(2,128)} %param.11) | copy-start | bytes 388
  23.5 31.2 %all-to-all-start = ((bf16[16,2,32,1024]{3,2,1,0:T(8,128)(2,1)}), bf16[16,2,32,1024]{3,2,1,0:T(8,128)(2,1)S(1)}, u32[]{:S(2)}, u32[]{:S(2)}) async-start(bf16[16,2,32,1024]{3,2,1,0:T(8,128)(2,1)} %get-tuple-element.14), calls=%async_computation | async-start | bytes 4194304 | tf_op jit(solution)/shard_map/all_to_all | solution.py:251
  54.7 1.4 copy-start
  115.3 7.3 %collective-permute-start.2 = (bf16[128,256]{1,0:T(8,128)(2,1)S(1)}, bf16[128,256]{1,0:T(8,128)(2,1)S(1)}, u32[]{:S(2)}, u32[]{:S(2)}) collective-permute-start(bf16[128,256]{1,0:T(8,128)(2,1)S(1)} %get-tuple-element.40), channel_id=1, source_target_pairs={{0,1},{1,2},{2,3},{3,4},{4,5},{5,6},{6,7},{7,8},{8,9},{9,10},{10,1... | collective-permute-start | bytes 196616 | tf_op jit(solution)/shard_map/ppermute | solution.py:188
  118.3 7.7 %collective-permute-start.3 = (bf16[128,256]{1,0:T(8,128)(2,1)S(1)}, bf16[128,256]{1,0:T(8,128)(2,1)S(1)}, u32[]{:S(2)}, u32[]{:S(2)}) collective-permute-start(bf16[128,256]{1,0:T(8,128)(2,1)S(1)} %get-tuple-element.39), channel_id=1, source_target_pairs={{1,0},{2,1},{3,2},{4,3},{5,4},{6,5},{7,6},{8,7},{9,8},{10,9},{11,1... | collective-permute-start | bytes 196616 | tf_op jit(solution)/shard_map/ppermute | solution.py:189
  122.6 9.1 %copy-start.1 = (bf16[16,3,3,16,256]{4,3,2,1,0:T(8,128)(2,1)S(1)}, bf16[16,3,3,16,256]{4,3,2,1,0:T(8,128)(2,1)}, u32[]{:S(2)}) copy-start(bf16[16,3,3,16,256]{4,3,2,1,0:T(8,128)(2,1)} %spatial.1) | copy-start | bytes 3538948
  122.6 9.1 %copy-start.2 = (bf16[16,64,256]{2,1,0:T(8,128)(2,1)S(1)}, bf16[16,64,256]{2,1,0:T(8,128)(2,1)}, u32[]{:S(2)}) copy-start(bf16[16,64,256]{2,1,0:T(8,128)(2,1)} %get-tuple-element.21) | copy-start | bytes 1572868
  122.6 3.4 %copy-start.3 = (bf16[128,256]{1,0:T(8,128)(2,1)}, bf16[128,256]{1,0:T(8,128)(2,1)S(1)}, u32[]{:S(2)}) copy-start(bf16[128,256]{1,0:T(8,128)(2,1)S(1)} %collective-permute-done.2.above_ref) | copy-start | bytes 196612
  126.0 0.6 copy-start.4
  133.0 5.6 %collective-permute-start.11 = (bf16[272,256]{1,0:T(8,128)(2,1)S(1)}, bf16[272,256]{1,0:T(8,128)(2,1)S(1)}, u32[]{:S(2)}, u32[]{:S(2)}) collective-permute-start(bf16[272,256]{1,0:T(8,128)(2,1)S(1)} %get-tuple-element.35), channel_id=1, source_target_pairs={{0,14},{1,15},{2,0},{3,1},{4,2},{5,3},{6,4},{7,5},{8,6},{9,7},{10,... | collective-permute-start | bytes 417800 | tf_op jit(solution)/shard_map/ppermute | solution.py:208
  134.1 6.3 %collective-permute-start.4 = (bf16[272,256]{1,0:T(8,128)(2,1)S(1)}, bf16[272,256]{1,0:T(8,128)(2,1)S(1)}, u32[]{:S(2)}, u32[]{:S(2)}) collective-permute-start(bf16[272,256]{1,0:T(8,128)(2,1)S(1)} %get-tuple-element.36), channel_id=1, source_target_pairs={{0,2},{1,3},{2,4},{3,5},{4,6},{5,7},{6,8},{7,9},{8,10},{9,11},{10,... | collective-permute-start | bytes 417800 | tf_op jit(solution)/shard_map/ppermute | solution.py:207
  140.5 5.1 %collective-permute-start.12 = (bf16[272,256]{1,0:T(8,128)(2,1)S(1)}, bf16[272,256]{1,0:T(8,128)(2,1)S(1)}, u32[]{:S(2)}, u32[]{:S(2)}) collective-permute-start(bf16[272,256]{1,0:T(8,128)(2,1)S(1)} %get-tuple-element.33), channel_id=1, source_target_pairs={{0,14},{1,15},{2,0},{3,1},{4,2},{5,3},{6,4},{7,5},{8,6},{9,7},{10,... | collective-permute-start | bytes 417800 | tf_op jit(solution)/shard_map/ppermute | solution.py:208
  140.6 6.4 %collective-permute-start.5 = (bf16[272,256]{1,0:T(8,128)(2,1)S(1)}, bf16[272,256]{1,0:T(8,128)(2,1)S(1)}, u32[]{:S(2)}, u32[]{:S(2)}) collective-permute-start(bf16[272,256]{1,0:T(8,128)(2,1)S(1)} %get-tuple-element.34), channel_id=1, source_target_pairs={{0,2},{1,3},{2,4},{3,5},{4,6},{5,7},{6,8},{7,9},{8,10},{9,11},{10,... | collective-permute-start | bytes 417800 | tf_op jit(solution)/shard_map/ppermute | solution.py:207
  147.2 5.1 %collective-permute-start.13 = (bf16[272,256]{1,0:T(8,128)(2,1)S(1)}, bf16[272,256]{1,0:T(8,128)(2,1)S(1)}, u32[]{:S(2)}, u32[]{:S(2)}) collective-permute-start(bf16[272,256]{1,0:T(8,128)(2,1)S(1)} %get-tuple-element.31), channel_id=1, source_target_pairs={{0,14},{1,15},{2,0},{3,1},{4,2},{5,3},{6,4},{7,5},{8,6},{9,7},{10,... | collective-permute-start | bytes 417800 | tf_op jit(solution)/shard_map/ppermute | solution.py:208
  147.3 6.3 %collective-permute-start.6 = (bf16[272,256]{1,0:T(8,128)(2,1)S(1)}, bf16[272,256]{1,0:T(8,128)(2,1)S(1)}, u32[]{:S(2)}, u32[]{:S(2)}) collective-permute-start(bf16[272,256]{1,0:T(8,128)(2,1)S(1)} %get-tuple-element.32), channel_id=1, source_target_pairs={{0,2},{1,3},{2,4},{3,5},{4,6},{5,7},{6,8},{7,9},{8,10},{9,11},{10,... | collective-permute-start | bytes 417800 | tf_op jit(solution)/shard_map/ppermute | solution.py:207
  153.7 5.7 %collective-permute-start.14 = (bf16[272,256]{1,0:T(8,128)(2,1)S(1)}, bf16[272,256]{1,0:T(8,128)(2,1)S(1)}, u32[]{:S(2)}, u32[]{:S(2)}) collective-permute-start(bf16[272,256]{1,0:T(8,128)(2,1)S(1)} %get-tuple-element.29), channel_id=1, source_target_pairs={{0,14},{1,15},{2,0},{3,1},{4,2},{5,3},{6,4},{7,5},{8,6},{9,7},{10,... | collective-permute-start | bytes 417800 | tf_op jit(solution)/shard_map/ppermute | solution.py:208
  154.9 7.7 %collective-permute-start.7 = (bf16[272,256]{1,0:T(8,128)(2,1)S(1)}, bf16[272,256]{1,0:T(8,128)(2,1)S(1)}, u32[]{:S(2)}, u32[]{:S(2)}) collective-permute-start(bf16[272,256]{1,0:T(8,128)(2,1)S(1)} %get-tuple-element.30), channel_id=1, source_target_pairs={{0,2},{1,3},{2,4},{3,5},{4,6},{5,7},{6,8},{7,9},{8,10},{9,11},{10,... | collective-permute-start | bytes 417800 | tf_op jit(solution)/shard_map/ppermute | solution.py:207
  162.7 5.8 %collective-permute-start.15 = (bf16[272,256]{1,0:T(8,128)(2,1)S(1)}, bf16[272,256]{1,0:T(8,128)(2,1)S(1)}, u32[]{:S(2)}, u32[]{:S(2)}) collective-permute-start(bf16[272,256]{1,0:T(8,128)(2,1)S(1)} %get-tuple-element.27), channel_id=1, source_target_pairs={{0,14},{1,15},{2,0},{3,1},{4,2},{5,3},{6,4},{7,5},{8,6},{9,7},{10,... | collective-permute-start | bytes 417800 | tf_op jit(solution)/shard_map/ppermute | solution.py:208
  163.7 6.3 %collective-permute-start.8 = (bf16[272,256]{1,0:T(8,128)(2,1)S(1)}, bf16[272,256]{1,0:T(8,128)(2,1)S(1)}, u32[]{:S(2)}, u32[]{:S(2)}) collective-permute-start(bf16[272,256]{1,0:T(8,128)(2,1)S(1)} %get-tuple-element.28), channel_id=1, source_target_pairs={{0,2},{1,3},{2,4},{3,5},{4,6},{5,7},{6,8},{7,9},{8,10},{9,11},{10,... | collective-permute-start | bytes 417800 | tf_op jit(solution)/shard_map/ppermute | solution.py:207
  170.1 5.1 %collective-permute-start.16 = (bf16[272,256]{1,0:T(8,128)(2,1)S(1)}, bf16[272,256]{1,0:T(8,128)(2,1)S(1)}, u32[]{:S(2)}, u32[]{:S(2)}) collective-permute-start(bf16[272,256]{1,0:T(8,128)(2,1)S(1)} %get-tuple-element.25), channel_id=1, source_target_pairs={{0,14},{1,15},{2,0},{3,1},{4,2},{5,3},{6,4},{7,5},{8,6},{9,7},{10,... | collective-permute-start | bytes 417800 | tf_op jit(solution)/shard_map/ppermute | solution.py:208
  170.5 6.3 %collective-permute-start.9 = (bf16[272,256]{1,0:T(8,128)(2,1)S(1)}, bf16[272,256]{1,0:T(8,128)(2,1)S(1)}, u32[]{:S(2)}, u32[]{:S(2)}) collective-permute-start(bf16[272,256]{1,0:T(8,128)(2,1)S(1)} %get-tuple-element.26), channel_id=1, source_target_pairs={{0,2},{1,3},{2,4},{3,5},{4,6},{5,7},{6,8},{7,9},{8,10},{9,11},{10,... | collective-permute-start | bytes 417800 | tf_op jit(solution)/shard_map/ppermute | solution.py:207
  176.9 6.3 %collective-permute-start.10 = (bf16[272,256]{1,0:T(8,128)(2,1)S(1)}, bf16[272,256]{1,0:T(8,128)(2,1)S(1)}, u32[]{:S(2)}, u32[]{:S(2)}) collective-permute-start(bf16[272,256]{1,0:T(8,128)(2,1)S(1)} %get-tuple-element.24), channel_id=1, source_target_pairs={{0,2},{1,3},{2,4},{3,5},{4,6},{5,7},{6,8},{7,9},{8,10},{9,11},{10,... | collective-permute-start | bytes 417800 | tf_op jit(solution)/shard_map/ppermute | solution.py:207
  177.4 5.8 %collective-permute-start.17 = (bf16[272,256]{1,0:T(8,128)(2,1)S(1)}, bf16[272,256]{1,0:T(8,128)(2,1)S(1)}, u32[]{:S(2)}, u32[]{:S(2)}) collective-permute-start(bf16[272,256]{1,0:T(8,128)(2,1)S(1)} %get-tuple-element.23), channel_id=1, source_target_pairs={{0,14},{1,15},{2,0},{3,1},{4,2},{5,3},{6,4},{7,5},{8,6},{9,7},{10,... | collective-permute-start | bytes 417800 | tf_op jit(solution)/shard_map/ppermute | solution.py:208
  183.3 6.6 %collective-permute-start.18 = (bf16[272,256]{1,0:T(8,128)(2,1)S(1)}, bf16[272,256]{1,0:T(8,128)(2,1)S(1)}, u32[]{:S(2)}, u32[]{:S(2)}) collective-permute-start(bf16[272,256]{1,0:T(8,128)(2,1)S(1)} %select_convert_fusion), channel_id=1, source_target_pairs={{0,1},{1,0},{2,3},{3,2},{4,5},{5,4},{6,7},{7,6},{8,9},{9,8},{10,11... | collective-permute-start | bytes 417800 | tf_op jit(solution)/shard_map/ppermute | solution.py:216

commit v2 on v1

v2 whole, which is shorter than its diff:
```python
import functools

import jax
import jax.numpy as jnp
from jax import lax
from jax.experimental import pallas as pl
from jax.experimental.pallas import tpu as pltpu
from jax.sharding import PartitionSpec as P

F32 = jnp.float32
BF16 = jnp.bfloat16
VMEM_LIMIT = 20 * 2**20
ROW_DOT = (((1,), (0,)), ((), ()))
LAST_DOT = (((1,), (1,)), ((), ()))
FIRST_DOT = (((0,), (0,)), ((), ()))


def dot(left, right, dims):
    return lax.dot_general(left, right, dims, preferred_element_type=F32)


def flat(value):
    return value.reshape(-1, value.shape[-1])


def shifted(value, step, cols):
    count = value.shape[0]
    moved = pltpu.roll(value, (-step) % count, 0)
    col = lax.broadcasted_iota(jnp.int32, value.shape, 0) % cols
    edge = cols - 1 if step == 1 else 0
    return jnp.where(col == edge, 0.0, moved)


def widened(parts, cols):
    return parts[1] + shifted(parts[0], -1, cols) + shifted(parts[2], 1, cols)


def narrowed(parts, cols):
    return parts[1] + shifted(parts[0], 1, cols) + shifted(parts[2], -1, cols)


def taps(sources, ws_ref, dims):
    sums = []
    for b in range(3):
        acc = None
        for a in range(3):
            part = dot(sources[a], ws_ref[a, b], dims)
            acc = part if acc is None else acc + part
        sums.append(acc)
    return sums


def edge_kernel(top_ref, end_ref, w_ref, first_ref, last_ref):
    for source, out in ((top_ref, first_ref), (end_ref, last_ref)):
        out[...] = jnp.maximum(dot(source[0], w_ref[...], ROW_DOT), 0.0).astype(BF16)


def inner_kernel(x_ref, wr_ref, first_ref, last_ref, ws_ref, we_ref, h_ref, h2_ref, s_ref):
    rows, cols, _ = h_ref.shape
    inside = rows - 2
    x_in = flat(x_ref[1 : rows - 1])
    h_in = jnp.maximum(dot(x_in, wr_ref[...], ROW_DOT), 0.0).astype(BF16)
    h_ref[0] = first_ref[...]
    h_ref[rows - 1] = last_ref[...]
    h_ref[1 : rows - 1] = h_in.reshape(inside, cols, -1)
    sums = taps([flat(h_ref[a : a + inside]) for a in range(3)], ws_ref, ROW_DOT)
    h_two = jnp.maximum(widened(sums, cols), 0.0).astype(BF16)
    h2_ref[...] = h_two
    pre = dot(h_two, we_ref[...], ROW_DOT) + x_in.astype(F32)
    s_ref[...] = jnp.maximum(pre, 0.0).astype(BF16).reshape(s_ref.shape)


def outer_kernel(h_ref, above_ref, below_ref, ws_ref, we_ref, x_ref, si_ref, h2_ref, s_ref):
    rows, cols, _ = h_ref.shape
    tops = [above_ref[...], h_ref[0], h_ref[1]]
    ends = [h_ref[rows - 2], h_ref[rows - 1], below_ref[...]]
    sources = [jnp.concatenate(pair, axis=0) for pair in zip(tops, ends)]
    h_two = jnp.maximum(widened(taps(sources, ws_ref, ROW_DOT), cols), 0.0).astype(BF16)
    h2_ref[...] = h_two
    x_out = jnp.concatenate([x_ref[0], x_ref[rows - 1]], axis=0)
    pre = dot(h_two, we_ref[...], ROW_DOT) + x_out.astype(F32)
    devices, split, channels = si_ref.shape
    s_ref[:, :split] = si_ref[...]
    s_ref[:, split:] = jnp.maximum(pre, 0.0).astype(BF16).reshape(devices, -1, channels)


def gram_kernel(base, parts_ref, *refs):
    value_ref, out_ref = refs[-2], refs[-1]
    images, chunk, _ = value_ref.shape
    count = images * chunk
    row = lax.broadcasted_iota(jnp.int32, (count, count), 0)
    col = lax.broadcasted_iota(jnp.int32, (count, count), 1)
    same = (row % chunk) == (col % chunk)
    image = lax.broadcasted_iota(jnp.int32, (images, count), 0)
    other = lax.broadcasted_iota(jnp.int32, (images, count), 1) // chunk
    slot_row = lax.broadcasted_iota(jnp.int32, (images, 128), 0)
    slot = lax.broadcasted_iota(jnp.int32, (images, 128), 1)
    message = jnp.zeros((images, 128), F32)
    value = flat(value_ref[...])
    gram = jnp.where(same, dot(value, value, LAST_DOT), 0.0)
    gram = gram.reshape(images, chunk, count).sum(axis=1)
    for k in range(3):
        partner = image if k == 0 else image ^ parts_ref[k - 1, 0]
        column = jnp.where(other == partner, gram, 0.0).sum(axis=1, keepdims=True)
        message = message + jnp.where(slot == 8 * slot_row + base + k, column, 0.0)
    total = message.sum(axis=0, keepdims=True)
    if len(refs) == 3:
        total = total + refs[0][...]
    out_ref[...] = jnp.broadcast_to(total, out_ref.shape)


def grad_kernel(scale, parts_ref, msg_ref, s_ref, g_ref, loss_ref):
    images = s_ref.shape[0]
    total = jnp.broadcast_to(msg_ref[...].sum(axis=0, keepdims=True), (images, 128))
    row = lax.broadcasted_iota(jnp.int32, (images, 128), 0)
    lane = lax.broadcasted_iota(jnp.int32, (images, 128), 1)

    def column(k):
        return jnp.where(lane == 8 * row + k, total, 0.0).sum(axis=1, keepdims=True)

    v_s = [column(k) for k in range(3)]
    v_t = [column(3 + k) for k in range(3)]
    nu_s = jnp.sqrt(v_s[0] * v_s[0] + v_s[1] * v_s[1] + v_s[2] * v_s[2] + 1e-06)
    nu_t = jnp.sqrt(v_t[0] * v_t[0] + v_t[1] * v_t[1] + v_t[2] * v_t[2] + 1e-06)
    n_s = [v / nu_s for v in v_s]
    diff = [a - b / nu_t for a, b in zip(n_s, v_t)]
    terms = diff[0] * diff[0] + diff[1] * diff[1] + diff[2] * diff[2]
    loss_ref[...] = terms.sum(axis=0, keepdims=True)
    err = [2.0 * d for d in diff]
    inner = err[0] * n_s[0] + err[1] * n_s[1] + err[2] * n_s[2]
    coefs = [(e - inner * n) / nu_s for e, n in zip(err, n_s)]
    weights = [2.0 * coefs[0]]
    for k in range(2):
        own = coefs[k + 1]
        as_row = jnp.where(row == lane, own, 0.0).sum(axis=0, keepdims=True)
        partner = row ^ parts_ref[k, 0]
        theirs = jnp.where(lane == partner, as_row, 0.0).sum(axis=1, keepdims=True)
        weights.append(own + theirs)
    for i in range(images):
        own = s_ref[i].astype(F32)
        acc = weights[0][i : i + 1] * own
        for k in range(2):
            acc = acc + weights[k + 1][i : i + 1] * s_ref[i ^ parts_ref[k, 0]].astype(F32)
        g_ref[i] = jnp.where(own > 0.0, scale * acc, 0.0).astype(BF16)


def halves(g_ref, h2i_ref):
    split = h2i_ref.shape[0] // g_ref.shape[0]
    return flat(g_ref[:, :split]), flat(g_ref[:, split:])


def back_kernel(g_ref, h2i_ref, h2o_ref, we_ref, g2_ref, first_ref, last_ref):
    rows, cols, _ = g2_ref.shape
    g_in, g_out = halves(g_ref, h2i_ref)
    back = dot(g_out, we_ref[...], LAST_DOT)
    g_two = jnp.where(h2o_ref[...] > 0, back, 0.0).astype(BF16)
    first_ref[...] = g_two[:cols]
    last_ref[...] = g_two[cols:]
    g2_ref[0] = g_two[:cols]
    g2_ref[rows - 1] = g_two[cols:]
    back = dot(g_in, we_ref[...], LAST_DOT)
    g_two = jnp.where(h2i_ref[...] > 0, back, 0.0).astype(BF16)
    g2_ref[1 : rows - 1] = g_two.reshape(rows - 2, cols, -1)


def window_kernel(
    g_ref, h2i_ref, h2o_ref, g2_ref, h_ref, above_ref, below_ref, ws_ref, out_ref, g1_ref, hp_ref
):
    rows, cols, mid = g2_ref.shape
    chunks = out_ref.shape[0]
    width = mid // chunks
    g_in, g_out = halves(g_ref, h2i_ref)
    expand = dot(g_in, h2i_ref[...], FIRST_DOT) + dot(g_out, h2o_ref[...], FIRST_DOT)
    part = expand.shape[0] // chunks
    out_ref[:, :part] = expand.astype(BF16).reshape(chunks, part, mid)
    hp_ref[0] = above_ref[...]
    hp_ref[rows + 1] = below_ref[...]
    hp_ref[1 : rows + 1] = h_ref[...]
    g_two = flat(g2_ref[...])
    wide = g_two.astype(F32)
    moved = [shifted(wide, 1, cols).astype(BF16), g_two, shifted(wide, -1, cols).astype(BF16)]
    for a in range(3):
        source = flat(hp_ref[a : a + rows])
        for b in range(3):
            start = part + (3 * a + b) * width
            grad = dot(moved[b], source, FIRST_DOT).astype(BF16)
            out_ref[:, start : start + width] = grad.reshape(chunks, width, mid)
    inside = rows - 2
    sums = taps([flat(g2_ref[2 - a : 2 - a + inside]) for a in range(3)], ws_ref, LAST_DOT)
    total = narrowed(sums, cols)
    g1_ref[...] = jnp.where(flat(h_ref[1 : rows - 1]) > 0, total, 0.0).astype(BF16)


def backward_kernel(
    g2_ref, above_ref, below_ref, h_ref, ws_ref, x_ref, g1i_ref, out_ref, g1o_ref
):
    rows = g2_ref.shape[0]
    cols = g2_ref.shape[1]
    tops = [g2_ref[1], g2_ref[0], above_ref[...]]
    ends = [below_ref[...], g2_ref[rows - 1], g2_ref[rows - 2]]
    sources = [jnp.concatenate(pair, axis=0) for pair in zip(tops, ends)]
    total = narrowed(taps(sources, ws_ref, LAST_DOT), cols)
    h_out = jnp.concatenate([h_ref[0], h_ref[rows - 1]], axis=0)
    g_one = jnp.where(h_out > 0, total, 0.0).astype(BF16)
    g1o_ref[...] = g_one
    x_out = jnp.concatenate([x_ref[0], x_ref[rows - 1]], axis=0)
    grad = dot(x_out, g_one, FIRST_DOT) + dot(flat(x_ref[1 : rows - 1]), g1i_ref[...], FIRST_DOT)
    out_ref[...] = grad.astype(BF16).reshape(out_ref.shape)


def images_kernel(g_ref, g1i_ref, g1o_ref, wr_ref, out_ref):
    _, rows, cols, _ = out_ref.shape
    g_in, g_out = halves(g_ref, g1i_ref)
    inner = (g_in.astype(F32) + dot(g1i_ref[...], wr_ref[...], LAST_DOT)).astype(BF16)
    outer = (g_out.astype(F32) + dot(g1o_ref[...], wr_ref[...], LAST_DOT)).astype(BF16)
    out_ref[0, 0] = outer[:cols]
    out_ref[0, rows - 1] = outer[cols:]
    out_ref[0, 1 : rows - 1] = inner.reshape(rows - 2, cols, -1)


def call(kernel, outs, flops, smem=0, scratch=()):
    def run(*args):
        specs = [
            pl.BlockSpec(memory_space=pltpu.SMEM if i < smem else pltpu.VMEM)
            for i in range(len(args))
        ]
        moved = sum(v.size * v.dtype.itemsize for v in args)
        return pl.pallas_call(
            kernel,
            out_shape=[jax.ShapeDtypeStruct(s, d) for s, d in outs],
            in_specs=specs,
            out_specs=[pl.BlockSpec(memory_space=pltpu.VMEM) for _ in outs],
            scratch_shapes=list(scratch),
            compiler_params=pltpu.CompilerParams(vmem_limit_bytes=VMEM_LIMIT),
            cost_estimate=pl.CostEstimate(flops=flops, bytes_accessed=moved, transcendentals=0),
        )(*args)

    return run


def exchanged(first, last):
    peers = lax.axis_size("space")
    up = [(i, i + 1) for i in range(peers - 1)]
    down = [(i + 1, i) for i in range(peers - 1)]
    return lax.ppermute(last, "space", up), lax.ppermute(first, "space", down)


def scattered(local):
    peers = lax.axis_size("space")
    depth, (_, rows, mid) = peers // 2, local.shape
    far = depth // 2
    place = lax.axis_index("space")
    z, half = place // 2, place % 2
    ring_up = [(i, (i + 2) % peers) for i in range(peers)]
    ring_down = [(i, (i - 2) % peers) for i in range(peers)]
    pairs = local.reshape(depth, 2, rows, mid)

    def mine(block):
        return lax.dynamic_index_in_dim(pairs, block % depth, 0, keepdims=False)

    start = mine(z + far)
    up, down = start[0], start[1]
    for step in range(1, far + 1):
        got_up = lax.ppermute(up, "space", ring_up)
        got_down = lax.ppermute(down, "space", ring_down)
        got_up, got_down = lax.optimization_barrier((got_up, got_down))
        got_up, got_down = got_up.astype(F32), got_down.astype(F32)
        if step == 1:
            got_up = jnp.stack([got_up, jnp.zeros_like(got_up)])
            got_down = jnp.stack([jnp.zeros_like(got_down), got_down])
        if step < far:
            up = (mine(z + far - step).astype(F32) + got_up).astype(BF16)
            down = (mine(z - far + step + depth).astype(F32) + got_down).astype(BF16)
    total = mine(z).astype(F32) + got_up + got_down
    keep = jnp.where(half == 0, total[0], total[1])
    give = jnp.where(half == 0, total[1], total[0]).astype(BF16)
    swap = [(i, i ^ 1) for i in range(peers)]
    return keep + lax.ppermute(give, "space", swap).astype(F32)


def step(images, teacher, w_reduce, w_spatial, w_expand, partners):
    _, rows, cols, channels = images.shape
    mid = w_reduce.shape[1]
    n_dp, n_space = lax.axis_size("dp"), lax.axis_size("space")
    pixels = rows * cols
    chunk = pixels // n_dp
    inside, outside = (rows - 2) * cols, 2 * cols
    split = inside // n_dp
    elems = float(pixels * n_space * channels)
    world = n_dp * n_space
    x = images.reshape(rows, cols, channels)

    t_all = lax.all_to_all(teacher.reshape(n_dp, chunk, channels), "dp", 0, 0, tiled=True)
    first, last = pl.pallas_call(
        edge_kernel,
        grid=(1,),
        in_specs=[
            pl.BlockSpec((1, cols, channels), lambda i: (0, 0, 0)),
            pl.BlockSpec((1, cols, channels), lambda i: (rows - 1, 0, 0)),
            pl.BlockSpec((channels, mid), lambda i: (0, 0)),
        ],
        out_specs=[pl.BlockSpec((cols, mid), lambda i: (0, 0))] * 2,
        out_shape=[jax.ShapeDtypeStruct((cols, mid), BF16)] * 2,
        compiler_params=pltpu.CompilerParams(vmem_limit_bytes=VMEM_LIMIT),
        name="edge",
    )(x, x, w_reduce)
    above, below = exchanged(first, last)
    mac = 2 * cols * mid * mid
    h_one, h_in, s_in = call(
        inner_kernel,
        [
            ((rows, cols, mid), BF16),
            ((inside, mid), BF16),
            ((n_dp, split, channels), BF16),
        ],
        26 * mac,
    )(x, w_reduce, first, last, w_spatial, w_expand)
    h_out, s_all = call(
        outer_kernel, [((outside, mid), BF16), ((n_dp, chunk, channels), BF16)], 26 * mac
    )(h_one, above, below, w_spatial, w_expand, x, s_in)
    s_all = lax.all_to_all(s_all, "dp", 0, 0, tiled=True)

    def gram(base, shape, flops):
        kernel = functools.partial(gram_kernel, base)
        return call(kernel, [(shape, F32)], flops, smem=1)

    (message,) = gram(3, (1, 128), 16 * mac)(partners, t_all)
    (message,) = gram(0, (world, 128), 16 * mac)(partners, message, s_all)
    message = lax.all_to_all(message, ("dp", "space"), 0, 0, tiled=True)
    grads, loss = call(
        functools.partial(grad_kernel, elems),
        [((n_dp, chunk, channels), BF16), ((1, 1), F32)],
        mac,
        smem=1,
    )(partners, message, s_all)
    grads = lax.all_to_all(grads, "dp", 0, 0, tiled=True)
    g_two, first, last = call(
        back_kernel, [((rows, cols, mid), BF16), ((cols, mid), BF16), ((cols, mid), BF16)], 16 * mac
    )(grads, h_in, h_out, w_expand)
    over, under = exchanged(first, last)
    part, width = channels // n_space, mid // n_space
    early, g1_in = call(
        window_kernel,
        [((n_space, part + 9 * width, mid), BF16), ((inside, mid), BF16)],
        70 * mac,
        scratch=[pltpu.VMEM((rows + 2, cols, mid), BF16)],
    )(grads, h_in, h_out, g_two, h_one, above, below, w_spatial)
    late, g1_out = call(
        backward_kernel, [((n_space, part, mid), BF16), ((outside, mid), BF16)], 34 * mac
    )(g_two, over, under, h_one, w_spatial, x, g1_in)
    (g_images,) = call(
        images_kernel, [((1, rows, cols, channels), BF16)], 16 * mac
    )(grads, g1_in, g1_out, w_reduce)
    early, late = scattered(early), scattered(late)
    grad_expand = early[:part].T[None]
    grad_reduce = late[None]
    grad_spatial = early[part:].reshape(3, 3, width, mid).swapaxes(2, 3)[None]
    return loss[0, 0], g_images, grad_reduce, grad_spatial, grad_expand


def solution(mesh):
    return jax.shard_map(
        step,
        mesh=mesh,
        in_specs=(P("dp", "space", None, None), P("dp", "space", None, None), P(), P(), P(), P()),
        out_specs=(
            P(),
            P("dp", "space", None, None),
            P("dp", "space", None),
            P("dp", None, None, None, "space"),
            P("dp", None, "space"),
        ),
        check_vma=False,
    )
```

time: 194 us -> 170 us (0.88)
  the two profiles are of different devices: /device:TPU:8 before, /device:TPU:4 now
where the time goes in v2:
time: 170 us; the launch traced here: 169 us
  waiting for transfers between devices  60.1 us (35%)
  starting transfers between devices  56.7 us (33%)
  blocking collectives  23.1 us (14%)
  Pallas kernels  11.9 us (7%)
  local copies, waits for them, and re-layouts  8.76 us (5%)
  other arithmetic  7.36 us (4%)
    ppermute x8, starting transfers between devices, scattered(): got_down = lax.ppermute(down, 'space', ring_down)  25.6 us
    all_to_all x1, blocking collectives, step(): message = lax.all_to_all(message, ('dp', 'space'), 0, 0, tiled=True)  23.1 us
    all_to_all x1, waiting for transfers between devices, step(): grads = lax.all_to_all(grads, 'dp', 0, 0, tiled=True)  16.4 us
    ppermute x4, starting transfers between devices, exchanged(): return (lax.ppermute(last, 'space', up), lax.ppermute(first, 'space', down))  14.8 us
    all_to_all x1, waiting for transfers between devices, step(): s_all = lax.all_to_all(s_all, 'dp', 0, 0, tiled=True)  14.4 us
    ppermute x8, waiting for transfers between devices, scattered(): got_up = lax.ppermute(up, 'space', ring_up)  11.9 us
    ppermute x4, waiting for transfers between devices, exchanged(): return (lax.ppermute(last, 'space', up), lax.ppermute(first, 'space', down))  11.7 us
    pallas_call x9, Pallas kernels, run(): pl.pallas_call(kernel, out_shape=[jax.ShapeDtypeStruct(s, d) for s, d in...  11.6 us
  transfers between devices with their start and end apart: 25, of which 10 were waited for; matrix products, arithmetic and copies ran while one was open for 3% of the time, Pallas kernels for 4%

profile of v2, /device:TPU:4, one launch (start us, length us, event | category | flops | bytes accessed | tf_op | source)
XLA Modules:
  0.0 169.2 jit_solution(1960093470216705912)
XLA Ops:
  0.7 5.4 %all-to-all-start = ((bf16[16,32,1024]{2,1,0:T(8,128)(2,1)}), bf16[16,32,1024]{2,1,0:T(8,128)(2,1)}, u32[]{:S(2)}, u32[]{:S(2)}) async-start(bf16[16,32,1024]{2,1,0:T(8,128)(2,1)} %bitcast.101), calls=%async_computation | async-start | bytes 2097152 | tf_op jit(solution)/shard_map/all_to_all | solution.py:293
  6.1 0.0 copy-start.2
  6.1 0.3 edge.1
  6.4 4.2 %collective-permute-start = (bf16[128,256]{1,0:T(8,128)(2,1)S(1)}, bf16[128,256]{1,0:T(8,128)(2,1)S(1)}, u32[]{:S(2)}, u32[]{:S(2)}) collective-permute-start(bf16[128,256]{1,0:T(8,128)(2,1)S(1)} %get-tuple-element.38.last_ref), channel_id=1, source_target_pairs={{0,1},{1,2},{2,3},{3,4},{4,5},{5,6},{6,7},{7,8},{8,9},{9,10},{10,1... | collective-permute-start | bytes 196616 | tf_op jit(solution)/shard_map/ppermute | solution.py:245
  10.6 3.3 %collective-permute-start.1 = (bf16[128,256]{1,0:T(8,128)(2,1)S(1)}, bf16[128,256]{1,0:T(8,128)(2,1)S(1)}, u32[]{:S(2)}, u32[]{:S(2)}) collective-permute-start(bf16[128,256]{1,0:T(8,128)(2,1)S(1)} %get-tuple-element.37.first_ref), channel_id=1, source_target_pairs={{1,0},{2,1},{3,2},{4,3},{5,4},{6,5},{7,6},{8,7},{9,8},{10,9},{11,1... | collective-permute-start | bytes 196616 | tf_op jit(solution)/shard_map/ppermute | solution.py:245
  13.9 1.1 shard_map.102
  15.1 0.6 copy-done.13
  15.7 7.1 %collective-permute-done.above_ref = bf16[128,256]{1,0:T(8,128)(2,1)S(1)} collective-permute-done((bf16[128,256]{1,0:T(8,128)(2,1)S(1)}, bf16[128,256]{1,0:T(8,128)(2,1)S(1)}, u32[]{:S(2)}, u32[]{:S(2)}) %collective-permute-start) | collective-permute-done | bytes 65568 | tf_op jit(solution)/shard_map/ppermute | solution.py:245
  22.8 0.8 shard_map.103
  23.6 1.0 copy-done.9
  24.6 0.7 copy-done.16
  25.2 0.6 copy-done.21
  25.9 0.6 copy-done.23
  26.5 6.2 %all-to-all-start.1 = ((bf16[16,32,1024]{2,1,0:T(8,128)(2,1)}), bf16[16,32,1024]{2,1,0:T(8,128)(2,1)S(1)}, u32[]{:S(2)}, u32[]{:S(2)}) async-start(bf16[16,32,1024]{2,1,0:T(8,128)(2,1)} %copy-done.9), calls=%async_computation.1 | async-start | bytes 2097152 | tf_op jit(solution)/shard_map/all_to_all | solution.py:321
  32.7 2.1 %shard_map.101.refs_0_ = f32[1,128]{1,0:T(1,128)S(1)} custom-call(s32[2,16]{1,0:T(2,128)S(1)} %copy-done.25, bf16[16,32,1024]{2,1,0:T(8,128)(2,1)} %all-to-all-done.refs_0_), custom_call_target="tpu_custom_call" | custom-call | flops 268435456 | bytes 1048704 | tf_op jit(solution)/shard_map/pallas_call | solution.py:228
  34.8 14.4 %all-to-all-done.1.refs_1_.s_ref = bf16[16,32,1024]{2,1,0:T(8,128)(2,1)S(1)} async-done(((bf16[16,32,1024]{2,1,0:T(8,128)(2,1)}), bf16[16,32,1024]{2,1,0:T(8,128)(2,1)S(1)}, u32[]{:S(2)}, u32[]{:S(2)}) %all-to-all-start.1) | async-done | bytes 1048608 | tf_op jit(solution)/shard_map/all_to_all | solution.py:321
  49.2 1.4 shard_map.104
  50.7 23.1 %all_to_all.26 = f32[256,1,128]{2,1,0:T(1,128)S(1)} all-to-all(f32[256,1,128]{2,1,0:T(1,128)S(1)} %bitcast.99), channel_id=1, replica_groups=mesh['dp'=16,'space'=16] {'dp','space'}, dimensions={0} | all-to-all | bytes 262144 | tf_op jit(solution)/shard_map/all_to_all | solution.py:329
  73.8 1.8 %shard_map.105 = (bf16[16,32,1024]{2,1,0:T(8,128)(2,1)S(1)}, f32[1,1]{1,0:T(1,128)}) custom-call(s32[2,16]{1,0:T(2,128)S(1)} %copy-done.25, f32[256,128]{1,0:T(8,128)S(1)} %bitcast.100, bf16[16,32,1024]{2,1,0:T(8,128)(2,1)S(1)} %all-to-all-done.1.refs_1_.s_ref), custom_call_target="tpu_custom_call" | custom-call | flops 16777216 | bytes 1179776 | tf_op jit(solution)/shard_map/pallas_call | solution.py:228
  75.6 1.0 copy-done.8
  76.5 3.7 %all-to-all-start.3 = ((bf16[16,32,1024]{2,1,0:T(8,128)(2,1)}), bf16[16,32,1024]{2,1,0:T(8,128)(2,1)S(1)}, u32[]{:S(2)}, u32[]{:S(2)}) async-start(bf16[16,32,1024]{2,1,0:T(8,128)(2,1)} %copy-done.8), calls=%async_computation.3 | async-start | bytes 2097152 | tf_op jit(solution)/shard_map/all_to_all | solution.py:336
  80.3 16.4 %all-to-all-done.3.g_ref = bf16[16,32,1024]{2,1,0:T(8,128)(2,1)S(1)} async-done(((bf16[16,32,1024]{2,1,0:T(8,128)(2,1)}), bf16[16,32,1024]{2,1,0:T(8,128)(2,1)S(1)}, u32[]{:S(2)}, u32[]{:S(2)}) %all-to-all-start.3) | async-done | bytes 1048608 | tf_op jit(solution)/shard_map/all_to_all | solution.py:336
  96.7 1.0 copy-done.3
  97.7 0.9 copy-done.14
  98.6 0.9 copy-done.17
  99.6 0.5 shard_map.106
  100.0 4.9 %collective-permute-start.2 = (bf16[128,256]{1,0:T(8,128)(2,1)S(1)}, bf16[128,256]{1,0:T(8,128)(2,1)S(1)}, u32[]{:S(2)}, u32[]{:S(2)}) collective-permute-start(bf16[128,256]{1,0:T(8,128)(2,1)S(1)} %get-tuple-element.48), channel_id=1, source_target_pairs={{0,1},{1,2},{2,3},{3,4},{4,5},{5,6},{6,7},{7,8},{8,9},{9,10},{10,1... | collective-permute-start | bytes 196616 | tf_op jit(solution)/shard_map/ppermute | solution.py:245
  105.0 2.4 %collective-permute-start.3 = (bf16[128,256]{1,0:T(8,128)(2,1)S(1)}, bf16[128,256]{1,0:T(8,128)(2,1)S(1)}, u32[]{:S(2)}, u32[]{:S(2)}) collective-permute-start(bf16[128,256]{1,0:T(8,128)(2,1)S(1)} %get-tuple-element.49), channel_id=1, source_target_pairs={{1,0},{2,1},{3,2},{4,3},{5,4},{6,5},{7,6},{8,7},{9,8},{10,9},{11,1... | collective-permute-start | bytes 196616 | tf_op jit(solution)/shard_map/ppermute | solution.py:245
  107.4 1.4 shard_map.107
  108.9 4.6 %collective-permute-done.3.below_ref = bf16[128,256]{1,0:T(8,128)(2,1)S(1)} collective-permute-done((bf16[128,256]{1,0:T(8,128)(2,1)S(1)}, bf16[128,256]{1,0:T(8,128)(2,1)S(1)}, u32[]{:S(2)}, u32[]{:S(2)}) %collective-permute-start.3) | collective-permute-done | bytes 65568 | tf_op jit(solution)/shard_map/ppermute | solution.py:245
  113.5 1.1 shard_map.108
  114.7 0.4 collective-permute-start.4
  115.1 2.9 %collective-permute-start.5 = (bf16[64,256]{1,0:T(8,128)(2,1)S(1)}, bf16[64,256]{1,0:T(8,128)(2,1)S(1)}, u32[]{:S(2)}, u32[]{:S(2)}) collective-permute-start(bf16[64,256]{1,0:T(8,128)(2,1)S(1)} %get-tuple-element.83), channel_id=1, source_target_pairs={{0,14},{1,15},{2,0},{3,1},{4,2},{5,3},{6,4},{7,5},{8,6},{9,7},{10,... | collective-permute-start | bytes 98312 | tf_op jit(solution)/shard_map/ppermute | solution.py:265
  118.0 0.1 collective-permute-start.13
  118.1 3.2 %collective-permute-start.14 = (bf16[208,256]{1,0:T(8,128)(2,1)S(1)}, bf16[208,256]{1,0:T(8,128)(2,1)S(1)}, u32[]{:S(2)}, u32[]{:S(2)}) collective-permute-start(bf16[208,256]{1,0:T(8,128)(2,1)S(1)} %get-tuple-element.75), channel_id=1, source_target_pairs={{0,14},{1,15},{2,0},{3,1},{4,2},{5,3},{6,4},{7,5},{8,6},{9,7},{10,... | collective-permute-start | bytes 319496 | tf_op jit(solution)/shard_map/ppermute | solution.py:265
  121.4 0.1 collective-permute-start.6
  121.5 3.2 %collective-permute-start.7 = (bf16[2,64,256]{2,1,0:T(8,128)(2,1)S(1)}, bf16[2,64,256]{2,1,0:T(8,128)(2,1)S(1)}, u32[]{:S(2)}, u32[]{:S(2)}) collective-permute-start(bf16[2,64,256]{2,1,0:T(8,128)(2,1)S(1)} %get-tuple-element.81), channel_id=1, source_target_pairs={{0,14},{1,15},{2,0},{3,1},{4,2},{5,3},{6,4},{7,5},{8,6},{9,7},{10,... | collective-permute-start | bytes 196616 | tf_op jit(solution)/shard_map/ppermute | solution.py:265
  124.7 2.2 %collective-permute-done.6 = bf16[2,64,256]{2,1,0:T(8,128)(2,1)S(1)} collective-permute-done((bf16[2,64,256]{2,1,0:T(8,128)(2,1)S(1)}, bf16[2,64,256]{2,1,0:T(8,128)(2,1)S(1)}, u32[]{:S(2)}, u32[]{:S(2)}) %collective-permute-start.6) | collective-permute-done | bytes 65568 | tf_op jit(solution)/shard_map/ppermute | solution.py:264
  127.0 0.9 fusion.8
  127.9 0.1 collective-permute-start.8
  128.0 3.3 %collective-permute-start.9 = (bf16[2,64,256]{2,1,0:T(8,128)(2,1)S(1)}, bf16[2,64,256]{2,1,0:T(8,128)(2,1)S(1)}, u32[]{:S(2)}, u32[]{:S(2)}) collective-permute-start(bf16[2,64,256]{2,1,0:T(8,128)(2,1)S(1)} %get-tuple-element.79), channel_id=1, source_target_pairs={{0,14},{1,15},{2,0},{3,1},{4,2},{5,3},{6,4},{7,5},{8,6},{9,7},{10,... | collective-permute-start | bytes 196616 | tf_op jit(solution)/shard_map/ppermute | solution.py:265
  131.3 1.9 %fusion.2 = (bf16[2,208,256]{2,1,0:T(8,128)(2,1)}, bf16[2,208,256]{2,1,0:T(8,128)(2,1)}) fusion(bf16[1,208,256]{2,1,0:T(8,128)(2,1)S(1)} %bitcast.104, bf16[8,2,208,256]{3,2,1,0:T(8,128)(2,1)} %bitcast.90, s32[]{:T(128)S(6)} %select_n.142, bf16[1,208,256]{2,1,0:T(8,128)(2,1)S(1)} %bitcast.103, s32[]{:T(128)S(6)} %select_n.138), kind=kLoop, calls=%fused_computation.5 | loop fusion | flops 851968 | bytes 1064968 | tf_op jit(solution)/shard_map/convert_element_type | solution.py:273
  133.1 3.2 %collective-permute-start.16 = (bf16[2,208,256]{2,1,0:T(8,128)(2,1)}, bf16[2,208,256]{2,1,0:T(8,128)(2,1)}, u32[]{:S(2)}, u32[]{:S(2)}) collective-permute-start(bf16[2,208,256]{2,1,0:T(8,128)(2,1)} %get-tuple-element.73), channel_id=1, source_target_pairs={{0,14},{1,15},{2,0},{3,1},{4,2},{5,3},{6,4},{7,5},{8,6},{9,7},{10,... | collective-permute-start | bytes 638984 | tf_op jit(solution)/shard_map/ppermute | solution.py:265
  136.4 1.6 fusion.7
  137.9 3.2 %collective-permute-start.11 = (bf16[2,64,256]{2,1,0:T(8,128)(2,1)}, bf16[2,64,256]{2,1,0:T(8,128)(2,1)}, u32[]{:S(2)}, u32[]{:S(2)}) collective-permute-start(bf16[2,64,256]{2,1,0:T(8,128)(2,1)} %get-tuple-element.77), channel_id=1, source_target_pairs={{0,14},{1,15},{2,0},{3,1},{4,2},{5,3},{6,4},{7,5},{8,6},{9,7},{10,... | collective-permute-start | bytes 196616 | tf_op jit(solution)/shard_map/ppermute | solution.py:265
  141.2 1.4 shard_map.109
  142.6 1.8 %collective-permute-done.10 = bf16[2,64,256]{2,1,0:T(8,128)(2,1)} collective-permute-done((bf16[2,64,256]{2,1,0:T(8,128)(2,1)}, bf16[2,64,256]{2,1,0:T(8,128)(2,1)}, u32[]{:S(2)}, u32[]{:S(2)}) %collective-permute-start.10) | collective-permute-done | bytes 65568 | tf_op jit(solution)/shard_map/ppermute | solution.py:264
  144.5 1.1 fusion.1
  145.6 0.1 collective-permute-start.17
  145.7 3.3 %collective-permute-start.18 = (bf16[2,208,256]{2,1,0:T(8,128)(2,1)S(1)}, bf16[2,208,256]{2,1,0:T(8,128)(2,1)S(1)}, u32[]{:S(2)}, u32[]{:S(2)}) collective-permute-start(bf16[2,208,256]{2,1,0:T(8,128)(2,1)S(1)} %get-tuple-element.71), channel_id=1, source_target_pairs={{0,14},{1,15},{2,0},{3,1},{4,2},{5,3},{6,4},{7,5},{8,6},{9,7},{10,... | collective-permute-start | bytes 638984 | tf_op jit(solution)/shard_map/ppermute | solution.py:265
  149.0 0.9 fusion.13
  149.9 4.2 %collective-permute-done.17 = bf16[2,208,256]{2,1,0:T(8,128)(2,1)S(1)} collective-permute-done((bf16[2,208,256]{2,1,0:T(8,128)(2,1)S(1)}, bf16[2,208,256]{2,1,0:T(8,128)(2,1)S(1)}, u32[]{:S(2)}, u32[]{:S(2)}) %collective-permute-start.17) | collective-permute-done | bytes 213024 | tf_op jit(solution)/shard_map/ppermute | solution.py:264
  154.1 0.1 fusion
  154.2 0.1 collective-permute-start.19
  154.3 3.2 %collective-permute-start.20 = (bf16[2,208,256]{2,1,0:T(8,128)(2,1)S(1)}, bf16[2,208,256]{2,1,0:T(8,128)(2,1)S(1)}, u32[]{:S(2)}, u32[]{:S(2)}) collective-permute-start(bf16[2,208,256]{2,1,0:T(8,128)(2,1)S(1)} %get-tuple-element.69), channel_id=1, source_target_pairs={{0,14},{1,15},{2,0},{3,1},{4,2},{5,3},{6,4},{7,5},{8,6},{9,7},{10,... | collective-permute-start | bytes 638984 | tf_op jit(solution)/shard_map/ppermute | solution.py:265
  157.6 0.1 collective-permute-start.12
  157.7 3.7 %collective-permute-done.19 = bf16[2,208,256]{2,1,0:T(8,128)(2,1)S(1)} collective-permute-done((bf16[2,208,256]{2,1,0:T(8,128)(2,1)S(1)}, bf16[2,208,256]{2,1,0:T(8,128)(2,1)S(1)}, u32[]{:S(2)}, u32[]{:S(2)}) %collective-permute-start.19) | collective-permute-done | bytes 213024 | tf_op jit(solution)/shard_map/ppermute | solution.py:264
  161.4 0.1 fusion.6
  161.5 0.1 collective-permute-start.21
  161.6 1.5 collective-permute-done.12
  163.1 0.6 fusion.15
  163.7 4.1 %collective-permute-done.21 = bf16[208,256]{1,0:T(8,128)(2,1)S(1)} collective-permute-done((bf16[208,256]{1,0:T(8,128)(2,1)S(1)}, bf16[208,256]{1,0:T(8,128)(2,1)S(1)}, u32[]{:S(2)}, u32[]{:S(2)}) %collective-permute-start.21) | collective-permute-done | bytes 106528 | tf_op jit(solution)/shard_map/ppermute | solution.py:278
  167.8 0.7 slice.52
  168.5 0.6 slice_bitcast_fusion
  (65 shorter events, 0.3 us)
Async XLA Ops:
  0.6 5.5 %copy-start = (bf16[1,4,128,1024]{3,2,1,0:T(8,128)(2,1)S(1)}, bf16[1,4,128,1024]{3,2,1,0:T(8,128)(2,1)}, u32[]{:S(2)}) copy-start(bf16[1,4,128,1024]{3,2,1,0:T(8,128)(2,1)} %param.6) | copy-start | bytes 3145732
  0.6 5.5 %copy-start.4 = (bf16[1024,256]{1,0:T(8,128)(2,1)S(1)}, bf16[1024,256]{1,0:T(8,128)(2,1)}, u32[]{:S(2)}) copy-start(bf16[1024,256]{1,0:T(8,128)(2,1)} %wr_ref.3) | copy-start | bytes 1572868
  0.7 25.9 %all-to-all-start = ((bf16[16,32,1024]{2,1,0:T(8,128)(2,1)}), bf16[16,32,1024]{2,1,0:T(8,128)(2,1)}, u32[]{:S(2)}, u32[]{:S(2)}) async-start(bf16[16,32,1024]{2,1,0:T(8,128)(2,1)} %bitcast.101), calls=%async_computation | async-start | bytes 2097152 | tf_op jit(solution)/shard_map/all_to_all | solution.py:293
  6.1 7.9 %copy-start.1 = (bf16[3,3,256,256]{3,2,1,0:T(8,128)(2,1)S(1)}, bf16[3,3,256,256]{3,2,1,0:T(8,128)(2,1)}, u32[]{:S(2)}) copy-start(bf16[3,3,256,256]{3,2,1,0:T(8,128)(2,1)} %ws_ref.7) | copy-start | bytes 3538948
  6.1 7.9 %copy-start.2 = (bf16[256,1024]{1,0:T(8,128)(2,1)S(1)}, bf16[256,1024]{1,0:T(8,128)(2,1)}, u32[]{:S(2)}) copy-start(bf16[256,1024]{1,0:T(8,128)(2,1)} %we_ref.5) | copy-start | bytes 1572868
  6.4 16.3 %collective-permute-start = (bf16[128,256]{1,0:T(8,128)(2,1)S(1)}, bf16[128,256]{1,0:T(8,128)(2,1)S(1)}, u32[]{:S(2)}, u32[]{:S(2)}) collective-permute-start(bf16[128,256]{1,0:T(8,128)(2,1)S(1)} %get-tuple-element.38.last_ref), channel_id=1, source_target_pairs={{0,1},{1,2},{2,3},{3,4},{4,5},{5,6},{6,7},{7,8},{8,9},{9,10},{10,1... | collective-permute-start | bytes 196616 | tf_op jit(solution)/shard_map/ppermute | solution.py:245
  10.6 12.2 %collective-permute-start.1 = (bf16[128,256]{1,0:T(8,128)(2,1)S(1)}, bf16[128,256]{1,0:T(8,128)(2,1)S(1)}, u32[]{:S(2)}, u32[]{:S(2)}) collective-permute-start(bf16[128,256]{1,0:T(8,128)(2,1)S(1)} %get-tuple-element.37.first_ref), channel_id=1, source_target_pairs={{1,0},{2,1},{3,2},{4,3},{5,4},{6,5},{7,6},{8,7},{9,8},{10,9},{11,1... | collective-permute-start | bytes 196616 | tf_op jit(solution)/shard_map/ppermute | solution.py:245
  15.0 0.7 copy-start.13
  23.6 1.0 copy-start.9
  24.6 0.7 copy-start.16
  25.2 0.6 copy-start.21
  25.9 0.6 copy-start.23
  26.5 6.2 %copy-start.25 = (s32[2,16]{1,0:T(2,128)S(1)}, s32[2,16]{1,0:T(2,128)}, u32[]{:S(2)}) copy-start(s32[2,16]{1,0:T(2,128)} %parts_ref.5) | copy-start | bytes 388
  26.5 22.7 %all-to-all-start.1 = ((bf16[16,32,1024]{2,1,0:T(8,128)(2,1)}), bf16[16,32,1024]{2,1,0:T(8,128)(2,1)S(1)}, u32[]{:S(2)}, u32[]{:S(2)}) async-start(bf16[16,32,1024]{2,1,0:T(8,128)(2,1)} %copy-done.9), calls=%async_computation.1 | async-start | bytes 2097152 | tf_op jit(solution)/shard_map/all_to_all | solution.py:321
  75.5 1.0 copy-start.8
  76.5 20.2 %all-to-all-start.3 = ((bf16[16,32,1024]{2,1,0:T(8,128)(2,1)}), bf16[16,32,1024]{2,1,0:T(8,128)(2,1)S(1)}, u32[]{:S(2)}, u32[]{:S(2)}) async-start(bf16[16,32,1024]{2,1,0:T(8,128)(2,1)} %copy-done.8), calls=%async_computation.3 | async-start | bytes 2097152 | tf_op jit(solution)/shard_map/all_to_all | solution.py:336
  96.7 1.0 copy-start.3
  97.7 0.9 copy-start.14
  98.6 0.9 copy-start.17
  99.5 7.9 %copy-start.15 = (bf16[256,256]{1,0:T(8,128)(2,1)S(1)}, bf16[256,256]{1,0:T(8,128)(2,1)}, u32[]{:S(2)}) copy-start(bf16[256,256]{1,0:T(8,128)(2,1)} %copy-done.13) | copy-start | bytes 393220
  99.5 7.9 %copy-start.18 = (bf16[256,256]{1,0:T(8,128)(2,1)S(1)}, bf16[256,256]{1,0:T(8,128)(2,1)}, u32[]{:S(2)}) copy-start(bf16[256,256]{1,0:T(8,128)(2,1)} %copy-done.16) | copy-start | bytes 393220
  99.5 7.9 %copy-start.22 = (bf16[128,256]{1,0:T(8,128)(2,1)S(1)}, bf16[128,256]{1,0:T(8,128)(2,1)}, u32[]{:S(2)}) copy-start(bf16[128,256]{1,0:T(8,128)(2,1)} %copy-done.21) | copy-start | bytes 196612
  99.5 7.9 %copy-start.24 = (bf16[128,256]{1,0:T(8,128)(2,1)S(1)}, bf16[128,256]{1,0:T(8,128)(2,1)}, u32[]{:S(2)}) copy-start(bf16[128,256]{1,0:T(8,128)(2,1)} %copy-done.23) | copy-start | bytes 196612
  100.0 8.8 %collective-permute-start.2 = (bf16[128,256]{1,0:T(8,128)(2,1)S(1)}, bf16[128,256]{1,0:T(8,128)(2,1)S(1)}, u32[]{:S(2)}, u32[]{:S(2)}) collective-permute-start(bf16[128,256]{1,0:T(8,128)(2,1)S(1)} %get-tuple-element.48), channel_id=1, source_target_pairs={{0,1},{1,2},{2,3},{3,4},{4,5},{5,6},{6,7},{7,8},{8,9},{9,10},{10,1... | collective-permute-start | bytes 196616 | tf_op jit(solution)/shard_map/ppermute | solution.py:245
  105.0 8.6 %collective-permute-start.3 = (bf16[128,256]{1,0:T(8,128)(2,1)S(1)}, bf16[128,256]{1,0:T(8,128)(2,1)S(1)}, u32[]{:S(2)}, u32[]{:S(2)}) collective-permute-start(bf16[128,256]{1,0:T(8,128)(2,1)S(1)} %get-tuple-element.49), channel_id=1, source_target_pairs={{1,0},{2,1},{3,2},{4,3},{5,4},{6,5},{7,6},{8,7},{9,8},{10,9},{11,1... | collective-permute-start | bytes 196616 | tf_op jit(solution)/shard_map/ppermute | solution.py:245
  108.9 9.1 %copy-start.6 = (bf16[16,208,256]{2,1,0:T(8,128)(2,1)}, bf16[16,208,256]{2,1,0:T(8,128)(2,1)S(1)}, u32[]{:S(2)}) copy-start(bf16[16,208,256]{2,1,0:T(8,128)(2,1)S(1)} %get-tuple-element.60) | copy-start | bytes 5111812
  108.9 9.1 %copy-start.10 = (bf16[256,256]{1,0:T(8,128)(2,1)}, bf16[256,256]{1,0:T(8,128)(2,1)S(1)}, u32[]{:S(2)}) copy-start(bf16[256,256]{1,0:T(8,128)(2,1)S(1)} %get-tuple-element.47.g1i_ref) | copy-start | bytes 393220
  114.6 6.7 %copy-start.12 = (bf16[16,64,256]{2,1,0:T(8,128)(2,1)}, bf16[16,64,256]{2,1,0:T(8,128)(2,1)S(1)}, u32[]{:S(2)}) copy-start(bf16[16,64,256]{2,1,0:T(8,128)(2,1)S(1)} %get-tuple-element.51) | copy-start | bytes 1572868
  114.6 6.8 %copy-start.19 = (bf16[256,256]{1,0:T(8,128)(2,1)}, bf16[256,256]{1,0:T(8,128)(2,1)S(1)}, u32[]{:S(2)}) copy-start(bf16[256,256]{1,0:T(8,128)(2,1)S(1)} %get-tuple-element.50.g1o_ref) | copy-start | bytes 393220
  114.6 26.6 %copy-start.5 = (bf16[1024,256]{1,0:T(8,128)(2,1)S(1)}, bf16[1024,256]{1,0:T(8,128)(2,1)}, u32[]{:S(2)}) copy-start(bf16[1024,256]{1,0:T(8,128)(2,1)} %wr_ref.3) | copy-start | bytes 1572868
  114.7 6.7 %collective-permute-start.4 = (bf16[64,256]{1,0:T(8,128)(2,1)S(1)}, bf16[64,256]{1,0:T(8,128)(2,1)S(1)}, u32[]{:S(2)}, u32[]{:S(2)}) collective-permute-start(bf16[64,256]{1,0:T(8,128)(2,1)S(1)} %get-tuple-element.84), channel_id=1, source_target_pairs={{0,2},{1,3},{2,4},{3,5},{4,6},{5,7},{6,8},{7,9},{8,10},{9,11},{10,... | collective-permute-start | bytes 98312 | tf_op jit(solution)/shard_map/ppermute | solution.py:264
  115.1 6.2 %collective-permute-start.5 = (bf16[64,256]{1,0:T(8,128)(2,1)S(1)}, bf16[64,256]{1,0:T(8,128)(2,1)S(1)}, u32[]{:S(2)}, u32[]{:S(2)}) collective-permute-start(bf16[64,256]{1,0:T(8,128)(2,1)S(1)} %get-tuple-element.83), channel_id=1, source_target_pairs={{0,14},{1,15},{2,0},{3,1},{4,2},{5,3},{6,4},{7,5},{8,6},{9,7},{10,... | collective-permute-start | bytes 98312 | tf_op jit(solution)/shard_map/ppermute | solution.py:265
  118.0 23.2 %copy-start.11 = (bf16[256,256]{1,0:T(8,128)(2,1)S(1)}, bf16[256,256]{1,0:T(8,128)(2,1)}, u32[]{:S(2)}) copy-start(bf16[256,256]{1,0:T(8,128)(2,1)} %copy-done.10) | copy-start | bytes 393220
  118.0 6.7 %collective-permute-start.13 = (bf16[208,256]{1,0:T(8,128)(2,1)S(1)}, bf16[208,256]{1,0:T(8,128)(2,1)S(1)}, u32[]{:S(2)}, u32[]{:S(2)}) collective-permute-start(bf16[208,256]{1,0:T(8,128)(2,1)S(1)} %get-tuple-element.76), channel_id=1, source_target_pairs={{0,2},{1,3},{2,4},{3,5},{4,6},{5,7},{6,8},{7,9},{8,10},{9,11},{10,... | collective-permute-start | bytes 319496 | tf_op jit(solution)/shard_map/ppermute | solution.py:264
  118.1 6.6 %collective-permute-start.14 = (bf16[208,256]{1,0:T(8,128)(2,1)S(1)}, bf16[208,256]{1,0:T(8,128)(2,1)S(1)}, u32[]{:S(2)}, u32[]{:S(2)}) collective-permute-start(bf16[208,256]{1,0:T(8,128)(2,1)S(1)} %get-tuple-element.75), channel_id=1, source_target_pairs={{0,14},{1,15},{2,0},{3,1},{4,2},{5,3},{6,4},{7,5},{8,6},{9,7},{10,... | collective-permute-start | bytes 319496 | tf_op jit(solution)/shard_map/ppermute | solution.py:265
  121.4 19.8 %copy-start.20 = (bf16[256,256]{1,0:T(8,128)(2,1)S(1)}, bf16[256,256]{1,0:T(8,128)(2,1)}, u32[]{:S(2)}) copy-start(bf16[256,256]{1,0:T(8,128)(2,1)} %copy-done.19) | copy-start | bytes 393220
  121.4 5.6 %collective-permute-start.6 = (bf16[2,64,256]{2,1,0:T(8,128)(2,1)S(1)}, bf16[2,64,256]{2,1,0:T(8,128)(2,1)S(1)}, u32[]{:S(2)}, u32[]{:S(2)}) collective-permute-start(bf16[2,64,256]{2,1,0:T(8,128)(2,1)S(1)} %get-tuple-element.82), channel_id=1, source_target_pairs={{0,2},{1,3},{2,4},{3,5},{4,6},{5,7},{6,8},{7,9},{8,10},{9,11},{10,... | collective-permute-start | bytes 196616 | tf_op jit(solution)/shard_map/ppermute | solution.py:264
  121.5 5.5 %collective-permute-start.7 = (bf16[2,64,256]{2,1,0:T(8,128)(2,1)S(1)}, bf16[2,64,256]{2,1,0:T(8,128)(2,1)S(1)}, u32[]{:S(2)}, u32[]{:S(2)}) collective-permute-start(bf16[2,64,256]{2,1,0:T(8,128)(2,1)S(1)} %get-tuple-element.81), channel_id=1, source_target_pairs={{0,14},{1,15},{2,0},{3,1},{4,2},{5,3},{6,4},{7,5},{8,6},{9,7},{10,... | collective-permute-start | bytes 196616 | tf_op jit(solution)/shard_map/ppermute | solution.py:265
  127.9 8.5 %collective-permute-start.8 = (bf16[2,64,256]{2,1,0:T(8,128)(2,1)S(1)}, bf16[2,64,256]{2,1,0:T(8,128)(2,1)S(1)}, u32[]{:S(2)}, u32[]{:S(2)}) collective-permute-start(bf16[2,64,256]{2,1,0:T(8,128)(2,1)S(1)} %get-tuple-element.80), channel_id=1, source_target_pairs={{0,2},{1,3},{2,4},{3,5},{4,6},{5,7},{6,8},{7,9},{8,10},{9,11},{10,... | collective-permute-start | bytes 196616 | tf_op jit(solution)/shard_map/ppermute | solution.py:264
  128.0 8.4 %collective-permute-start.9 = (bf16[2,64,256]{2,1,0:T(8,128)(2,1)S(1)}, bf16[2,64,256]{2,1,0:T(8,128)(2,1)S(1)}, u32[]{:S(2)}, u32[]{:S(2)}) collective-permute-start(bf16[2,64,256]{2,1,0:T(8,128)(2,1)S(1)} %get-tuple-element.79), channel_id=1, source_target_pairs={{0,14},{1,15},{2,0},{3,1},{4,2},{5,3},{6,4},{7,5},{8,6},{9,7},{10,... | collective-permute-start | bytes 196616 | tf_op jit(solution)/shard_map/ppermute | solution.py:265
  133.1 11.3 %copy-start.7 = (bf16[16,208,256]{2,1,0:T(8,128)(2,1)S(1)}, bf16[16,208,256]{2,1,0:T(8,128)(2,1)}, u32[]{:S(2)}) copy-start(bf16[16,208,256]{2,1,0:T(8,128)(2,1)} %copy-done.6) | copy-start | bytes 5111812
  133.1 11.3 %collective-permute-start.15 = (bf16[2,208,256]{2,1,0:T(8,128)(2,1)}, bf16[2,208,256]{2,1,0:T(8,128)(2,1)}, u32[]{:S(2)}, u32[]{:S(2)}) collective-permute-start(bf16[2,208,256]{2,1,0:T(8,128)(2,1)} %get-tuple-element.74), channel_id=1, source_target_pairs={{0,2},{1,3},{2,4},{3,5},{4,6},{5,7},{6,8},{7,9},{8,10},{9,11},{10,... | collective-permute-start | bytes 638984 | tf_op jit(solution)/shard_map/ppermute | solution.py:264
  133.1 11.3 %collective-permute-start.16 = (bf16[2,208,256]{2,1,0:T(8,128)(2,1)}, bf16[2,208,256]{2,1,0:T(8,128)(2,1)}, u32[]{:S(2)}, u32[]{:S(2)}) collective-permute-start(bf16[2,208,256]{2,1,0:T(8,128)(2,1)} %get-tuple-element.73), channel_id=1, source_target_pairs={{0,14},{1,15},{2,0},{3,1},{4,2},{5,3},{6,4},{7,5},{8,6},{9,7},{10,... | collective-permute-start | bytes 638984 | tf_op jit(solution)/shard_map/ppermute | solution.py:265
  137.9 6.5 %collective-permute-start.10 = (bf16[2,64,256]{2,1,0:T(8,128)(2,1)}, bf16[2,64,256]{2,1,0:T(8,128)(2,1)}, u32[]{:S(2)}, u32[]{:S(2)}) collective-permute-start(bf16[2,64,256]{2,1,0:T(8,128)(2,1)} %get-tuple-element.78), channel_id=1, source_target_pairs={{0,2},{1,3},{2,4},{3,5},{4,6},{5,7},{6,8},{7,9},{8,10},{9,11},{10,... | collective-permute-start | bytes 196616 | tf_op jit(solution)/shard_map/ppermute | solution.py:264
  137.9 6.5 %collective-permute-start.11 = (bf16[2,64,256]{2,1,0:T(8,128)(2,1)}, bf16[2,64,256]{2,1,0:T(8,128)(2,1)}, u32[]{:S(2)}, u32[]{:S(2)}) collective-permute-start(bf16[2,64,256]{2,1,0:T(8,128)(2,1)} %get-tuple-element.77), channel_id=1, source_target_pairs={{0,14},{1,15},{2,0},{3,1},{4,2},{5,3},{6,4},{7,5},{8,6},{9,7},{10,... | collective-permute-start | bytes 196616 | tf_op jit(solution)/shard_map/ppermute | solution.py:265
  145.6 8.5 %collective-permute-start.17 = (bf16[2,208,256]{2,1,0:T(8,128)(2,1)S(1)}, bf16[2,208,256]{2,1,0:T(8,128)(2,1)S(1)}, u32[]{:S(2)}, u32[]{:S(2)}) collective-permute-start(bf16[2,208,256]{2,1,0:T(8,128)(2,1)S(1)} %get-tuple-element.72), channel_id=1, source_target_pairs={{0,2},{1,3},{2,4},{3,5},{4,6},{5,7},{6,8},{7,9},{8,10},{9,11},{10,... | collective-permute-start | bytes 638984 | tf_op jit(solution)/shard_map/ppermute | solution.py:264
  145.7 8.4 %collective-permute-start.18 = (bf16[2,208,256]{2,1,0:T(8,128)(2,1)S(1)}, bf16[2,208,256]{2,1,0:T(8,128)(2,1)S(1)}, u32[]{:S(2)}, u32[]{:S(2)}) collective-permute-start(bf16[2,208,256]{2,1,0:T(8,128)(2,1)S(1)} %get-tuple-element.71), channel_id=1, source_target_pairs={{0,14},{1,15},{2,0},{3,1},{4,2},{5,3},{6,4},{7,5},{8,6},{9,7},{10,... | collective-permute-start | bytes 638984 | tf_op jit(solution)/shard_map/ppermute | solution.py:265
  154.2 7.1 %collective-permute-start.19 = (bf16[2,208,256]{2,1,0:T(8,128)(2,1)S(1)}, bf16[2,208,256]{2,1,0:T(8,128)(2,1)S(1)}, u32[]{:S(2)}, u32[]{:S(2)}) collective-permute-start(bf16[2,208,256]{2,1,0:T(8,128)(2,1)S(1)} %get-tuple-element.70), channel_id=1, source_target_pairs={{0,2},{1,3},{2,4},{3,5},{4,6},{5,7},{6,8},{7,9},{8,10},{9,11},{10,... | collective-permute-start | bytes 638984 | tf_op jit(solution)/shard_map/ppermute | solution.py:264
  154.3 7.0 %collective-permute-start.20 = (bf16[2,208,256]{2,1,0:T(8,128)(2,1)S(1)}, bf16[2,208,256]{2,1,0:T(8,128)(2,1)S(1)}, u32[]{:S(2)}, u32[]{:S(2)}) collective-permute-start(bf16[2,208,256]{2,1,0:T(8,128)(2,1)S(1)} %get-tuple-element.69), channel_id=1, source_target_pairs={{0,14},{1,15},{2,0},{3,1},{4,2},{5,3},{6,4},{7,5},{8,6},{9,7},{10,... | collective-permute-start | bytes 638984 | tf_op jit(solution)/shard_map/ppermute | solution.py:265
  157.6 5.5 %collective-permute-start.12 = (bf16[64,256]{1,0:T(8,128)(2,1)S(1)}, bf16[64,256]{1,0:T(8,128)(2,1)S(1)}, u32[]{:S(2)}, u32[]{:S(2)}) collective-permute-start(bf16[64,256]{1,0:T(8,128)(2,1)S(1)} %fusion.16), channel_id=1, source_target_pairs={{0,1},{1,0},{2,3},{3,2},{4,5},{5,4},{6,7},{7,6},{8,9},{9,8},{10,11... | collective-permute-start | bytes 98312 | tf_op jit(solution)/shard_map/ppermute | solution.py:278
  161.5 6.3 %collective-permute-start.21 = (bf16[208,256]{1,0:T(8,128)(2,1)S(1)}, bf16[208,256]{1,0:T(8,128)(2,1)S(1)}, u32[]{:S(2)}, u32[]{:S(2)}) collective-permute-start(bf16[208,256]{1,0:T(8,128)(2,1)S(1)} %fusion.14), channel_id=1, source_target_pairs={{0,1},{1,0},{2,3},{3,2},{4,5},{5,4},{6,7},{7,6},{8,9},{9,8},{10,11... | collective-permute-start | bytes 319496 | tf_op jit(solution)/shard_map/ppermute | solution.py:278

commit v3 on v2

--- a/solution.py
+++ b/solution.py
@@ -70,23 +70,29 @@
     s_ref[...] = jnp.maximum(pre, 0.0).astype(BF16).reshape(s_ref.shape)
 
 
-def outer_kernel(h_ref, above_ref, below_ref, ws_ref, we_ref, x_ref, si_ref, h2_ref, s_ref):
+def outer_kernel(
+    h_ref, h2i_ref, above_ref, below_ref, ws_ref, we_ref, x_ref, si_ref, hp_ref, h2_ref, s_ref
+):
     rows, cols, _ = h_ref.shape
+    devices, split, channels = si_ref.shape
+    inside = h2i_ref.shape[0]
+    s_ref[:, :split] = si_ref[...]
+    hp_ref[0] = above_ref[...]
+    hp_ref[1 : rows + 1] = h_ref[...]
+    hp_ref[rows + 1] = below_ref[...]
     tops = [above_ref[...], h_ref[0], h_ref[1]]
     ends = [h_ref[rows - 2], h_ref[rows - 1], below_ref[...]]
     sources = [jnp.concatenate(pair, axis=0) for pair in zip(tops, ends)]
     h_two = jnp.maximum(widened(taps(sources, ws_ref, ROW_DOT), cols), 0.0).astype(BF16)
-    h2_ref[...] = h_two
+    h2_ref[:inside] = h2i_ref[...]
+    h2_ref[inside:] = h_two
     x_out = jnp.concatenate([x_ref[0], x_ref[rows - 1]], axis=0)
     pre = dot(h_two, we_ref[...], ROW_DOT) + x_out.astype(F32)
-    devices, split, channels = si_ref.shape
-    s_ref[:, :split] = si_ref[...]
     s_ref[:, split:] = jnp.maximum(pre, 0.0).astype(BF16).reshape(devices, -1, channels)
 
 
-def gram_kernel(base, parts_ref, *refs):
-    value_ref, out_ref = refs[-2], refs[-1]
-    images, chunk, _ = value_ref.shape
+def gram_kernel(parts_ref, s_ref, t_ref, out_ref):
+    images, chunk, _ = s_ref.shape
     count = images * chunk
     row = lax.broadcasted_iota(jnp.int32, (count, count), 0)
     col = lax.broadcasted_iota(jnp.int32, (count, count), 1)
@@ -96,17 +102,15 @@
     slot_row = lax.broadcasted_iota(jnp.int32, (images, 128), 0)
     slot = lax.broadcasted_iota(jnp.int32, (images, 128), 1)
     message = jnp.zeros((images, 128), F32)
-    value = flat(value_ref[...])
-    gram = jnp.where(same, dot(value, value, LAST_DOT), 0.0)
-    gram = gram.reshape(images, chunk, count).sum(axis=1)
-    for k in range(3):
-        partner = image if k == 0 else image ^ parts_ref[k - 1, 0]
-        column = jnp.where(other == partner, gram, 0.0).sum(axis=1, keepdims=True)
-        message = message + jnp.where(slot == 8 * slot_row + base + k, column, 0.0)
-    total = message.sum(axis=0, keepdims=True)
-    if len(refs) == 3:
-        total = total + refs[0][...]
-    out_ref[...] = jnp.broadcast_to(total, out_ref.shape)
+    for base, value_ref in ((0, s_ref), (3, t_ref)):
+        value = flat(value_ref[...])
+        gram = jnp.where(same, dot(value, value, LAST_DOT), 0.0)
+        gram = gram.reshape(images, chunk, count).sum(axis=1)
+        for k in range(3):
+            partner = image if k == 0 else image ^ parts_ref[k - 1, 0]
+            column = jnp.where(other == partner, gram, 0.0).sum(axis=1, keepdims=True)
+            message = message + jnp.where(slot == 8 * slot_row + base + k, column, 0.0)
+    out_ref[...] = jnp.broadcast_to(message.sum(axis=0, keepdims=True), out_ref.shape)
 
 
 def grad_kernel(scale, parts_ref, msg_ref, s_ref, g_ref, loss_ref):
@@ -144,38 +148,44 @@
         g_ref[i] = jnp.where(own > 0.0, scale * acc, 0.0).astype(BF16)
 
 
-def halves(g_ref, h2i_ref):
-    split = h2i_ref.shape[0] // g_ref.shape[0]
+def halves(g_ref, inside):
+    split = inside // g_ref.shape[0]
     return flat(g_ref[:, :split]), flat(g_ref[:, split:])
 
 
-def back_kernel(g_ref, h2i_ref, h2o_ref, we_ref, g2_ref, first_ref, last_ref):
+def back_kernel(g_ref, h2_ref, we_ref, g2_ref, first_ref, last_ref):
     rows, cols, _ = g2_ref.shape
-    g_in, g_out = halves(g_ref, h2i_ref)
+    inside = (rows - 2) * cols
+    g_in, g_out = halves(g_ref, inside)
     back = dot(g_out, we_ref[...], LAST_DOT)
-    g_two = jnp.where(h2o_ref[...] > 0, back, 0.0).astype(BF16)
+    g_two = jnp.where(h2_ref[inside:] > 0, back, 0.0).astype(BF16)
     first_ref[...] = g_two[:cols]
     last_ref[...] = g_two[cols:]
     g2_ref[0] = g_two[:cols]
     g2_ref[rows - 1] = g_two[cols:]
     back = dot(g_in, we_ref[...], LAST_DOT)
-    g_two = jnp.where(h2i_ref[...] > 0, back, 0.0).astype(BF16)
+    g_two = jnp.where(h2_ref[:inside] > 0, back, 0.0).astype(BF16)
     g2_ref[1 : rows - 1] = g_two.reshape(rows - 2, cols, -1)
 
 
+def farthest(place_ref, local_ref, up_ref, down_ref):
+    depth = local_ref.shape[0] // 2
+    block = 2 * ((place_ref[0] // 2 + depth // 2) % depth)
+    up_ref[...] = local_ref[block]
+    down_ref[...] = local_ref[block + 1]
+
+
 def window_kernel(
-    g_ref, h2i_ref, h2o_ref, g2_ref, h_ref, above_ref, below_ref, ws_ref, out_ref, g1_ref, hp_ref
+    place_ref, g_ref, h2_ref, g2_ref, hp_ref, ws_ref, out_ref, g1_ref, up_ref, down_ref
 ):
     rows, cols, mid = g2_ref.shape
     chunks = out_ref.shape[0]
     width = mid // chunks
-    g_in, g_out = halves(g_ref, h2i_ref)
-    expand = dot(g_in, h2i_ref[...], FIRST_DOT) + dot(g_out, h2o_ref[...], FIRST_DOT)
+    inside = (rows - 2) * cols
+    g_in, g_out = halves(g_ref, inside)
+    expand = dot(g_in, h2_ref[:inside], FIRST_DOT) + dot(g_out, h2_ref[inside:], FIRST_DOT)
     part = expand.shape[0] // chunks
     out_ref[:, :part] = expand.astype(BF16).reshape(chunks, part, mid)
-    hp_ref[0] = above_ref[...]
-    hp_ref[rows + 1] = below_ref[...]
-    hp_ref[1 : rows + 1] = h_ref[...]
     g_two = flat(g2_ref[...])
     wide = g_two.astype(F32)
     moved = [shifted(wide, 1, cols).astype(BF16), g_two, shifted(wide, -1, cols).astype(BF16)]
@@ -185,14 +195,15 @@
             start = part + (3 * a + b) * width
             grad = dot(moved[b], source, FIRST_DOT).astype(BF16)
             out_ref[:, start : start + width] = grad.reshape(chunks, width, mid)
-    inside = rows - 2
-    sums = taps([flat(g2_ref[2 - a : 2 - a + inside]) for a in range(3)], ws_ref, LAST_DOT)
+    farthest(place_ref, out_ref, up_ref, down_ref)
+    sums = taps([flat(g2_ref[2 - a : rows - a]) for a in range(3)], ws_ref, LAST_DOT)
     total = narrowed(sums, cols)
-    g1_ref[...] = jnp.where(flat(h_ref[1 : rows - 1]) > 0, total, 0.0).astype(BF16)
+    g1_ref[...] = jnp.where(flat(hp_ref[2:rows]) > 0, total, 0.0).astype(BF16)
 
 
 def backward_kernel(
-    g2_ref, above_ref, below_ref, h_ref, ws_ref, x_ref, g1i_ref, out_ref, g1o_ref
+    place_ref, g2_ref, above_ref, below_ref, hp_ref, ws_ref, x_ref, g1i_ref,
+    out_ref, g1o_ref, up_ref, down_ref,
 ):
     rows = g2_ref.shape[0]
     cols = g2_ref.shape[1]
@@ -200,22 +211,73 @@
     ends = [below_ref[...], g2_ref[rows - 1], g2_ref[rows - 2]]
     sources = [jnp.concatenate(pair, axis=0) for pair in zip(tops, ends)]
     total = narrowed(taps(sources, ws_ref, LAST_DOT), cols)
-    h_out = jnp.concatenate([h_ref[0], h_ref[rows - 1]], axis=0)
+    h_out = jnp.concatenate([hp_ref[1], hp_ref[rows]], axis=0)
     g_one = jnp.where(h_out > 0, total, 0.0).astype(BF16)
     g1o_ref[...] = g_one
     x_out = jnp.concatenate([x_ref[0], x_ref[rows - 1]], axis=0)
     grad = dot(x_out, g_one, FIRST_DOT) + dot(flat(x_ref[1 : rows - 1]), g1i_ref[...], FIRST_DOT)
     out_ref[...] = grad.astype(BF16).reshape(out_ref.shape)
+    farthest(place_ref, out_ref, up_ref, down_ref)
 
 
 def images_kernel(g_ref, g1i_ref, g1o_ref, wr_ref, out_ref):
     _, rows, cols, _ = out_ref.shape
-    g_in, g_out = halves(g_ref, g1i_ref)
+    g_in, g_out = halves(g_ref, g1i_ref.shape[0])
     inner = (g_in.astype(F32) + dot(g1i_ref[...], wr_ref[...], LAST_DOT)).astype(BF16)
     outer = (g_out.astype(F32) + dot(g1o_ref[...], wr_ref[...], LAST_DOT)).astype(BF16)
     out_ref[0, 0] = outer[:cols]
     out_ref[0, rows - 1] = outer[cols:]
     out_ref[0, 1 : rows - 1] = inner.reshape(rows - 2, cols, -1)
+
+
+def local_blocks(place_ref, offset, early_ref, late_ref):
+    depth = early_ref.shape[0] // 2
+    block = 2 * ((place_ref[0] // 2 + offset + depth) % depth)
+    pairs = []
+    for side in range(2):
+        pairs.append(
+            (early_ref[block + side].astype(F32), late_ref[block + side].astype(F32))
+        )
+    return pairs
+
+
+def join_kernel(offset, place_ref, early_ref, late_ref, eu, ed, lu, ld, up_ref, down_ref):
+    rows = early_ref.shape[1]
+    for side_got, sign, got, out_ref in ((0, 1, (eu, lu), up_ref), (1, -1, (ed, ld), down_ref)):
+        pairs = local_blocks(place_ref, sign * offset, early_ref, late_ref)
+        for side, (early, late) in enumerate(pairs):
+            if side == side_got:
+                early, late = early + got[0][...].astype(F32), late + got[1][...].astype(F32)
+            out_ref[side, :rows] = early.astype(BF16)
+            out_ref[side, rows:] = late.astype(BF16)
+
+
+def pass_kernel(offset, place_ref, early_ref, late_ref, gu_ref, gd_ref, up_ref, down_ref):
+    rows = early_ref.shape[1]
+    for sign, got_ref, out_ref in ((1, gu_ref, up_ref), (-1, gd_ref, down_ref)):
+        pairs = local_blocks(place_ref, sign * offset, early_ref, late_ref)
+        for side, (early, late) in enumerate(pairs):
+            out_ref[side, :rows] = (early + got_ref[side, :rows].astype(F32)).astype(BF16)
+            out_ref[side, rows:] = (late + got_ref[side, rows:].astype(F32)).astype(BF16)
+
+
+def close_kernel(place_ref, early_ref, late_ref, gu_ref, gd_ref, keep_ref, give_ref):
+    rows = early_ref.shape[1]
+    half = place_ref[0] % 2
+    for ref, side in ((keep_ref, half), (give_ref, 1 - half)):
+        block = 2 * (place_ref[0] // 2) + side
+        for local_ref, place in ((early_ref, slice(0, rows)), (late_ref, slice(rows, None))):
+            total = local_ref[block].astype(F32) + gu_ref[side, place].astype(F32)
+            total = total + gd_ref[side, place].astype(F32)
+            ref[place] = total.astype(ref.dtype)
+
+
+def last_kernel(keep_ref, got_ref, expand_ref, spatial_ref, reduce_ref):
+    total = keep_ref[...] + got_ref[...].astype(F32)
+    part, own = expand_ref.shape[0], reduce_ref.shape[0]
+    expand_ref[...] = total[:part]
+    spatial_ref[...] = total[part:-own].reshape(spatial_ref.shape)
+    reduce_ref[...] = total[-own:]
 
 
 def call(kernel, outs, flops, smem=0, scratch=()):
@@ -245,37 +307,29 @@
     return lax.ppermute(last, "space", up), lax.ppermute(first, "space", down)
 
 
-def scattered(local):
+def scattered(early, late, early_sends, late_sends, place):
     peers = lax.axis_size("space")
-    depth, (_, rows, mid) = peers // 2, local.shape
-    far = depth // 2
-    place = lax.axis_index("space")
-    z, half = place // 2, place % 2
+    far = peers // 4
     ring_up = [(i, (i + 2) % peers) for i in range(peers)]
     ring_down = [(i, (i - 2) % peers) for i in range(peers)]
-    pairs = local.reshape(depth, 2, rows, mid)
-
-    def mine(block):
-        return lax.dynamic_index_in_dim(pairs, block % depth, 0, keepdims=False)
-
-    start = mine(z + far)
-    up, down = start[0], start[1]
-    for step in range(1, far + 1):
-        got_up = lax.ppermute(up, "space", ring_up)
-        got_down = lax.ppermute(down, "space", ring_down)
-        got_up, got_down = lax.optimization_barrier((got_up, got_down))
-        got_up, got_down = got_up.astype(F32), got_down.astype(F32)
-        if step == 1:
-            got_up = jnp.stack([got_up, jnp.zeros_like(got_up)])
-            got_down = jnp.stack([jnp.zeros_like(got_down), got_down])
-        if step < far:
-            up = (mine(z + far - step).astype(F32) + got_up).astype(BF16)
-            down = (mine(z - far + step + depth).astype(F32) + got_down).astype(BF16)
-    total = mine(z).astype(F32) + got_up + got_down
-    keep = jnp.where(half == 0, total[0], total[1])
-    give = jnp.where(half == 0, total[1], total[0]).astype(BF16)
+    rows, mid = early.shape[1] + late.shape[1], early.shape[2]
+    pair = [((2, rows, mid), BF16)] * 2
+
+    def moved(up, down):
+        up = lax.ppermute(up, "space", ring_up)
+        down = lax.ppermute(down, "space", ring_down)
+        return up, down
+
+    got = moved(*early_sends) + moved(*late_sends)
+    for step in range(2, far + 1):
+        kernel = join_kernel if step == 2 else pass_kernel
+        kernel = functools.partial(kernel, far + 1 - step)
+        got = call(kernel, pair, rows * mid, smem=1)(place, early, late, *got)
+        got = moved(*got)
+    outs = [((rows, mid), F32), ((rows, mid), BF16)]
+    keep, give = call(close_kernel, outs, rows * mid, smem=1)(place, early, late, *got)
     swap = [(i, i ^ 1) for i in range(peers)]
-    return keep + lax.ppermute(give, "space", swap).astype(F32)
+    return keep, lax.ppermute(give, "space", swap)
 
 
 def step(images, teacher, w_reduce, w_spatial, w_expand, partners):
@@ -289,6 +343,8 @@
     elems = float(pixels * n_space * channels)
     world = n_dp * n_space
     x = images.reshape(rows, cols, channels)
+    place = lax.axis_index("space").reshape(1)
+    teacher, place = lax.optimization_barrier((teacher, place))
 
     t_all = lax.all_to_all(teacher.reshape(n_dp, chunk, channels), "dp", 0, 0, tiled=True)
     first, last = pl.pallas_call(
@@ -315,17 +371,18 @@
         ],
         26 * mac,
     )(x, w_reduce, first, last, w_spatial, w_expand)
-    h_out, s_all = call(
-        outer_kernel, [((outside, mid), BF16), ((n_dp, chunk, channels), BF16)], 26 * mac
-    )(h_one, above, below, w_spatial, w_expand, x, s_in)
+    h_pad, h_two, s_all = call(
+        outer_kernel,
+        [
+            ((rows + 2, cols, mid), BF16),
+            ((pixels, mid), BF16),
+            ((n_dp, chunk, channels), BF16),
+        ],
+        26 * mac,
+    )(h_one, h_in, above, below, w_spatial, w_expand, x, s_in)
     s_all = lax.all_to_all(s_all, "dp", 0, 0, tiled=True)
 
-    def gram(base, shape, flops):
-        kernel = functools.partial(gram_kernel, base)
-        return call(kernel, [(shape, F32)], flops, smem=1)
-
-    (message,) = gram(3, (1, 128), 16 * mac)(partners, t_all)
-    (message,) = gram(0, (world, 128), 16 * mac)(partners, message, s_all)
+    (message,) = call(gram_kernel, [((world, 128), F32)], 32 * mac, smem=1)(partners, s_all, t_all)
     message = lax.all_to_all(message, ("dp", "space"), 0, 0, tiled=True)
     grads, loss = call(
         functools.partial(grad_kernel, elems),
@@ -336,26 +393,35 @@
     grads = lax.all_to_all(grads, "dp", 0, 0, tiled=True)
     g_two, first, last = call(
         back_kernel, [((rows, cols, mid), BF16), ((cols, mid), BF16), ((cols, mid), BF16)], 16 * mac
-    )(grads, h_in, h_out, w_expand)
+    )(grads, h_two, w_expand)
     over, under = exchanged(first, last)
     part, width = channels // n_space, mid // n_space
-    early, g1_in = call(
+    early, g1_in, *early_sends = call(
         window_kernel,
-        [((n_space, part + 9 * width, mid), BF16), ((inside, mid), BF16)],
+        [((n_space, part + 9 * width, mid), BF16), ((inside, mid), BF16)]
+        + [((part + 9 * width, mid), BF16)] * 2,
         70 * mac,
-        scratch=[pltpu.VMEM((rows + 2, cols, mid), BF16)],
-    )(grads, h_in, h_out, g_two, h_one, above, below, w_spatial)
-    late, g1_out = call(
-        backward_kernel, [((n_space, part, mid), BF16), ((outside, mid), BF16)], 34 * mac
-    )(g_two, over, under, h_one, w_spatial, x, g1_in)
+        smem=1,
+    )(place, grads, h_two, g_two, h_pad, w_spatial)
+    late, g1_out, *late_sends = call(
+        backward_kernel,
+        [((n_space, part, mid), BF16), ((outside, mid), BF16)] + [((part, mid), BF16)] * 2,
+        34 * mac,
+        smem=1,
+    )(place, g_two, over, under, h_pad, w_spatial, x, g1_in)
     (g_images,) = call(
         images_kernel, [((1, rows, cols, channels), BF16)], 16 * mac
     )(grads, g1_in, g1_out, w_reduce)
-    early, late = scattered(early), scattered(late)
-    grad_expand = early[:part].T[None]
-    grad_reduce = late[None]
-    grad_spatial = early[part:].reshape(3, 3, width, mid).swapaxes(2, 3)[None]
-    return loss[0, 0], g_images, grad_reduce, grad_spatial, grad_expand
+    g_expand, g_spatial, g_reduce = call(
+        last_kernel, [((part, mid), F32), ((3, 3, width, mid), F32), ((part, mid), F32)], mac
+    )(*scattered(early, late, early_sends, late_sends, place))
+    return (
+        loss[0, 0],
+        g_images,
+        g_reduce[None],
+        g_spatial.swapaxes(2, 3)[None],
+        g_expand.T[None],
+    )
 
 
 def solution(mesh):

time: 170 us -> 150 us (0.88)
  the two profiles are of different devices: /device:TPU:4 before, /device:TPU:32 now
where the time goes in v3:
time: 150 us
  blocking collectives  64.2 us (43%)
  waiting for transfers between devices  36.5 us (24%)
  starting transfers between devices  34.3 us (23%)
  Pallas kernels  12.4 us (8%)
  local copies, waits for them, and re-layouts  1.74 us (1%)
    all_to_all x1, blocking collectives, step(): message = lax.all_to_all(message, ('dp', 'space'), 0, 0, tiled=True)  23.7 us
    all_to_all x1, blocking collectives, step(): s_all = lax.all_to_all(s_all, 'dp', 0, 0, tiled=True)  21.3 us
    all_to_all x1, blocking collectives, step(): grads = lax.all_to_all(grads, 'dp', 0, 0, tiled=True)  19.2 us
    ppermute x5, waiting for transfers between devices, moved(): up = lax.ppermute(up, 'space', ring_up)  16.8 us
    ppermute x4, starting transfers between devices, exchanged(): return (lax.ppermute(last, 'space', up), lax.ppermute(first, 'space', down))  16.6 us
    pallas_call x13, Pallas kernels, run(): pl.pallas_call(kernel, out_shape=[jax.ShapeDtypeStruct(s, d) for s, d in...  12 us
    ppermute x4, waiting for transfers between devices, exchanged(): return (lax.ppermute(last, 'space', up), lax.ppermute(first, 'space', down))  8.44 us
    ppermute x5, waiting for transfers between devices, moved(): down = lax.ppermute(down, 'space', ring_down)  6.77 us
  transfers between devices with their start and end apart: 16, of which 11 were waited for; matrix products, arithmetic and copies ran while one was open for 0% of the time, Pallas kernels for 4%

profile of v3, /device:TPU:32, one launch (start us, length us, event | category | flops | bytes accessed | tf_op | source)
XLA Modules:
  0.0 150.0 jit_solution(12147860012687087779)
XLA Ops:
  0.6 0.0 copy-start
  0.6 0.0 copy-start.2
  0.7 5.7 %all-to-all-start.1 = ((bf16[16,32,1024]{2,1,0:T(8,128)(2,1)}), bf16[16,32,1024]{2,1,0:T(8,128)(2,1)}, u32[]{:S(2)}, u32[]{:S(2)}) async-start(bf16[16,32,1024]{2,1,0:T(8,128)(2,1)} %bitcast.22), calls=%async_computation.1 | async-start | bytes 2097152 | tf_op jit(solution)/shard_map/all_to_all | solution.py:349
  6.4 0.0 copy-start.1
  6.4 0.0 copy-start.3
  6.4 0.0 copy-done
  6.4 0.0 copy-done.2
  6.4 0.3 edge.1
  6.7 4.8 %collective-permute-start = (bf16[128,256]{1,0:T(8,128)(2,1)S(1)}, bf16[128,256]{1,0:T(8,128)(2,1)S(1)}, u32[]{:S(2)}, u32[]{:S(2)}) collective-permute-start(bf16[128,256]{1,0:T(8,128)(2,1)S(1)} %get-tuple-element.40.last_ref), channel_id=1, source_target_pairs={{0,1},{1,2},{2,3},{3,4},{4,5},{5,6},{6,7},{7,8},{8,9},{9,10},{10,1... | collective-permute-start | bytes 196616 | tf_op jit(solution)/shard_map/ppermute | solution.py:307
  11.5 3.6 %collective-permute-start.1 = (bf16[128,256]{1,0:T(8,128)(2,1)S(1)}, bf16[128,256]{1,0:T(8,128)(2,1)S(1)}, u32[]{:S(2)}, u32[]{:S(2)}) collective-permute-start(bf16[128,256]{1,0:T(8,128)(2,1)S(1)} %get-tuple-element.39.first_ref), channel_id=1, source_target_pairs={{1,0},{2,1},{3,2},{4,3},{5,4},{6,5},{7,6},{8,7},{9,8},{10,9},{11,1... | collective-permute-start | bytes 196616 | tf_op jit(solution)/shard_map/ppermute | solution.py:307
  15.1 0.0 copy-done.1
  15.1 0.0 copy-done.3
  15.1 1.1 shard_map.101
  16.2 5.3 %collective-permute-done.above_ref = bf16[128,256]{1,0:T(8,128)(2,1)S(1)} collective-permute-done((bf16[128,256]{1,0:T(8,128)(2,1)S(1)}, bf16[128,256]{1,0:T(8,128)(2,1)S(1)}, u32[]{:S(2)}, u32[]{:S(2)}) %collective-permute-start) | collective-permute-done | bytes 65568 | tf_op jit(solution)/shard_map/ppermute | solution.py:307
  21.6 3.1 %collective-permute-done.1.below_ref = bf16[128,256]{1,0:T(8,128)(2,1)S(1)} collective-permute-done((bf16[128,256]{1,0:T(8,128)(2,1)S(1)}, bf16[128,256]{1,0:T(8,128)(2,1)S(1)}, u32[]{:S(2)}, u32[]{:S(2)}) %collective-permute-start.1) | collective-permute-done | bytes 65568 | tf_op jit(solution)/shard_map/ppermute | solution.py:307
  24.7 0.9 shard_map.102
  25.5 0.0 copy-start.4
  25.6 1.0 copy-done.4
  26.5 0.0 copy-start.5
  26.5 0.7 copy-done.5
  27.3 0.0 all-to-all-done.1.t_ref
  27.3 21.3 %all_to_all.26.s_ref = bf16[16,32,1024]{2,1,0:T(8,128)(2,1)S(1)} all-to-all(bf16[16,32,1024]{2,1,0:T(8,128)(2,1)} %copy-done.4), channel_id=1, replica_groups=mesh['dp'=16,'space'=16] {'dp'}, dimensions={0} | all-to-all | bytes 2097152 | tf_op jit(solution)/shard_map/all_to_all | solution.py:383
  48.6 0.0 copy-done.7
  48.6 2.7 %shard_map.103 = f32[256,128]{1,0:T(8,128)S(1)} custom-call(s32[2,16]{1,0:T(2,128)S(1)} %copy-done.7, bf16[16,32,1024]{2,1,0:T(8,128)(2,1)S(1)} %all_to_all.26.s_ref, bf16[16,32,1024]{2,1,0:T(8,128)(2,1)} %all-to-all-done.1.t_ref), custom_call_target="tpu_custom_call" | custom-call | flops 536870912 | bytes 2097280 | tf_op jit(solution)/shard_map/pallas_call | solution.py:290
  51.3 23.7 %all_to_all.27 = f32[256,1,128]{2,1,0:T(1,128)S(1)} all-to-all(f32[256,1,128]{2,1,0:T(1,128)S(1)} %bitcast.20), channel_id=1, replica_groups=mesh['dp'=16,'space'=16] {'dp','space'}, dimensions={0} | all-to-all | bytes 262144 | tf_op jit(solution)/shard_map/all_to_all | solution.py:386
  75.0 1.8 %shard_map.104 = (bf16[16,32,1024]{2,1,0:T(8,128)(2,1)S(1)}, f32[1,1]{1,0:T(1,128)}) custom-call(s32[2,16]{1,0:T(2,128)S(1)} %copy-done.7, f32[256,128]{1,0:T(8,128)S(1)} %bitcast.21, bf16[16,32,1024]{2,1,0:T(8,128)(2,1)S(1)} %all_to_all.26.s_ref), custom_call_target="tpu_custom_call" | custom-call | flops 16777216 | bytes 1179776 | tf_op jit(solution)/shard_map/pallas_call | solution.py:290
  76.7 0.0 copy-start.6
  76.8 19.2 %all_to_all.28.g_ref = bf16[16,32,1024]{2,1,0:T(8,128)(2,1)S(1)} all-to-all(bf16[16,32,1024]{2,1,0:T(8,128)(2,1)S(1)} %get-tuple-element.47), channel_id=1, replica_groups=mesh['dp'=16,'space'=16] {'dp'}, dimensions={0} | all-to-all | bytes 2097152 | tf_op jit(solution)/shard_map/all_to_all | solution.py:393
  96.0 0.5 shard_map.105
  96.5 3.0 %collective-permute-start.2 = (bf16[128,256]{1,0:T(8,128)(2,1)S(1)}, bf16[128,256]{1,0:T(8,128)(2,1)S(1)}, u32[]{:S(2)}, u32[]{:S(2)}) collective-permute-start(bf16[128,256]{1,0:T(8,128)(2,1)S(1)} %get-tuple-element.53), channel_id=1, source_target_pairs={{0,1},{1,2},{2,3},{3,4},{4,5},{5,6},{6,7},{7,8},{8,9},{9,10},{10,1... | collective-permute-start | bytes 196616 | tf_op jit(solution)/shard_map/ppermute | solution.py:307
  99.5 5.2 %collective-permute-start.3 = (bf16[128,256]{1,0:T(8,128)(2,1)S(1)}, bf16[128,256]{1,0:T(8,128)(2,1)S(1)}, u32[]{:S(2)}, u32[]{:S(2)}) collective-permute-start(bf16[128,256]{1,0:T(8,128)(2,1)S(1)} %get-tuple-element.54), channel_id=1, source_target_pairs={{1,0},{2,1},{3,2},{4,3},{5,4},{6,5},{7,6},{8,7},{9,8},{10,9},{11,1... | collective-permute-start | bytes 196616 | tf_op jit(solution)/shard_map/ppermute | solution.py:307
  104.7 0.0 copy-done.6
  104.7 1.4 shard_map.106
  106.2 0.5 collective-permute-start.4
  106.6 1.6 %collective-permute-start.5 = (bf16[208,256]{1,0:T(8,128)(2,1)S(1)}, bf16[208,256]{1,0:T(8,128)(2,1)S(1)}, u32[]{:S(2)}, u32[]{:S(2)}) collective-permute-start(bf16[208,256]{1,0:T(8,128)(2,1)S(1)} %get-tuple-element.59), channel_id=1, source_target_pairs={{0,14},{1,15},{2,0},{3,1},{4,2},{5,3},{6,4},{7,5},{8,6},{9,7},{10,... | collective-permute-start | bytes 319496 | tf_op jit(solution)/shard_map/ppermute | solution.py:320
  108.3 0.0 collective-permute-done.2.above_ref
  108.3 0.0 collective-permute-done.3.below_ref
  108.3 1.1 shard_map.107
  109.4 0.5 collective-permute-start.6
  109.8 1.6 %collective-permute-start.7 = (bf16[64,256]{1,0:T(8,128)(2,1)S(1)}, bf16[64,256]{1,0:T(8,128)(2,1)S(1)}, u32[]{:S(2)}, u32[]{:S(2)}) collective-permute-start(bf16[64,256]{1,0:T(8,128)(2,1)S(1)} %get-tuple-element.61), channel_id=1, source_target_pairs={{0,14},{1,15},{2,0},{3,1},{4,2},{5,3},{6,4},{7,5},{8,6},{9,7},{10,... | collective-permute-start | bytes 98312 | tf_op jit(solution)/shard_map/ppermute | solution.py:320
  111.5 1.9 %collective-permute-done.6.lu = bf16[64,256]{1,0:T(8,128)(2,1)S(1)} collective-permute-done((bf16[64,256]{1,0:T(8,128)(2,1)S(1)}, bf16[64,256]{1,0:T(8,128)(2,1)S(1)}, u32[]{:S(2)}, u32[]{:S(2)}) %collective-permute-start.6) | collective-permute-done | bytes 32800 | tf_op jit(solution)/shard_map/ppermute | solution.py:319
  113.4 0.4 collective-permute-done.7.ld
  113.7 0.0 collective-permute-done.4.eu
  113.7 0.0 collective-permute-done.5.ed
  113.7 0.1 shard_map.109
  113.8 1.9 %collective-permute-start.8 = (bf16[2,272,256]{2,1,0:T(8,128)(2,1)S(1)}, bf16[2,272,256]{2,1,0:T(8,128)(2,1)S(1)}, u32[]{:S(2)}, u32[]{:S(2)}) collective-permute-start(bf16[2,272,256]{2,1,0:T(8,128)(2,1)S(1)} %get-tuple-element.62), channel_id=1, source_target_pairs={{0,2},{1,3},{2,4},{3,5},{4,6},{5,7},{6,8},{7,9},{8,10},{9,11},{10,... | collective-permute-start | bytes 835592 | tf_op jit(solution)/shard_map/ppermute | solution.py:319
  115.8 0.3 collective-permute-start.9
  116.1 4.5 %collective-permute-done.8.gu_ref = bf16[2,272,256]{2,1,0:T(8,128)(2,1)S(1)} collective-permute-done((bf16[2,272,256]{2,1,0:T(8,128)(2,1)S(1)}, bf16[2,272,256]{2,1,0:T(8,128)(2,1)S(1)}, u32[]{:S(2)}, u32[]{:S(2)}) %collective-permute-start.8) | collective-permute-done | bytes 278560 | tf_op jit(solution)/shard_map/ppermute | solution.py:319
  120.6 2.9 %collective-permute-done.9.gd_ref = bf16[2,272,256]{2,1,0:T(8,128)(2,1)S(1)} collective-permute-done((bf16[2,272,256]{2,1,0:T(8,128)(2,1)S(1)}, bf16[2,272,256]{2,1,0:T(8,128)(2,1)S(1)}, u32[]{:S(2)}, u32[]{:S(2)}) %collective-permute-start.9) | collective-permute-done | bytes 278560 | tf_op jit(solution)/shard_map/ppermute | solution.py:320
  123.5 0.1 shard_map.110
  123.7 2.7 %collective-permute-start.10 = (bf16[2,272,256]{2,1,0:T(8,128)(2,1)S(1)}, bf16[2,272,256]{2,1,0:T(8,128)(2,1)S(1)}, u32[]{:S(2)}, u32[]{:S(2)}) collective-permute-start(bf16[2,272,256]{2,1,0:T(8,128)(2,1)S(1)} %get-tuple-element.64), channel_id=1, source_target_pairs={{0,2},{1,3},{2,4},{3,5},{4,6},{5,7},{6,8},{7,9},{8,10},{9,11},{10,... | collective-permute-start | bytes 835592 | tf_op jit(solution)/shard_map/ppermute | solution.py:319
  126.4 0.0 collective-permute-start.11
  126.4 5.8 %collective-permute-done.10.gu_ref = bf16[2,272,256]{2,1,0:T(8,128)(2,1)S(1)} collective-permute-done((bf16[2,272,256]{2,1,0:T(8,128)(2,1)S(1)}, bf16[2,272,256]{2,1,0:T(8,128)(2,1)S(1)}, u32[]{:S(2)}, u32[]{:S(2)}) %collective-permute-start.10) | collective-permute-done | bytes 278560 | tf_op jit(solution)/shard_map/ppermute | solution.py:319
  132.2 2.8 %collective-permute-done.11.gd_ref = bf16[2,272,256]{2,1,0:T(8,128)(2,1)S(1)} collective-permute-done((bf16[2,272,256]{2,1,0:T(8,128)(2,1)S(1)}, bf16[2,272,256]{2,1,0:T(8,128)(2,1)S(1)}, u32[]{:S(2)}, u32[]{:S(2)}) %collective-permute-start.11) | collective-permute-done | bytes 278560 | tf_op jit(solution)/shard_map/ppermute | solution.py:320
  135.0 0.1 shard_map.111
  135.1 0.8 collective-permute-start.12
  135.9 1.3 collective-permute-start.13
  137.2 4.5 %collective-permute-done.12.gu_ref = bf16[2,272,256]{2,1,0:T(8,128)(2,1)S(1)} collective-permute-done((bf16[2,272,256]{2,1,0:T(8,128)(2,1)S(1)}, bf16[2,272,256]{2,1,0:T(8,128)(2,1)S(1)}, u32[]{:S(2)}, u32[]{:S(2)}) %collective-permute-start.12) | collective-permute-done | bytes 278560 | tf_op jit(solution)/shard_map/ppermute | solution.py:319
  141.8 0.7 collective-permute-done.13.gd_ref
  142.5 0.1 shard_map.112
  142.6 0.7 collective-permute-start.14
  143.2 1.4 shard_map.108
  144.7 4.5 %collective-permute-done.14.got_ref = bf16[272,256]{1,0:T(8,128)(2,1)S(1)} collective-permute-done((bf16[272,256]{1,0:T(8,128)(2,1)S(1)}, bf16[272,256]{1,0:T(8,128)(2,1)S(1)}, u32[]{:S(2)}, u32[]{:S(2)}) %collective-permute-start.14) | collective-permute-done | bytes 139296 | tf_op jit(solution)/shard_map/ppermute | solution.py:332
  149.2 0.7 shard_map.113
  (1 shorter events, 0.0 us)
Async XLA Ops:
  0.6 5.8 %copy-start = (bf16[1,4,128,1024]{3,2,1,0:T(8,128)(2,1)S(1)}, bf16[1,4,128,1024]{3,2,1,0:T(8,128)(2,1)}, u32[]{:S(2)}) copy-start(bf16[1,4,128,1024]{3,2,1,0:T(8,128)(2,1)} %param.6) | copy-start | bytes 3145732
  0.6 5.8 %copy-start.2 = (bf16[1024,256]{1,0:T(8,128)(2,1)S(1)}, bf16[1024,256]{1,0:T(8,128)(2,1)}, u32[]{:S(2)}) copy-start(bf16[1024,256]{1,0:T(8,128)(2,1)} %wr_ref.3) | copy-start | bytes 1572868
  0.7 26.6 %all-to-all-start.1 = ((bf16[16,32,1024]{2,1,0:T(8,128)(2,1)}), bf16[16,32,1024]{2,1,0:T(8,128)(2,1)}, u32[]{:S(2)}, u32[]{:S(2)}) async-start(bf16[16,32,1024]{2,1,0:T(8,128)(2,1)} %bitcast.22), calls=%async_computation.1 | async-start | bytes 2097152 | tf_op jit(solution)/shard_map/all_to_all | solution.py:349
  6.4 8.8 %copy-start.1 = (bf16[3,3,256,256]{3,2,1,0:T(8,128)(2,1)S(1)}, bf16[3,3,256,256]{3,2,1,0:T(8,128)(2,1)}, u32[]{:S(2)}) copy-start(bf16[3,3,256,256]{3,2,1,0:T(8,128)(2,1)} %ws_ref.7) | copy-start | bytes 3538948
  6.4 8.8 %copy-start.3 = (bf16[256,1024]{1,0:T(8,128)(2,1)S(1)}, bf16[256,1024]{1,0:T(8,128)(2,1)}, u32[]{:S(2)}) copy-start(bf16[256,1024]{1,0:T(8,128)(2,1)} %we_ref.5) | copy-start | bytes 1572868
  6.7 14.8 %collective-permute-start = (bf16[128,256]{1,0:T(8,128)(2,1)S(1)}, bf16[128,256]{1,0:T(8,128)(2,1)S(1)}, u32[]{:S(2)}, u32[]{:S(2)}) collective-permute-start(bf16[128,256]{1,0:T(8,128)(2,1)S(1)} %get-tuple-element.40.last_ref), channel_id=1, source_target_pairs={{0,1},{1,2},{2,3},{3,4},{4,5},{5,6},{6,7},{7,8},{8,9},{9,10},{10,1... | collective-permute-start | bytes 196616 | tf_op jit(solution)/shard_map/ppermute | solution.py:307
  11.5 13.2 %collective-permute-start.1 = (bf16[128,256]{1,0:T(8,128)(2,1)S(1)}, bf16[128,256]{1,0:T(8,128)(2,1)S(1)}, u32[]{:S(2)}, u32[]{:S(2)}) collective-permute-start(bf16[128,256]{1,0:T(8,128)(2,1)S(1)} %get-tuple-element.39.first_ref), channel_id=1, source_target_pairs={{1,0},{2,1},{3,2},{4,3},{5,4},{6,5},{7,6},{8,7},{9,8},{10,9},{11,1... | collective-permute-start | bytes 196616 | tf_op jit(solution)/shard_map/ppermute | solution.py:307
  25.5 1.0 copy-start.4
  26.5 0.7 copy-start.5
  27.3 21.3 %copy-start.7 = (s32[2,16]{1,0:T(2,128)S(1)}, s32[2,16]{1,0:T(2,128)}, u32[]{:S(2)}) copy-start(s32[2,16]{1,0:T(2,128)} %parts_ref.3) | copy-start | bytes 388
  76.7 28.0 %copy-start.6 = (bf16[6,128,256]{2,1,0:T(8,128)(2,1)S(1)}, bf16[6,128,256]{2,1,0:T(8,128)(2,1)}, u32[]{:S(2)}) copy-start(bf16[6,128,256]{2,1,0:T(8,128)(2,1)} %copy-done.5) | copy-start | bytes 1179652
  96.5 11.8 %collective-permute-start.2 = (bf16[128,256]{1,0:T(8,128)(2,1)S(1)}, bf16[128,256]{1,0:T(8,128)(2,1)S(1)}, u32[]{:S(2)}, u32[]{:S(2)}) collective-permute-start(bf16[128,256]{1,0:T(8,128)(2,1)S(1)} %get-tuple-element.53), channel_id=1, source_target_pairs={{0,1},{1,2},{2,3},{3,4},{4,5},{5,6},{6,7},{7,8},{8,9},{9,10},{10,1... | collective-permute-start | bytes 196616 | tf_op jit(solution)/shard_map/ppermute | solution.py:307
  99.5 8.8 %collective-permute-start.3 = (bf16[128,256]{1,0:T(8,128)(2,1)S(1)}, bf16[128,256]{1,0:T(8,128)(2,1)S(1)}, u32[]{:S(2)}, u32[]{:S(2)}) collective-permute-start(bf16[128,256]{1,0:T(8,128)(2,1)S(1)} %get-tuple-element.54), channel_id=1, source_target_pairs={{1,0},{2,1},{3,2},{4,3},{5,4},{6,5},{7,6},{8,7},{9,8},{10,9},{11,1... | collective-permute-start | bytes 196616 | tf_op jit(solution)/shard_map/ppermute | solution.py:307
  106.2 7.6 %collective-permute-start.4 = (bf16[208,256]{1,0:T(8,128)(2,1)S(1)}, bf16[208,256]{1,0:T(8,128)(2,1)S(1)}, u32[]{:S(2)}, u32[]{:S(2)}) collective-permute-start(bf16[208,256]{1,0:T(8,128)(2,1)S(1)} %get-tuple-element.58), channel_id=1, source_target_pairs={{0,2},{1,3},{2,4},{3,5},{4,6},{5,7},{6,8},{7,9},{8,10},{9,11},{10,... | collective-permute-start | bytes 319496 | tf_op jit(solution)/shard_map/ppermute | solution.py:319
  106.6 7.1 %collective-permute-start.5 = (bf16[208,256]{1,0:T(8,128)(2,1)S(1)}, bf16[208,256]{1,0:T(8,128)(2,1)S(1)}, u32[]{:S(2)}, u32[]{:S(2)}) collective-permute-start(bf16[208,256]{1,0:T(8,128)(2,1)S(1)} %get-tuple-element.59), channel_id=1, source_target_pairs={{0,14},{1,15},{2,0},{3,1},{4,2},{5,3},{6,4},{7,5},{8,6},{9,7},{10,... | collective-permute-start | bytes 319496 | tf_op jit(solution)/shard_map/ppermute | solution.py:320
  109.4 4.0 %collective-permute-start.6 = (bf16[64,256]{1,0:T(8,128)(2,1)S(1)}, bf16[64,256]{1,0:T(8,128)(2,1)S(1)}, u32[]{:S(2)}, u32[]{:S(2)}) collective-permute-start(bf16[64,256]{1,0:T(8,128)(2,1)S(1)} %get-tuple-element.60), channel_id=1, source_target_pairs={{0,2},{1,3},{2,4},{3,5},{4,6},{5,7},{6,8},{7,9},{8,10},{9,11},{10,... | collective-permute-start | bytes 98312 | tf_op jit(solution)/shard_map/ppermute | solution.py:319
  109.8 3.9 %collective-permute-start.7 = (bf16[64,256]{1,0:T(8,128)(2,1)S(1)}, bf16[64,256]{1,0:T(8,128)(2,1)S(1)}, u32[]{:S(2)}, u32[]{:S(2)}) collective-permute-start(bf16[64,256]{1,0:T(8,128)(2,1)S(1)} %get-tuple-element.61), channel_id=1, source_target_pairs={{0,14},{1,15},{2,0},{3,1},{4,2},{5,3},{6,4},{7,5},{8,6},{9,7},{10,... | collective-permute-start | bytes 98312 | tf_op jit(solution)/shard_map/ppermute | solution.py:320
  113.8 6.8 %collective-permute-start.8 = (bf16[2,272,256]{2,1,0:T(8,128)(2,1)S(1)}, bf16[2,272,256]{2,1,0:T(8,128)(2,1)S(1)}, u32[]{:S(2)}, u32[]{:S(2)}) collective-permute-start(bf16[2,272,256]{2,1,0:T(8,128)(2,1)S(1)} %get-tuple-element.62), channel_id=1, source_target_pairs={{0,2},{1,3},{2,4},{3,5},{4,6},{5,7},{6,8},{7,9},{8,10},{9,11},{10,... | collective-permute-start | bytes 835592 | tf_op jit(solution)/shard_map/ppermute | solution.py:319
  115.8 7.8 %collective-permute-start.9 = (bf16[2,272,256]{2,1,0:T(8,128)(2,1)S(1)}, bf16[2,272,256]{2,1,0:T(8,128)(2,1)S(1)}, u32[]{:S(2)}, u32[]{:S(2)}) collective-permute-start(bf16[2,272,256]{2,1,0:T(8,128)(2,1)S(1)} %get-tuple-element.63), channel_id=1, source_target_pairs={{0,14},{1,15},{2,0},{3,1},{4,2},{5,3},{6,4},{7,5},{8,6},{9,7},{10,... | collective-permute-start | bytes 835592 | tf_op jit(solution)/shard_map/ppermute | solution.py:320
  123.7 8.6 %collective-permute-start.10 = (bf16[2,272,256]{2,1,0:T(8,128)(2,1)S(1)}, bf16[2,272,256]{2,1,0:T(8,128)(2,1)S(1)}, u32[]{:S(2)}, u32[]{:S(2)}) collective-permute-start(bf16[2,272,256]{2,1,0:T(8,128)(2,1)S(1)} %get-tuple-element.64), channel_id=1, source_target_pairs={{0,2},{1,3},{2,4},{3,5},{4,6},{5,7},{6,8},{7,9},{8,10},{9,11},{10,... | collective-permute-start | bytes 835592 | tf_op jit(solution)/shard_map/ppermute | solution.py:319
  126.4 8.6 %collective-permute-start.11 = (bf16[2,272,256]{2,1,0:T(8,128)(2,1)S(1)}, bf16[2,272,256]{2,1,0:T(8,128)(2,1)S(1)}, u32[]{:S(2)}, u32[]{:S(2)}) collective-permute-start(bf16[2,272,256]{2,1,0:T(8,128)(2,1)S(1)} %get-tuple-element.65), channel_id=1, source_target_pairs={{0,14},{1,15},{2,0},{3,1},{4,2},{5,3},{6,4},{7,5},{8,6},{9,7},{10,... | collective-permute-start | bytes 835592 | tf_op jit(solution)/shard_map/ppermute | solution.py:320
  135.1 6.6 %collective-permute-start.12 = (bf16[2,272,256]{2,1,0:T(8,128)(2,1)S(1)}, bf16[2,272,256]{2,1,0:T(8,128)(2,1)S(1)}, u32[]{:S(2)}, u32[]{:S(2)}) collective-permute-start(bf16[2,272,256]{2,1,0:T(8,128)(2,1)S(1)} %get-tuple-element.66), channel_id=1, source_target_pairs={{0,2},{1,3},{2,4},{3,5},{4,6},{5,7},{6,8},{7,9},{8,10},{9,11},{10,... | collective-permute-start | bytes 835592 | tf_op jit(solution)/shard_map/ppermute | solution.py:319
  135.9 6.5 %collective-permute-start.13 = (bf16[2,272,256]{2,1,0:T(8,128)(2,1)S(1)}, bf16[2,272,256]{2,1,0:T(8,128)(2,1)S(1)}, u32[]{:S(2)}, u32[]{:S(2)}) collective-permute-start(bf16[2,272,256]{2,1,0:T(8,128)(2,1)S(1)} %get-tuple-element.67), channel_id=1, source_target_pairs={{0,14},{1,15},{2,0},{3,1},{4,2},{5,3},{6,4},{7,5},{8,6},{9,7},{10,... | collective-permute-start | bytes 835592 | tf_op jit(solution)/shard_map/ppermute | solution.py:320
  142.6 6.6 %collective-permute-start.14 = (bf16[272,256]{1,0:T(8,128)(2,1)S(1)}, bf16[272,256]{1,0:T(8,128)(2,1)S(1)}, u32[]{:S(2)}, u32[]{:S(2)}) collective-permute-start(bf16[272,256]{1,0:T(8,128)(2,1)S(1)} %get-tuple-element.69), channel_id=1, source_target_pairs={{0,1},{1,0},{2,3},{3,2},{4,5},{5,4},{6,7},{7,6},{8,9},{9,8},{10,11... | collective-permute-start | bytes 417800 | tf_op jit(solution)/shard_map/ppermute | solution.py:332

commit v4 on v3

--- a/solution.py
+++ b/solution.py
@@ -93,19 +93,23 @@
 
 def gram_kernel(parts_ref, s_ref, t_ref, out_ref):
     images, chunk, _ = s_ref.shape
-    count = images * chunk
+    group = 16 if chunk % 16 == 0 else chunk
+    count = images * group
     row = lax.broadcasted_iota(jnp.int32, (count, count), 0)
     col = lax.broadcasted_iota(jnp.int32, (count, count), 1)
-    same = (row % chunk) == (col % chunk)
+    same = (row % group) == (col % group)
     image = lax.broadcasted_iota(jnp.int32, (images, count), 0)
-    other = lax.broadcasted_iota(jnp.int32, (images, count), 1) // chunk
+    other = lax.broadcasted_iota(jnp.int32, (images, count), 1) // group
     slot_row = lax.broadcasted_iota(jnp.int32, (images, 128), 0)
     slot = lax.broadcasted_iota(jnp.int32, (images, 128), 1)
     message = jnp.zeros((images, 128), F32)
     for base, value_ref in ((0, s_ref), (3, t_ref)):
-        value = flat(value_ref[...])
-        gram = jnp.where(same, dot(value, value, LAST_DOT), 0.0)
-        gram = gram.reshape(images, chunk, count).sum(axis=1)
+        gram = None
+        for start in range(0, chunk, group):
+            value = flat(value_ref[:, start : start + group])
+            part = dot(value, value, LAST_DOT)
+            gram = part if gram is None else gram + part
+        gram = jnp.where(same, gram, 0.0).reshape(images, group, count).sum(axis=1)
         for k in range(3):
             partner = image if k == 0 else image ^ parts_ref[k - 1, 0]
             column = jnp.where(other == partner, gram, 0.0).sum(axis=1, keepdims=True)
@@ -230,54 +234,47 @@
     out_ref[0, 1 : rows - 1] = inner.reshape(rows - 2, cols, -1)
 
 
-def local_blocks(place_ref, offset, early_ref, late_ref):
+def add_kernel(offset, first, last, place_ref, early_ref, late_ref, *refs):
+    rows = early_ref.shape[1]
     depth = early_ref.shape[0] // 2
-    block = 2 * ((place_ref[0] // 2 + offset + depth) % depth)
-    pairs = []
-    for side in range(2):
-        pairs.append(
-            (early_ref[block + side].astype(F32), late_ref[block + side].astype(F32))
-        )
-    return pairs
-
-
-def join_kernel(offset, place_ref, early_ref, late_ref, eu, ed, lu, ld, up_ref, down_ref):
+    z, half = place_ref[0] // 2, place_ref[0] % 2
+    outs = list(refs[4:] if first else refs[2:])
+    if first:
+        give_ref = outs.pop()
+        block = 2 * z + 1 - half
+        give_ref[:rows] = early_ref[block]
+        give_ref[rows:] = late_ref[block]
+    for way, sign in enumerate((1, -1)):
+        block = 2 * ((z + sign * offset + depth) % depth)
+        for index, side in enumerate((half, 1 - half) if last else (0, 1)):
+            early = early_ref[block + side].astype(F32)
+            late = late_ref[block + side].astype(F32)
+            if first:
+                here = jnp.where(side == way, 1.0, 0.0).astype(F32)
+                early = early + here * refs[way][...].astype(F32)
+                late = late + here * refs[2 + way][...].astype(F32)
+            else:
+                early = early + refs[way][side, :rows].astype(F32)
+                late = late + refs[way][side, rows:].astype(F32)
+            target = outs[2 * way + index] if last else outs[way].at[side]
+            target[:rows] = early.astype(BF16)
+            target[rows:] = late.astype(BF16)
+
+
+def last_kernel(
+    place_ref, early_ref, late_ref, own_ref, us, uc, ds, dc, expand_ref, spatial_ref, reduce_ref
+):
     rows = early_ref.shape[1]
-    for side_got, sign, got, out_ref in ((0, 1, (eu, lu), up_ref), (1, -1, (ed, ld), down_ref)):
-        pairs = local_blocks(place_ref, sign * offset, early_ref, late_ref)
-        for side, (early, late) in enumerate(pairs):
-            if side == side_got:
-                early, late = early + got[0][...].astype(F32), late + got[1][...].astype(F32)
-            out_ref[side, :rows] = early.astype(BF16)
-            out_ref[side, rows:] = late.astype(BF16)
-
-
-def pass_kernel(offset, place_ref, early_ref, late_ref, gu_ref, gd_ref, up_ref, down_ref):
-    rows = early_ref.shape[1]
-    for sign, got_ref, out_ref in ((1, gu_ref, up_ref), (-1, gd_ref, down_ref)):
-        pairs = local_blocks(place_ref, sign * offset, early_ref, late_ref)
-        for side, (early, late) in enumerate(pairs):
-            out_ref[side, :rows] = (early + got_ref[side, :rows].astype(F32)).astype(BF16)
-            out_ref[side, rows:] = (late + got_ref[side, rows:].astype(F32)).astype(BF16)
-
-
-def close_kernel(place_ref, early_ref, late_ref, gu_ref, gd_ref, keep_ref, give_ref):
-    rows = early_ref.shape[1]
-    half = place_ref[0] % 2
-    for ref, side in ((keep_ref, half), (give_ref, 1 - half)):
-        block = 2 * (place_ref[0] // 2) + side
-        for local_ref, place in ((early_ref, slice(0, rows)), (late_ref, slice(rows, None))):
-            total = local_ref[block].astype(F32) + gu_ref[side, place].astype(F32)
-            total = total + gd_ref[side, place].astype(F32)
-            ref[place] = total.astype(ref.dtype)
-
-
-def last_kernel(keep_ref, got_ref, expand_ref, spatial_ref, reduce_ref):
-    total = keep_ref[...] + got_ref[...].astype(F32)
-    part, own = expand_ref.shape[0], reduce_ref.shape[0]
-    expand_ref[...] = total[:part]
-    spatial_ref[...] = total[part:-own].reshape(spatial_ref.shape)
-    reduce_ref[...] = total[-own:]
+    block = place_ref[0]
+    early = early_ref[block].astype(F32)
+    late = late_ref[block].astype(F32)
+    for ref in (own_ref, us, uc, ds, dc):
+        early = early + ref[:rows].astype(F32)
+        late = late + ref[rows:].astype(F32)
+    part = expand_ref.shape[0]
+    expand_ref[...] = early[:part]
+    spatial_ref[...] = early[part:].reshape(spatial_ref.shape)
+    reduce_ref[...] = late
 
 
 def call(kernel, outs, flops, smem=0, scratch=()):
@@ -310,26 +307,34 @@
 def scattered(early, late, early_sends, late_sends, place):
     peers = lax.axis_size("space")
     far = peers // 4
-    ring_up = [(i, (i + 2) % peers) for i in range(peers)]
-    ring_down = [(i, (i - 2) % peers) for i in range(peers)]
+    ups = [(i, (i + 2) % peers) for i in range(peers)]
+    downs = [(i, (i - 2) % peers) for i in range(peers)]
     rows, mid = early.shape[1] + late.shape[1], early.shape[2]
-    pair = [((2, rows, mid), BF16)] * 2
 
     def moved(up, down):
-        up = lax.ppermute(up, "space", ring_up)
-        down = lax.ppermute(down, "space", ring_down)
+        up = lax.ppermute(up, "space", ups)
+        down = lax.ppermute(down, "space", downs)
         return up, down
 
     got = moved(*early_sends) + moved(*late_sends)
     for step in range(2, far + 1):
-        kernel = join_kernel if step == 2 else pass_kernel
-        kernel = functools.partial(kernel, far + 1 - step)
-        got = call(kernel, pair, rows * mid, smem=1)(place, early, late, *got)
-        got = moved(*got)
-    outs = [((rows, mid), F32), ((rows, mid), BF16)]
-    keep, give = call(close_kernel, outs, rows * mid, smem=1)(place, early, late, *got)
-    swap = [(i, i ^ 1) for i in range(peers)]
-    return keep, lax.ppermute(give, "space", swap)
+        first, last = step == 2, step == far
+        kernel = functools.partial(add_kernel, far + 1 - step, first, last)
+        half = ((rows, mid), BF16)
+        outs = [half] * 4 if last else [((2, rows, mid), BF16)] * 2
+        outs = outs + [half] * first
+        got = list(call(kernel, outs, rows * mid, smem=1)(place, early, late, *got))
+        if first:
+            own = lax.ppermute(got.pop(), "space", [(i, i ^ 1) for i in range(peers)])
+        if not last:
+            got = moved(*got)
+    cross_ups = [(i, j ^ 1) for i, j in ups]
+    cross_downs = [(i, j ^ 1) for i, j in downs]
+    sends = ((1, cross_ups), (3, cross_downs), (0, ups), (2, downs))
+    ended = []
+    for index, path in sends:
+        ended.append(lax.ppermute(got[index], "space", path))
+    return own, *ended
 
 
 def step(images, teacher, w_reduce, w_spatial, w_expand, partners):
@@ -413,8 +418,11 @@
         images_kernel, [((1, rows, cols, channels), BF16)], 16 * mac
     )(grads, g1_in, g1_out, w_reduce)
     g_expand, g_spatial, g_reduce = call(
-        last_kernel, [((part, mid), F32), ((3, 3, width, mid), F32), ((part, mid), F32)], mac
-    )(*scattered(early, late, early_sends, late_sends, place))
+        last_kernel,
+        [((part, mid), F32), ((3, 3, width, mid), F32), ((part, mid), F32)],
+        mac,
+        smem=1,
+    )(place, early, late, *scattered(early, late, early_sends, late_sends, place))
     return (
         loss[0, 0],
         g_images,

time: 150 us -> 150 us (level)
  the two profiles are of different devices: /device:TPU:32 before, /device:TPU:4 now
where the time goes in v4:
time: 150 us; the launch traced here: 149 us
  blocking collectives  65.3 us (44%)
  starting transfers between devices  42.6 us (28%)
  waiting for transfers between devices  27.1 us (18%)
  Pallas kernels  11.8 us (8%)
  local copies, waits for them, and re-layouts  1.74 us (1%)
    all_to_all x1, blocking collectives, step(): message = lax.all_to_all(message, ('dp', 'space'), 0, 0, tiled=True)  23.1 us
    all_to_all x1, blocking collectives, step(): s_all = lax.all_to_all(s_all, 'dp', 0, 0, tiled=True)  22.6 us
    all_to_all x1, blocking collectives, step(): grads = lax.all_to_all(grads, 'dp', 0, 0, tiled=True)  19.5 us
    ppermute x4, starting transfers between devices, exchanged(): return (lax.ppermute(last, 'space', up), lax.ppermute(first, 'space', down))  14.8 us
    ppermute x4, waiting for transfers between devices, moved(): up = lax.ppermute(up, 'space', ups)  12.6 us
    ppermute x4, starting transfers between devices, moved(): down = lax.ppermute(down, 'space', downs)  12 us
    pallas_call x12, Pallas kernels, run(): pl.pallas_call(kernel, out_shape=[jax.ShapeDtypeStruct(s, d) for s, d in...  11.5 us
    ppermute x4, starting transfers between devices, scattered(): ended.append(lax.ppermute(got[index], 'space', path))  8.95 us
  transfers between devices with their start and end apart: 18, of which 7 were waited for; matrix products, arithmetic and copies ran while one was open for 0% of the time, Pallas kernels for 4%

profile of v4, /device:TPU:4, one launch (start us, length us, event | category | flops | bytes accessed | tf_op | source)
XLA Modules:
  0.0 149.3 jit_solution(7836265554638211424)
XLA Ops:
  0.6 0.0 copy-start
  0.6 0.0 copy-start.2
  0.7 5.4 %all-to-all-start.1 = ((bf16[16,32,1024]{2,1,0:T(8,128)(2,1)}), bf16[16,32,1024]{2,1,0:T(8,128)(2,1)}, u32[]{:S(2)}, u32[]{:S(2)}) async-start(bf16[16,32,1024]{2,1,0:T(8,128)(2,1)} %bitcast.22), calls=%async_computation.1 | async-start | bytes 2097152 | tf_op jit(solution)/shard_map/all_to_all | solution.py:354
  6.1 0.0 copy-start.1
  6.1 0.0 copy-start.3
  6.1 0.0 copy-done
  6.1 0.0 copy-done.2
  6.1 0.3 edge.1
  6.4 4.2 %collective-permute-start = (bf16[128,256]{1,0:T(8,128)(2,1)S(1)}, bf16[128,256]{1,0:T(8,128)(2,1)S(1)}, u32[]{:S(2)}, u32[]{:S(2)}) collective-permute-start(bf16[128,256]{1,0:T(8,128)(2,1)S(1)} %get-tuple-element.41.last_ref), channel_id=1, source_target_pairs={{0,1},{1,2},{2,3},{3,4},{4,5},{5,6},{6,7},{7,8},{8,9},{9,10},{10,1... | collective-permute-start | bytes 196616 | tf_op jit(solution)/shard_map/ppermute | solution.py:304
  10.6 3.3 %collective-permute-start.1 = (bf16[128,256]{1,0:T(8,128)(2,1)S(1)}, bf16[128,256]{1,0:T(8,128)(2,1)S(1)}, u32[]{:S(2)}, u32[]{:S(2)}) collective-permute-start(bf16[128,256]{1,0:T(8,128)(2,1)S(1)} %get-tuple-element.40.first_ref), channel_id=1, source_target_pairs={{1,0},{2,1},{3,2},{4,3},{5,4},{6,5},{7,6},{8,7},{9,8},{10,9},{11,1... | collective-permute-start | bytes 196616 | tf_op jit(solution)/shard_map/ppermute | solution.py:304
  13.9 0.0 copy-done.1
  13.9 0.0 copy-done.3
  13.9 1.1 shard_map.101
  15.0 7.7 %collective-permute-done.above_ref = bf16[128,256]{1,0:T(8,128)(2,1)S(1)} collective-permute-done((bf16[128,256]{1,0:T(8,128)(2,1)S(1)}, bf16[128,256]{1,0:T(8,128)(2,1)S(1)}, u32[]{:S(2)}, u32[]{:S(2)}) %collective-permute-start) | collective-permute-done | bytes 65568 | tf_op jit(solution)/shard_map/ppermute | solution.py:304
  22.8 0.0 collective-permute-done.1.below_ref
  22.8 0.9 shard_map.102
  23.7 0.0 copy-start.4
  23.7 1.0 copy-done.4
  24.6 0.7 copy-done.5
  25.4 0.0 all-to-all-done.1.t_ref
  25.4 22.6 %all_to_all.26.s_ref = bf16[16,32,1024]{2,1,0:T(8,128)(2,1)S(1)} all-to-all(bf16[16,32,1024]{2,1,0:T(8,128)(2,1)} %copy-done.4), channel_id=1, replica_groups=mesh['dp'=16,'space'=16] {'dp'}, dimensions={0} | all-to-all | bytes 2097152 | tf_op jit(solution)/shard_map/all_to_all | solution.py:388
  48.0 0.0 copy-done.7
  48.0 2.1 %shard_map.103 = f32[256,128]{1,0:T(8,128)S(1)} custom-call(s32[2,16]{1,0:T(2,128)S(1)} %copy-done.7, bf16[16,32,1024]{2,1,0:T(8,128)(2,1)S(1)} %all_to_all.26.s_ref, bf16[16,32,1024]{2,1,0:T(8,128)(2,1)} %all-to-all-done.1.t_ref), custom_call_target="tpu_custom_call" | custom-call | flops 536870912 | bytes 2097280 | tf_op jit(solution)/shard_map/pallas_call | solution.py:287
  50.1 23.1 %all_to_all.27 = f32[256,1,128]{2,1,0:T(1,128)S(1)} all-to-all(f32[256,1,128]{2,1,0:T(1,128)S(1)} %bitcast.20), channel_id=1, replica_groups=mesh['dp'=16,'space'=16] {'dp','space'}, dimensions={0} | all-to-all | bytes 262144 | tf_op jit(solution)/shard_map/all_to_all | solution.py:391
  73.3 1.8 %shard_map.104 = (bf16[16,32,1024]{2,1,0:T(8,128)(2,1)S(1)}, f32[1,1]{1,0:T(1,128)}) custom-call(s32[2,16]{1,0:T(2,128)S(1)} %copy-done.7, f32[256,128]{1,0:T(8,128)S(1)} %bitcast.21, bf16[16,32,1024]{2,1,0:T(8,128)(2,1)S(1)} %all_to_all.26.s_ref), custom_call_target="tpu_custom_call" | custom-call | flops 16777216 | bytes 1179776 | tf_op jit(solution)/shard_map/pallas_call | solution.py:287
  75.1 19.5 %all_to_all.28.g_ref = bf16[16,32,1024]{2,1,0:T(8,128)(2,1)S(1)} all-to-all(bf16[16,32,1024]{2,1,0:T(8,128)(2,1)S(1)} %get-tuple-element.48), channel_id=1, replica_groups=mesh['dp'=16,'space'=16] {'dp'}, dimensions={0} | all-to-all | bytes 2097152 | tf_op jit(solution)/shard_map/all_to_all | solution.py:398
  94.5 0.5 shard_map.105
  95.0 4.6 %collective-permute-start.2 = (bf16[128,256]{1,0:T(8,128)(2,1)S(1)}, bf16[128,256]{1,0:T(8,128)(2,1)S(1)}, u32[]{:S(2)}, u32[]{:S(2)}) collective-permute-start(bf16[128,256]{1,0:T(8,128)(2,1)S(1)} %get-tuple-element.54), channel_id=1, source_target_pairs={{0,1},{1,2},{2,3},{3,4},{4,5},{5,6},{6,7},{7,8},{8,9},{9,10},{10,1... | collective-permute-start | bytes 196616 | tf_op jit(solution)/shard_map/ppermute | solution.py:304
  99.7 2.7 %collective-permute-start.3 = (bf16[128,256]{1,0:T(8,128)(2,1)S(1)}, bf16[128,256]{1,0:T(8,128)(2,1)S(1)}, u32[]{:S(2)}, u32[]{:S(2)}) collective-permute-start(bf16[128,256]{1,0:T(8,128)(2,1)S(1)} %get-tuple-element.55), channel_id=1, source_target_pairs={{1,0},{2,1},{3,2},{4,3},{5,4},{6,5},{7,6},{8,7},{9,8},{10,9},{11,1... | collective-permute-start | bytes 196616 | tf_op jit(solution)/shard_map/ppermute | solution.py:304
  102.4 1.4 shard_map.106
  103.8 0.9 collective-permute-start.4
  104.8 2.4 %collective-permute-start.5 = (bf16[208,256]{1,0:T(8,128)(2,1)S(1)}, bf16[208,256]{1,0:T(8,128)(2,1)S(1)}, u32[]{:S(2)}, u32[]{:S(2)}) collective-permute-start(bf16[208,256]{1,0:T(8,128)(2,1)S(1)} %get-tuple-element.60), channel_id=1, source_target_pairs={{0,14},{1,15},{2,0},{3,1},{4,2},{5,3},{6,4},{7,5},{8,6},{9,7},{10,... | collective-permute-start | bytes 319496 | tf_op jit(solution)/shard_map/ppermute | solution.py:316
  107.1 0.0 collective-permute-done.2.above_ref
  107.2 1.1 collective-permute-done.3.below_ref
  108.2 1.1 shard_map.107
  109.3 0.4 collective-permute-start.6
  109.8 2.9 %collective-permute-start.7 = (bf16[64,256]{1,0:T(8,128)(2,1)S(1)}, bf16[64,256]{1,0:T(8,128)(2,1)S(1)}, u32[]{:S(2)}, u32[]{:S(2)}) collective-permute-start(bf16[64,256]{1,0:T(8,128)(2,1)S(1)} %get-tuple-element.62), channel_id=1, source_target_pairs={{0,14},{1,15},{2,0},{3,1},{4,2},{5,3},{6,4},{7,5},{8,6},{9,7},{10,... | collective-permute-start | bytes 98312 | tf_op jit(solution)/shard_map/ppermute | solution.py:316
  112.6 1.9 %collective-permute-done.6.refs_2_ = bf16[64,256]{1,0:T(8,128)(2,1)S(1)} collective-permute-done((bf16[64,256]{1,0:T(8,128)(2,1)S(1)}, bf16[64,256]{1,0:T(8,128)(2,1)S(1)}, u32[]{:S(2)}, u32[]{:S(2)}) %collective-permute-start.6) | collective-permute-done | bytes 32800 | tf_op jit(solution)/shard_map/ppermute | solution.py:315
  114.5 0.0 collective-permute-done.7.refs_3_
  114.5 0.0 collective-permute-done.4.refs_0_
  114.5 0.0 collective-permute-done.5.refs_1_
  114.5 0.2 shard_map.109
  114.7 3.5 %collective-permute-start.10 = (bf16[2,272,256]{2,1,0:T(8,128)(2,1)S(1)}, bf16[2,272,256]{2,1,0:T(8,128)(2,1)S(1)}, u32[]{:S(2)}, u32[]{:S(2)}) collective-permute-start(bf16[2,272,256]{2,1,0:T(8,128)(2,1)S(1)} %get-tuple-element.65), channel_id=1, source_target_pairs={{0,14},{1,15},{2,0},{3,1},{4,2},{5,3},{6,4},{7,5},{8,6},{9,7},{10,... | collective-permute-start | bytes 835592 | tf_op jit(solution)/shard_map/ppermute | solution.py:316
  118.2 0.0 collective-permute-start.9
  118.2 4.1 %collective-permute-done.10.refs_1_ = bf16[2,272,256]{2,1,0:T(8,128)(2,1)S(1)} collective-permute-done((bf16[2,272,256]{2,1,0:T(8,128)(2,1)S(1)}, bf16[2,272,256]{2,1,0:T(8,128)(2,1)S(1)}, u32[]{:S(2)}, u32[]{:S(2)}) %collective-permute-start.10) | collective-permute-done | bytes 278560 | tf_op jit(solution)/shard_map/ppermute | solution.py:316
  122.3 4.7 %collective-permute-done.9.refs_0_ = bf16[2,272,256]{2,1,0:T(8,128)(2,1)S(1)} collective-permute-done((bf16[2,272,256]{2,1,0:T(8,128)(2,1)S(1)}, bf16[2,272,256]{2,1,0:T(8,128)(2,1)S(1)}, u32[]{:S(2)}, u32[]{:S(2)}) %collective-permute-start.9) | collective-permute-done | bytes 278560 | tf_op jit(solution)/shard_map/ppermute | solution.py:315
  127.0 0.1 shard_map.110
  127.1 0.1 collective-permute-start.11
  127.2 3.2 %collective-permute-start.12 = (bf16[2,272,256]{2,1,0:T(8,128)(2,1)S(1)}, bf16[2,272,256]{2,1,0:T(8,128)(2,1)S(1)}, u32[]{:S(2)}, u32[]{:S(2)}) collective-permute-start(bf16[2,272,256]{2,1,0:T(8,128)(2,1)S(1)} %get-tuple-element.67), channel_id=1, source_target_pairs={{0,14},{1,15},{2,0},{3,1},{4,2},{5,3},{6,4},{7,5},{8,6},{9,7},{10,... | collective-permute-start | bytes 835592 | tf_op jit(solution)/shard_map/ppermute | solution.py:316
  130.4 0.0 collective-permute-start.8
  130.4 6.0 %collective-permute-done.11.refs_0_ = bf16[2,272,256]{2,1,0:T(8,128)(2,1)S(1)} collective-permute-done((bf16[2,272,256]{2,1,0:T(8,128)(2,1)S(1)}, bf16[2,272,256]{2,1,0:T(8,128)(2,1)S(1)}, u32[]{:S(2)}, u32[]{:S(2)}) %collective-permute-start.11) | collective-permute-done | bytes 278560 | tf_op jit(solution)/shard_map/ppermute | solution.py:315
  136.4 0.0 collective-permute-done.12.refs_1_
  136.4 0.1 shard_map.111
  136.6 0.1 collective-permute-start.13
  136.7 5.6 %collective-permute-start.14 = (bf16[272,256]{1,0:T(8,128)(2,1)S(1)}, bf16[272,256]{1,0:T(8,128)(2,1)S(1)}, u32[]{:S(2)}, u32[]{:S(2)}) collective-permute-start(bf16[272,256]{1,0:T(8,128)(2,1)S(1)} %get-tuple-element.69), channel_id=1, source_target_pairs={{0,15},{1,14},{2,1},{3,0},{4,3},{5,2},{6,5},{7,4},{8,7},{9,6},{10,... | collective-permute-start | bytes 417800 | tf_op jit(solution)/shard_map/ppermute | solution.py:336
  142.3 0.0 collective-permute-start.15
  142.3 3.2 %collective-permute-start.16 = (bf16[272,256]{1,0:T(8,128)(2,1)S(1)}, bf16[272,256]{1,0:T(8,128)(2,1)S(1)}, u32[]{:S(2)}, u32[]{:S(2)}) collective-permute-start(bf16[272,256]{1,0:T(8,128)(2,1)S(1)} %get-tuple-element.71), channel_id=1, source_target_pairs={{0,14},{1,15},{2,0},{3,1},{4,2},{5,3},{6,4},{7,5},{8,6},{9,7},{10,... | collective-permute-start | bytes 417800 | tf_op jit(solution)/shard_map/ppermute | solution.py:336
  145.5 1.4 shard_map.108
  147.0 0.0 collective-permute-done.8.own_ref
  147.0 0.0 collective-permute-done.13.us
  147.0 0.0 collective-permute-done.14.uc
  147.0 1.6 %collective-permute-done.15.ds = bf16[272,256]{1,0:T(8,128)(2,1)S(1)} collective-permute-done((bf16[272,256]{1,0:T(8,128)(2,1)S(1)}, bf16[272,256]{1,0:T(8,128)(2,1)S(1)}, u32[]{:S(2)}, u32[]{:S(2)}) %collective-permute-start.15) | collective-permute-done | bytes 139296 | tf_op jit(solution)/shard_map/ppermute | solution.py:336
  148.6 0.0 collective-permute-done.16.dc
  148.6 0.8 shard_map.112
  (4 shorter events, 0.0 us)
Async XLA Ops:
  0.6 5.5 %copy-start = (bf16[1,4,128,1024]{3,2,1,0:T(8,128)(2,1)S(1)}, bf16[1,4,128,1024]{3,2,1,0:T(8,128)(2,1)}, u32[]{:S(2)}) copy-start(bf16[1,4,128,1024]{3,2,1,0:T(8,128)(2,1)} %param.6) | copy-start | bytes 3145732
  0.6 5.5 %copy-start.2 = (bf16[1024,256]{1,0:T(8,128)(2,1)S(1)}, bf16[1024,256]{1,0:T(8,128)(2,1)}, u32[]{:S(2)}) copy-start(bf16[1024,256]{1,0:T(8,128)(2,1)} %wr_ref.3) | copy-start | bytes 1572868
  0.7 24.7 %all-to-all-start.1 = ((bf16[16,32,1024]{2,1,0:T(8,128)(2,1)}), bf16[16,32,1024]{2,1,0:T(8,128)(2,1)}, u32[]{:S(2)}, u32[]{:S(2)}) async-start(bf16[16,32,1024]{2,1,0:T(8,128)(2,1)} %bitcast.22), calls=%async_computation.1 | async-start | bytes 2097152 | tf_op jit(solution)/shard_map/all_to_all | solution.py:354
  6.1 7.9 %copy-start.1 = (bf16[3,3,256,256]{3,2,1,0:T(8,128)(2,1)S(1)}, bf16[3,3,256,256]{3,2,1,0:T(8,128)(2,1)}, u32[]{:S(2)}) copy-start(bf16[3,3,256,256]{3,2,1,0:T(8,128)(2,1)} %ws_ref.7) | copy-start | bytes 3538948
  6.1 7.9 %copy-start.3 = (bf16[256,1024]{1,0:T(8,128)(2,1)S(1)}, bf16[256,1024]{1,0:T(8,128)(2,1)}, u32[]{:S(2)}) copy-start(bf16[256,1024]{1,0:T(8,128)(2,1)} %we_ref.5) | copy-start | bytes 1572868
  6.4 16.3 %collective-permute-start = (bf16[128,256]{1,0:T(8,128)(2,1)S(1)}, bf16[128,256]{1,0:T(8,128)(2,1)S(1)}, u32[]{:S(2)}, u32[]{:S(2)}) collective-permute-start(bf16[128,256]{1,0:T(8,128)(2,1)S(1)} %get-tuple-element.41.last_ref), channel_id=1, source_target_pairs={{0,1},{1,2},{2,3},{3,4},{4,5},{5,6},{6,7},{7,8},{8,9},{9,10},{10,1... | collective-permute-start | bytes 196616 | tf_op jit(solution)/shard_map/ppermute | solution.py:304
  10.6 12.1 %collective-permute-start.1 = (bf16[128,256]{1,0:T(8,128)(2,1)S(1)}, bf16[128,256]{1,0:T(8,128)(2,1)S(1)}, u32[]{:S(2)}, u32[]{:S(2)}) collective-permute-start(bf16[128,256]{1,0:T(8,128)(2,1)S(1)} %get-tuple-element.40.first_ref), channel_id=1, source_target_pairs={{1,0},{2,1},{3,2},{4,3},{5,4},{6,5},{7,6},{8,7},{9,8},{10,9},{11,1... | collective-permute-start | bytes 196616 | tf_op jit(solution)/shard_map/ppermute | solution.py:304
  23.7 1.0 copy-start.4
  24.6 0.7 copy-start.5
  25.4 22.6 %copy-start.7 = (s32[2,16]{1,0:T(2,128)S(1)}, s32[2,16]{1,0:T(2,128)}, u32[]{:S(2)}) copy-start(s32[2,16]{1,0:T(2,128)} %parts_ref.3) | copy-start | bytes 388
  75.0 27.4 %copy-start.6 = (bf16[6,128,256]{2,1,0:T(8,128)(2,1)S(1)}, bf16[6,128,256]{2,1,0:T(8,128)(2,1)}, u32[]{:S(2)}) copy-start(bf16[6,128,256]{2,1,0:T(8,128)(2,1)} %copy-done.5) | copy-start | bytes 1179652
  95.0 12.1 %collective-permute-start.2 = (bf16[128,256]{1,0:T(8,128)(2,1)S(1)}, bf16[128,256]{1,0:T(8,128)(2,1)S(1)}, u32[]{:S(2)}, u32[]{:S(2)}) collective-permute-start(bf16[128,256]{1,0:T(8,128)(2,1)S(1)} %get-tuple-element.54), channel_id=1, source_target_pairs={{0,1},{1,2},{2,3},{3,4},{4,5},{5,6},{6,7},{7,8},{8,9},{9,10},{10,1... | collective-permute-start | bytes 196616 | tf_op jit(solution)/shard_map/ppermute | solution.py:304
  99.7 8.6 %collective-permute-start.3 = (bf16[128,256]{1,0:T(8,128)(2,1)S(1)}, bf16[128,256]{1,0:T(8,128)(2,1)S(1)}, u32[]{:S(2)}, u32[]{:S(2)}) collective-permute-start(bf16[128,256]{1,0:T(8,128)(2,1)S(1)} %get-tuple-element.55), channel_id=1, source_target_pairs={{1,0},{2,1},{3,2},{4,3},{5,4},{6,5},{7,6},{8,7},{9,8},{10,9},{11,1... | collective-permute-start | bytes 196616 | tf_op jit(solution)/shard_map/ppermute | solution.py:304
  103.8 10.7 %collective-permute-start.4 = (bf16[208,256]{1,0:T(8,128)(2,1)S(1)}, bf16[208,256]{1,0:T(8,128)(2,1)S(1)}, u32[]{:S(2)}, u32[]{:S(2)}) collective-permute-start(bf16[208,256]{1,0:T(8,128)(2,1)S(1)} %get-tuple-element.59), channel_id=1, source_target_pairs={{0,2},{1,3},{2,4},{3,5},{4,6},{5,7},{6,8},{7,9},{8,10},{9,11},{10,... | collective-permute-start | bytes 319496 | tf_op jit(solution)/shard_map/ppermute | solution.py:315
  104.8 9.8 %collective-permute-start.5 = (bf16[208,256]{1,0:T(8,128)(2,1)S(1)}, bf16[208,256]{1,0:T(8,128)(2,1)S(1)}, u32[]{:S(2)}, u32[]{:S(2)}) collective-permute-start(bf16[208,256]{1,0:T(8,128)(2,1)S(1)} %get-tuple-element.60), channel_id=1, source_target_pairs={{0,14},{1,15},{2,0},{3,1},{4,2},{5,3},{6,4},{7,5},{8,6},{9,7},{10,... | collective-permute-start | bytes 319496 | tf_op jit(solution)/shard_map/ppermute | solution.py:316
  109.3 5.2 %collective-permute-start.6 = (bf16[64,256]{1,0:T(8,128)(2,1)S(1)}, bf16[64,256]{1,0:T(8,128)(2,1)S(1)}, u32[]{:S(2)}, u32[]{:S(2)}) collective-permute-start(bf16[64,256]{1,0:T(8,128)(2,1)S(1)} %get-tuple-element.61), channel_id=1, source_target_pairs={{0,2},{1,3},{2,4},{3,5},{4,6},{5,7},{6,8},{7,9},{8,10},{9,11},{10,... | collective-permute-start | bytes 98312 | tf_op jit(solution)/shard_map/ppermute | solution.py:315
  109.8 4.8 %collective-permute-start.7 = (bf16[64,256]{1,0:T(8,128)(2,1)S(1)}, bf16[64,256]{1,0:T(8,128)(2,1)S(1)}, u32[]{:S(2)}, u32[]{:S(2)}) collective-permute-start(bf16[64,256]{1,0:T(8,128)(2,1)S(1)} %get-tuple-element.62), channel_id=1, source_target_pairs={{0,14},{1,15},{2,0},{3,1},{4,2},{5,3},{6,4},{7,5},{8,6},{9,7},{10,... | collective-permute-start | bytes 98312 | tf_op jit(solution)/shard_map/ppermute | solution.py:316
  114.7 7.6 %collective-permute-start.10 = (bf16[2,272,256]{2,1,0:T(8,128)(2,1)S(1)}, bf16[2,272,256]{2,1,0:T(8,128)(2,1)S(1)}, u32[]{:S(2)}, u32[]{:S(2)}) collective-permute-start(bf16[2,272,256]{2,1,0:T(8,128)(2,1)S(1)} %get-tuple-element.65), channel_id=1, source_target_pairs={{0,14},{1,15},{2,0},{3,1},{4,2},{5,3},{6,4},{7,5},{8,6},{9,7},{10,... | collective-permute-start | bytes 835592 | tf_op jit(solution)/shard_map/ppermute | solution.py:316
  118.2 8.8 %collective-permute-start.9 = (bf16[2,272,256]{2,1,0:T(8,128)(2,1)S(1)}, bf16[2,272,256]{2,1,0:T(8,128)(2,1)S(1)}, u32[]{:S(2)}, u32[]{:S(2)}) collective-permute-start(bf16[2,272,256]{2,1,0:T(8,128)(2,1)S(1)} %get-tuple-element.64), channel_id=1, source_target_pairs={{0,2},{1,3},{2,4},{3,5},{4,6},{5,7},{6,8},{7,9},{8,10},{9,11},{10,... | collective-permute-start | bytes 835592 | tf_op jit(solution)/shard_map/ppermute | solution.py:315
  127.1 9.3 %collective-permute-start.11 = (bf16[2,272,256]{2,1,0:T(8,128)(2,1)S(1)}, bf16[2,272,256]{2,1,0:T(8,128)(2,1)S(1)}, u32[]{:S(2)}, u32[]{:S(2)}) collective-permute-start(bf16[2,272,256]{2,1,0:T(8,128)(2,1)S(1)} %get-tuple-element.66), channel_id=1, source_target_pairs={{0,2},{1,3},{2,4},{3,5},{4,6},{5,7},{6,8},{7,9},{8,10},{9,11},{10,... | collective-permute-start | bytes 835592 | tf_op jit(solution)/shard_map/ppermute | solution.py:315
  127.2 9.2 %collective-permute-start.12 = (bf16[2,272,256]{2,1,0:T(8,128)(2,1)S(1)}, bf16[2,272,256]{2,1,0:T(8,128)(2,1)S(1)}, u32[]{:S(2)}, u32[]{:S(2)}) collective-permute-start(bf16[2,272,256]{2,1,0:T(8,128)(2,1)S(1)} %get-tuple-element.67), channel_id=1, source_target_pairs={{0,14},{1,15},{2,0},{3,1},{4,2},{5,3},{6,4},{7,5},{8,6},{9,7},{10,... | collective-permute-start | bytes 835592 | tf_op jit(solution)/shard_map/ppermute | solution.py:316
  130.4 16.6 %collective-permute-start.8 = (bf16[272,256]{1,0:T(8,128)(2,1)S(1)}, bf16[272,256]{1,0:T(8,128)(2,1)S(1)}, u32[]{:S(2)}, u32[]{:S(2)}) collective-permute-start(bf16[272,256]{1,0:T(8,128)(2,1)S(1)} %get-tuple-element.63), channel_id=1, source_target_pairs={{0,1},{1,0},{2,3},{3,2},{4,5},{5,4},{6,7},{7,6},{8,9},{9,8},{10,11... | collective-permute-start | bytes 417800 | tf_op jit(solution)/shard_map/ppermute | solution.py:328
  136.6 10.4 %collective-permute-start.13 = (bf16[272,256]{1,0:T(8,128)(2,1)S(1)}, bf16[272,256]{1,0:T(8,128)(2,1)S(1)}, u32[]{:S(2)}, u32[]{:S(2)}) collective-permute-start(bf16[272,256]{1,0:T(8,128)(2,1)S(1)} %get-tuple-element.68), channel_id=1, source_target_pairs={{0,3},{1,2},{2,5},{3,4},{4,7},{5,6},{6,9},{7,8},{8,11},{9,10},{10,... | collective-permute-start | bytes 417800 | tf_op jit(solution)/shard_map/ppermute | solution.py:336
  136.7 10.3 %collective-permute-start.14 = (bf16[272,256]{1,0:T(8,128)(2,1)S(1)}, bf16[272,256]{1,0:T(8,128)(2,1)S(1)}, u32[]{:S(2)}, u32[]{:S(2)}) collective-permute-start(bf16[272,256]{1,0:T(8,128)(2,1)S(1)} %get-tuple-element.69), channel_id=1, source_target_pairs={{0,15},{1,14},{2,1},{3,0},{4,3},{5,2},{6,5},{7,4},{8,7},{9,6},{10,... | collective-permute-start | bytes 417800 | tf_op jit(solution)/shard_map/ppermute | solution.py:336
  142.3 6.3 %collective-permute-start.15 = (bf16[272,256]{1,0:T(8,128)(2,1)S(1)}, bf16[272,256]{1,0:T(8,128)(2,1)S(1)}, u32[]{:S(2)}, u32[]{:S(2)}) collective-permute-start(bf16[272,256]{1,0:T(8,128)(2,1)S(1)} %get-tuple-element.70), channel_id=1, source_target_pairs={{0,2},{1,3},{2,4},{3,5},{4,6},{5,7},{6,8},{7,9},{8,10},{9,11},{10,... | collective-permute-start | bytes 417800 | tf_op jit(solution)/shard_map/ppermute | solution.py:336
  142.3 6.3 %collective-permute-start.16 = (bf16[272,256]{1,0:T(8,128)(2,1)S(1)}, bf16[272,256]{1,0:T(8,128)(2,1)S(1)}, u32[]{:S(2)}, u32[]{:S(2)}) collective-permute-start(bf16[272,256]{1,0:T(8,128)(2,1)S(1)} %get-tuple-element.71), channel_id=1, source_target_pairs={{0,14},{1,15},{2,0},{3,1},{4,2},{5,3},{6,4},{7,5},{8,6},{9,7},{10,... | collective-permute-start | bytes 417800 | tf_op jit(solution)/shard_map/ppermute | solution.py:336

commit v5 on v4

--- a/solution.py
+++ b/solution.py
@@ -180,7 +180,8 @@
 
 
 def window_kernel(
-    place_ref, g_ref, h2_ref, g2_ref, hp_ref, ws_ref, out_ref, g1_ref, up_ref, down_ref
+    place_ref, g_ref, h2_ref, g2_ref, hp_ref, ws_ref,
+    out_ref, g1_ref, up_ref, down_ref, near_ref,
 ):
     rows, cols, mid = g2_ref.shape
     chunks = out_ref.shape[0]
@@ -200,6 +201,7 @@
             grad = dot(moved[b], source, FIRST_DOT).astype(BF16)
             out_ref[:, start : start + width] = grad.reshape(chunks, width, mid)
     farthest(place_ref, out_ref, up_ref, down_ref)
+    near_others(place_ref, out_ref, near_ref)
     sums = taps([flat(g2_ref[2 - a : rows - a]) for a in range(3)], ws_ref, LAST_DOT)
     total = narrowed(sums, cols)
     g1_ref[...] = jnp.where(flat(hp_ref[2:rows]) > 0, total, 0.0).astype(BF16)
@@ -234,41 +236,72 @@
     out_ref[0, 1 : rows - 1] = inner.reshape(rows - 2, cols, -1)
 
 
-def add_kernel(offset, first, last, place_ref, early_ref, late_ref, *refs):
+def near_others(place_ref, local_ref, out_ref):
+    depth = local_ref.shape[0] // 2
+    z, half = place_ref[0] // 2, place_ref[0] % 2
+    for index in range(3):
+        out_ref[index] = local_ref[2 * ((z + index - 1 + depth) % depth) + 1 - half]
+
+
+def join_kernel(
+    offset, place_ref, early_ref, late_ref, eu, ed, lu, ld, up_ref, down_ref, near_ref
+):
+    rows = early_ref.shape[1]
+    depth = early_ref.shape[0] // 2
+    near_others(place_ref, late_ref, near_ref)
+    for way, (sign, got, out_ref) in enumerate(((1, (eu, lu), up_ref), (-1, (ed, ld), down_ref))):
+        block = 2 * ((place_ref[0] // 2 + sign * offset + depth) % depth)
+        for side in range(2):
+            early, late = early_ref[block + side], late_ref[block + side]
+            if side == way:
+                early = (early.astype(F32) + got[0][...].astype(F32)).astype(BF16)
+                late = (late.astype(F32) + got[1][...].astype(F32)).astype(BF16)
+            out_ref[side, :rows] = early
+            out_ref[side, rows:] = late
+
+
+def pass_kernel(offset, split, place_ref, early_ref, late_ref, gu_ref, gd_ref, *outs):
     rows = early_ref.shape[1]
     depth = early_ref.shape[0] // 2
     z, half = place_ref[0] // 2, place_ref[0] % 2
-    outs = list(refs[4:] if first else refs[2:])
-    if first:
-        give_ref = outs.pop()
-        block = 2 * z + 1 - half
-        give_ref[:rows] = early_ref[block]
-        give_ref[rows:] = late_ref[block]
-    for way, sign in enumerate((1, -1)):
+    for way, (sign, got_ref) in enumerate(((1, gu_ref), (-1, gd_ref))):
         block = 2 * ((z + sign * offset + depth) % depth)
-        for index, side in enumerate((half, 1 - half) if last else (0, 1)):
-            early = early_ref[block + side].astype(F32)
-            late = late_ref[block + side].astype(F32)
-            if first:
-                here = jnp.where(side == way, 1.0, 0.0).astype(F32)
-                early = early + here * refs[way][...].astype(F32)
-                late = late + here * refs[2 + way][...].astype(F32)
-            else:
-                early = early + refs[way][side, :rows].astype(F32)
-                late = late + refs[way][side, rows:].astype(F32)
-            target = outs[2 * way + index] if last else outs[way].at[side]
+        for index, side in enumerate((half, 1 - half) if split else (0, 1)):
+            early = early_ref[block + side].astype(F32) + got_ref[side, :rows].astype(F32)
+            late = late_ref[block + side].astype(F32) + got_ref[side, rows:].astype(F32)
+            target = outs[2 * way + index] if split else outs[way].at[side]
             target[:rows] = early.astype(BF16)
             target[rows:] = late.astype(BF16)
 
 
+def own_terms(place_ref, early_ref, late_ref, ne_ref, nl_ref, offset):
+    depth = early_ref.shape[0] // 2
+    z, half = place_ref[0] // 2, place_ref[0] % 2
+    block = 2 * ((z + offset + depth) % depth) + half
+    early = early_ref[block].astype(F32) + ne_ref[1 + offset].astype(F32)
+    return early, late_ref[block].astype(F32) + nl_ref[1 + offset].astype(F32)
+
+
+def side_kernel(
+    place_ref, early_ref, late_ref, ne_ref, nl_ref, us, uc, ds, dc, up_ref, down_ref
+):
+    rows = early_ref.shape[1]
+    for offset, got, out_ref in ((1, (us, uc), up_ref), (-1, (ds, dc), down_ref)):
+        early, late = own_terms(place_ref, early_ref, late_ref, ne_ref, nl_ref, offset)
+        for ref in got:
+            early = early + ref[:rows].astype(F32)
+            late = late + ref[rows:].astype(F32)
+        out_ref[:rows] = early.astype(BF16)
+        out_ref[rows:] = late.astype(BF16)
+
+
 def last_kernel(
-    place_ref, early_ref, late_ref, own_ref, us, uc, ds, dc, expand_ref, spatial_ref, reduce_ref
+    place_ref, early_ref, late_ref, ne_ref, nl_ref, gu_ref, gd_ref,
+    expand_ref, spatial_ref, reduce_ref,
 ):
     rows = early_ref.shape[1]
-    block = place_ref[0]
-    early = early_ref[block].astype(F32)
-    late = late_ref[block].astype(F32)
-    for ref in (own_ref, us, uc, ds, dc):
+    early, late = own_terms(place_ref, early_ref, late_ref, ne_ref, nl_ref, 0)
+    for ref in (gu_ref, gd_ref):
         early = early + ref[:rows].astype(F32)
         late = late + ref[rows:].astype(F32)
     part = expand_ref.shape[0]
@@ -304,37 +337,43 @@
     return lax.ppermute(last, "space", up), lax.ppermute(first, "space", down)
 
 
-def scattered(early, late, early_sends, late_sends, place):
+def scattered(early, late, early_sends, late_sends, near_early, place):
     peers = lax.axis_size("space")
     far = peers // 4
     ups = [(i, (i + 2) % peers) for i in range(peers)]
     downs = [(i, (i - 2) % peers) for i in range(peers)]
+    swap = [(i, i ^ 1) for i in range(peers)]
     rows, mid = early.shape[1] + late.shape[1], early.shape[2]
+    side = ((rows, mid), BF16)
+    pair = [((2, rows, mid), BF16)] * 2
+
+    def sent(value, path):
+        return lax.ppermute(value, "space", path)
 
     def moved(up, down):
-        up = lax.ppermute(up, "space", ups)
-        down = lax.ppermute(down, "space", downs)
-        return up, down
-
-    got = moved(*early_sends) + moved(*late_sends)
-    for step in range(2, far + 1):
-        first, last = step == 2, step == far
-        kernel = functools.partial(add_kernel, far + 1 - step, first, last)
-        half = ((rows, mid), BF16)
-        outs = [half] * 4 if last else [((2, rows, mid), BF16)] * 2
-        outs = outs + [half] * first
-        got = list(call(kernel, outs, rows * mid, smem=1)(place, early, late, *got))
-        if first:
-            own = lax.ppermute(got.pop(), "space", [(i, i ^ 1) for i in range(peers)])
-        if not last:
-            got = moved(*got)
-    cross_ups = [(i, j ^ 1) for i, j in ups]
-    cross_downs = [(i, j ^ 1) for i, j in downs]
-    sends = ((1, cross_ups), (3, cross_downs), (0, ups), (2, downs))
-    ended = []
-    for index, path in sends:
-        ended.append(lax.ppermute(got[index], "space", path))
-    return own, *ended
+        return sent(up, ups), sent(down, downs)
+
+    got = moved(*early_sends)
+    near_early = sent(near_early, swap)
+    got = got + moved(*late_sends)
+    near = ((3, *late.shape[1:]), BF16)
+    join = functools.partial(join_kernel, far - 1)
+    up, down, near_late = call(join, pair + [near], rows * mid, smem=1)(place, early, late, *got)
+    up, down = moved(up, down)
+    near_late = sent(near_late, swap)
+    for step in range(3, far):
+        split = step == far - 1
+        kernel = functools.partial(pass_kernel, far + 1 - step, split)
+        outs = [side] * 4 if split else pair
+        got = call(kernel, outs, rows * mid, smem=1)(place, early, late, up, down)
+        if not split:
+            up, down = moved(*got)
+    uc = sent(got[1], [(i, j ^ 1) for i, j in ups])
+    dc = sent(got[3], [(i, j ^ 1) for i, j in downs])
+    us, ds = moved(got[0], got[2])
+    terms = (place, early, late, near_early, near_late)
+    up, down = call(side_kernel, [side] * 2, rows * mid, smem=1)(*terms, us, uc, ds, dc)
+    return *terms, *moved(up, down)
 
 
 def step(images, teacher, w_reduce, w_spatial, w_expand, partners):
@@ -401,10 +440,11 @@
     )(grads, h_two, w_expand)
     over, under = exchanged(first, last)
     part, width = channels // n_space, mid // n_space
-    early, g1_in, *early_sends = call(
+    early, g1_in, *early_sends, near_early = call(
         window_kernel,
         [((n_space, part + 9 * width, mid), BF16), ((inside, mid), BF16)]
-        + [((part + 9 * width, mid), BF16)] * 2,
+        + [((part + 9 * width, mid), BF16)] * 2
+        + [((3, part + 9 * width, mid), BF16)],
         70 * mac,
         smem=1,
     )(place, grads, h_two, g_two, h_pad, w_spatial)
@@ -422,7 +462,7 @@
         [((part, mid), F32), ((3, 3, width, mid), F32), ((part, mid), F32)],
         mac,
         smem=1,
-    )(place, early, late, *scattered(early, late, early_sends, late_sends, place))
+    )(*scattered(early, late, early_sends, late_sends, near_early, place))
     return (
         loss[0, 0],
         g_images,

time: 150 us -> 148 us (0.987)
  the two profiles are of different devices: /device:TPU:4 before, /device:TPU:6 now
where the time goes in v5:
time: 148 us
  blocking collectives  63.8 us (43%)
  starting transfers between devices  43.5 us (29%)
  waiting for transfers between devices  25.9 us (18%)
  Pallas kernels  11.7 us (8%)
  local copies, waits for them, and re-layouts  1.76 us (1%)
    all_to_all x1, blocking collectives, step(): message = lax.all_to_all(message, ('dp', 'space'), 0, 0, tiled=True)  23.6 us
    ppermute x14, starting transfers between devices, sent(): return lax.ppermute(value, 'space', path)  22.6 us
    all_to_all x1, blocking collectives, step(): s_all = lax.all_to_all(s_all, 'dp', 0, 0, tiled=True)  21.2 us
    all_to_all x1, blocking collectives, step(): grads = lax.all_to_all(grads, 'dp', 0, 0, tiled=True)  19.1 us
    ppermute x14, waiting for transfers between devices, sent(): return lax.ppermute(value, 'space', path)  16.2 us
    ppermute x4, starting transfers between devices, exchanged(): return (lax.ppermute(last, 'space', up), lax.ppermute(first, 'space', down))  14.8 us
    pallas_call x12, Pallas kernels, run(): pl.pallas_call(kernel, out_shape=[jax.ShapeDtypeStruct(s, d) for s, d in...  11.4 us
    ppermute x4, waiting for transfers between devices, exchanged(): return (lax.ppermute(last, 'space', up), lax.ppermute(first, 'space', down))  9.67 us
  transfers between devices with their start and end apart: 19, of which 7 were waited for; matrix products, arithmetic and copies ran while one was open for 0% of the time, Pallas kernels for 4%

profile of v5, /device:TPU:6, one launch (start us, length us, event | category | flops | bytes accessed | tf_op | source)
XLA Modules:
  0.0 147.6 jit_solution(7732681039744250202)
XLA Ops:
  0.6 0.0 copy-start
  0.6 0.0 copy-start.2
  0.7 6.1 %all-to-all-start.1 = ((bf16[16,32,1024]{2,1,0:T(8,128)(2,1)}), bf16[16,32,1024]{2,1,0:T(8,128)(2,1)}, u32[]{:S(2)}, u32[]{:S(2)}) async-start(bf16[16,32,1024]{2,1,0:T(8,128)(2,1)} %bitcast.22), calls=%async_computation.1 | async-start | bytes 2097152 | tf_op jit(solution)/shard_map/all_to_all | solution.py:393
  6.8 0.0 copy-start.3
  6.8 0.0 copy-done
  6.8 0.0 copy-done.2
  6.8 0.3 edge.1
  7.1 4.8 %collective-permute-start = (bf16[128,256]{1,0:T(8,128)(2,1)S(1)}, bf16[128,256]{1,0:T(8,128)(2,1)S(1)}, u32[]{:S(2)}, u32[]{:S(2)}) collective-permute-start(bf16[128,256]{1,0:T(8,128)(2,1)S(1)} %get-tuple-element.42.last_ref), channel_id=1, source_target_pairs={{0,1},{1,2},{2,3},{3,4},{4,5},{5,6},{6,7},{7,8},{8,9},{9,10},{10,1... | collective-permute-start | bytes 196616 | tf_op jit(solution)/shard_map/ppermute | solution.py:337
  11.9 2.7 %collective-permute-start.1 = (bf16[128,256]{1,0:T(8,128)(2,1)S(1)}, bf16[128,256]{1,0:T(8,128)(2,1)S(1)}, u32[]{:S(2)}, u32[]{:S(2)}) collective-permute-start(bf16[128,256]{1,0:T(8,128)(2,1)S(1)} %get-tuple-element.41.first_ref), channel_id=1, source_target_pairs={{1,0},{2,1},{3,2},{4,3},{5,4},{6,5},{7,6},{8,7},{9,8},{10,9},{11,1... | collective-permute-start | bytes 196616 | tf_op jit(solution)/shard_map/ppermute | solution.py:337
  14.6 0.0 copy-done.1
  14.6 0.0 copy-done.3
  14.6 1.1 shard_map.101
  15.7 8.1 %collective-permute-done.above_ref = bf16[128,256]{1,0:T(8,128)(2,1)S(1)} collective-permute-done((bf16[128,256]{1,0:T(8,128)(2,1)S(1)}, bf16[128,256]{1,0:T(8,128)(2,1)S(1)}, u32[]{:S(2)}, u32[]{:S(2)}) %collective-permute-start) | collective-permute-done | bytes 65568 | tf_op jit(solution)/shard_map/ppermute | solution.py:337
  23.8 0.0 collective-permute-done.1.below_ref
  23.8 0.9 shard_map.102
  24.7 0.0 copy-start.4
  24.7 1.0 copy-done.4
  25.6 0.8 copy-done.5
  26.4 0.0 all-to-all-done.1.t_ref
  26.4 21.2 %all_to_all.26.s_ref = bf16[16,32,1024]{2,1,0:T(8,128)(2,1)S(1)} all-to-all(bf16[16,32,1024]{2,1,0:T(8,128)(2,1)} %copy-done.4), channel_id=1, replica_groups=mesh['dp'=16,'space'=16] {'dp'}, dimensions={0} | all-to-all | bytes 2097152 | tf_op jit(solution)/shard_map/all_to_all | solution.py:427
  47.6 2.1 %shard_map.103 = f32[256,128]{1,0:T(8,128)S(1)} custom-call(s32[2,16]{1,0:T(2,128)S(1)} %copy-done.7, bf16[16,32,1024]{2,1,0:T(8,128)(2,1)S(1)} %all_to_all.26.s_ref, bf16[16,32,1024]{2,1,0:T(8,128)(2,1)} %all-to-all-done.1.t_ref), custom_call_target="tpu_custom_call" | custom-call | flops 536870912 | bytes 2097280 | tf_op jit(solution)/shard_map/pallas_call | solution.py:320
  49.7 23.6 %all_to_all.27 = f32[256,1,128]{2,1,0:T(1,128)S(1)} all-to-all(f32[256,1,128]{2,1,0:T(1,128)S(1)} %bitcast.20), channel_id=1, replica_groups=mesh['dp'=16,'space'=16] {'dp','space'}, dimensions={0} | all-to-all | bytes 262144 | tf_op jit(solution)/shard_map/all_to_all | solution.py:430
  73.3 1.8 %shard_map.104 = (bf16[16,32,1024]{2,1,0:T(8,128)(2,1)S(1)}, f32[1,1]{1,0:T(1,128)}) custom-call(s32[2,16]{1,0:T(2,128)S(1)} %copy-done.7, f32[256,128]{1,0:T(8,128)S(1)} %bitcast.21, bf16[16,32,1024]{2,1,0:T(8,128)(2,1)S(1)} %all_to_all.26.s_ref), custom_call_target="tpu_custom_call" | custom-call | flops 16777216 | bytes 1179776 | tf_op jit(solution)/shard_map/pallas_call | solution.py:320
  75.1 19.1 %all_to_all.28.g_ref = bf16[16,32,1024]{2,1,0:T(8,128)(2,1)S(1)} all-to-all(bf16[16,32,1024]{2,1,0:T(8,128)(2,1)S(1)} %get-tuple-element.49), channel_id=1, replica_groups=mesh['dp'=16,'space'=16] {'dp'}, dimensions={0} | all-to-all | bytes 2097152 | tf_op jit(solution)/shard_map/all_to_all | solution.py:437
  94.1 0.5 shard_map.105
  94.6 5.2 %collective-permute-start.2 = (bf16[128,256]{1,0:T(8,128)(2,1)S(1)}, bf16[128,256]{1,0:T(8,128)(2,1)S(1)}, u32[]{:S(2)}, u32[]{:S(2)}) collective-permute-start(bf16[128,256]{1,0:T(8,128)(2,1)S(1)} %get-tuple-element.55), channel_id=1, source_target_pairs={{0,1},{1,2},{2,3},{3,4},{4,5},{5,6},{6,7},{7,8},{8,9},{9,10},{10,1... | collective-permute-start | bytes 196616 | tf_op jit(solution)/shard_map/ppermute | solution.py:337
  99.8 2.2 %collective-permute-start.3 = (bf16[128,256]{1,0:T(8,128)(2,1)S(1)}, bf16[128,256]{1,0:T(8,128)(2,1)S(1)}, u32[]{:S(2)}, u32[]{:S(2)}) collective-permute-start(bf16[128,256]{1,0:T(8,128)(2,1)S(1)} %get-tuple-element.56), channel_id=1, source_target_pairs={{1,0},{2,1},{3,2},{4,3},{5,4},{6,5},{7,6},{8,7},{9,8},{10,9},{11,1... | collective-permute-start | bytes 196616 | tf_op jit(solution)/shard_map/ppermute | solution.py:337
  102.0 1.5 shard_map.106
  103.5 0.9 collective-permute-start.5
  104.4 2.4 %collective-permute-start.6 = (bf16[208,256]{1,0:T(8,128)(2,1)S(1)}, bf16[208,256]{1,0:T(8,128)(2,1)S(1)}, u32[]{:S(2)}, u32[]{:S(2)}) collective-permute-start(bf16[208,256]{1,0:T(8,128)(2,1)S(1)} %get-tuple-element.62), channel_id=1, source_target_pairs={{0,14},{1,15},{2,0},{3,1},{4,2},{5,3},{6,4},{7,5},{8,6},{9,7},{10,... | collective-permute-start | bytes 319496 | tf_op jit(solution)/shard_map/ppermute | solution.py:351
  106.8 0.0 collective-permute-done.2.above_ref
  106.8 1.6 %collective-permute-done.3.below_ref = bf16[128,256]{1,0:T(8,128)(2,1)S(1)} collective-permute-done((bf16[128,256]{1,0:T(8,128)(2,1)S(1)}, bf16[128,256]{1,0:T(8,128)(2,1)S(1)}, u32[]{:S(2)}, u32[]{:S(2)}) %collective-permute-start.3) | collective-permute-done | bytes 65568 | tf_op jit(solution)/shard_map/ppermute | solution.py:337
  108.4 1.1 shard_map.107
  109.5 0.5 collective-permute-start.7
  109.9 2.9 %collective-permute-start.8 = (bf16[64,256]{1,0:T(8,128)(2,1)S(1)}, bf16[64,256]{1,0:T(8,128)(2,1)S(1)}, u32[]{:S(2)}, u32[]{:S(2)}) collective-permute-start(bf16[64,256]{1,0:T(8,128)(2,1)S(1)} %get-tuple-element.64), channel_id=1, source_target_pairs={{0,14},{1,15},{2,0},{3,1},{4,2},{5,3},{6,4},{7,5},{8,6},{9,7},{10,... | collective-permute-start | bytes 98312 | tf_op jit(solution)/shard_map/ppermute | solution.py:351
  112.8 1.9 %collective-permute-done.7.lu = bf16[64,256]{1,0:T(8,128)(2,1)S(1)} collective-permute-done((bf16[64,256]{1,0:T(8,128)(2,1)S(1)}, bf16[64,256]{1,0:T(8,128)(2,1)S(1)}, u32[]{:S(2)}, u32[]{:S(2)}) %collective-permute-start.7) | collective-permute-done | bytes 32800 | tf_op jit(solution)/shard_map/ppermute | solution.py:351
  114.7 0.0 collective-permute-done.8.ld
  114.7 0.0 collective-permute-done.5.eu
  114.7 0.0 collective-permute-done.6.ed
  114.7 0.1 shard_map.109
  114.8 0.3 collective-permute-start.10
  115.1 3.3 %collective-permute-start.11 = (bf16[2,272,256]{2,1,0:T(8,128)(2,1)S(1)}, bf16[2,272,256]{2,1,0:T(8,128)(2,1)S(1)}, u32[]{:S(2)}, u32[]{:S(2)}) collective-permute-start(bf16[2,272,256]{2,1,0:T(8,128)(2,1)S(1)} %get-tuple-element.67), channel_id=1, source_target_pairs={{0,14},{1,15},{2,0},{3,1},{4,2},{5,3},{6,4},{7,5},{8,6},{9,7},{10,... | collective-permute-start | bytes 835592 | tf_op jit(solution)/shard_map/ppermute | solution.py:351
  118.4 0.6 collective-permute-start.4
  119.0 2.9 %collective-permute-start.9 = (bf16[3,64,256]{2,1,0:T(8,128)(2,1)S(1)}, bf16[3,64,256]{2,1,0:T(8,128)(2,1)S(1)}, u32[]{:S(2)}, u32[]{:S(2)}) collective-permute-start(bf16[3,64,256]{2,1,0:T(8,128)(2,1)S(1)} %get-tuple-element.65), channel_id=1, source_target_pairs={{0,1},{1,0},{2,3},{3,2},{4,5},{5,4},{6,7},{7,6},{8,9},{9,8},{10,11... | collective-permute-start | bytes 294920 | tf_op jit(solution)/shard_map/ppermute | solution.py:351
  121.9 0.9 collective-permute-done.10.gu_ref
  122.8 0.0 collective-permute-done.11.gd_ref
  122.8 0.1 shard_map.110
  122.9 0.5 collective-permute-start.12
  123.5 3.8 %collective-permute-start.13 = (bf16[272,256]{1,0:T(8,128)(2,1)S(1)}, bf16[272,256]{1,0:T(8,128)(2,1)S(1)}, u32[]{:S(2)}, u32[]{:S(2)}) collective-permute-start(bf16[272,256]{1,0:T(8,128)(2,1)S(1)} %get-tuple-element.69), channel_id=1, source_target_pairs={{0,3},{1,2},{2,5},{3,4},{4,7},{5,6},{6,9},{7,8},{8,11},{9,10},{10,... | collective-permute-start | bytes 417800 | tf_op jit(solution)/shard_map/ppermute | solution.py:351
  127.3 1.2 collective-permute-start.14
  128.5 4.4 %collective-permute-done.9.nl_ref = bf16[3,64,256]{2,1,0:T(8,128)(2,1)S(1)} collective-permute-done((bf16[3,64,256]{2,1,0:T(8,128)(2,1)S(1)}, bf16[3,64,256]{2,1,0:T(8,128)(2,1)S(1)}, u32[]{:S(2)}, u32[]{:S(2)}) %collective-permute-start.9) | collective-permute-done | bytes 98336 | tf_op jit(solution)/shard_map/ppermute | solution.py:351
  132.9 0.0 collective-permute-start.15
  132.9 0.0 collective-permute-done.4.ne_ref
  132.9 0.0 collective-permute-done.12.us
  132.9 0.0 collective-permute-done.13.uc
  132.9 0.0 collective-permute-done.14.ds
  132.9 7.4 %collective-permute-done.15.dc = bf16[272,256]{1,0:T(8,128)(2,1)S(1)} collective-permute-done((bf16[272,256]{1,0:T(8,128)(2,1)S(1)}, bf16[272,256]{1,0:T(8,128)(2,1)S(1)}, u32[]{:S(2)}, u32[]{:S(2)}) %collective-permute-start.15) | collective-permute-done | bytes 139296 | tf_op jit(solution)/shard_map/ppermute | solution.py:351
  140.3 0.2 shard_map.111
  140.5 0.1 collective-permute-start.16
  140.6 3.2 %collective-permute-start.17 = (bf16[272,256]{1,0:T(8,128)(2,1)S(1)}, bf16[272,256]{1,0:T(8,128)(2,1)S(1)}, u32[]{:S(2)}, u32[]{:S(2)}) collective-permute-start(bf16[272,256]{1,0:T(8,128)(2,1)S(1)} %get-tuple-element.73), channel_id=1, source_target_pairs={{0,14},{1,15},{2,0},{3,1},{4,2},{5,3},{6,4},{7,5},{8,6},{9,7},{10,... | collective-permute-start | bytes 417800 | tf_op jit(solution)/shard_map/ppermute | solution.py:351
  143.8 1.4 shard_map.108
  145.2 1.6 %collective-permute-done.16.gu_ref = bf16[272,256]{1,0:T(8,128)(2,1)S(1)} collective-permute-done((bf16[272,256]{1,0:T(8,128)(2,1)S(1)}, bf16[272,256]{1,0:T(8,128)(2,1)S(1)}, u32[]{:S(2)}, u32[]{:S(2)}) %collective-permute-start.16) | collective-permute-done | bytes 139296 | tf_op jit(solution)/shard_map/ppermute | solution.py:351
  146.8 0.0 collective-permute-done.17.gd_ref
  146.8 0.8 shard_map.112
  (6 shorter events, 0.0 us)
Async XLA Ops:
  0.6 6.1 %copy-start = (bf16[1,4,128,1024]{3,2,1,0:T(8,128)(2,1)S(1)}, bf16[1,4,128,1024]{3,2,1,0:T(8,128)(2,1)}, u32[]{:S(2)}) copy-start(bf16[1,4,128,1024]{3,2,1,0:T(8,128)(2,1)} %param.6) | copy-start | bytes 3145732
  0.6 6.1 %copy-start.2 = (bf16[1024,256]{1,0:T(8,128)(2,1)S(1)}, bf16[1024,256]{1,0:T(8,128)(2,1)}, u32[]{:S(2)}) copy-start(bf16[1024,256]{1,0:T(8,128)(2,1)} %wr_ref.3) | copy-start | bytes 1572868
  0.7 25.8 %all-to-all-start.1 = ((bf16[16,32,1024]{2,1,0:T(8,128)(2,1)}), bf16[16,32,1024]{2,1,0:T(8,128)(2,1)}, u32[]{:S(2)}, u32[]{:S(2)}) async-start(bf16[16,32,1024]{2,1,0:T(8,128)(2,1)} %bitcast.22), calls=%async_computation.1 | async-start | bytes 2097152 | tf_op jit(solution)/shard_map/all_to_all | solution.py:393
  6.7 7.9 %copy-start.1 = (bf16[3,3,256,256]{3,2,1,0:T(8,128)(2,1)S(1)}, bf16[3,3,256,256]{3,2,1,0:T(8,128)(2,1)}, u32[]{:S(2)}) copy-start(bf16[3,3,256,256]{3,2,1,0:T(8,128)(2,1)} %ws_ref.7) | copy-start | bytes 3538948
  6.8 7.9 %copy-start.3 = (bf16[256,1024]{1,0:T(8,128)(2,1)S(1)}, bf16[256,1024]{1,0:T(8,128)(2,1)}, u32[]{:S(2)}) copy-start(bf16[256,1024]{1,0:T(8,128)(2,1)} %we_ref.5) | copy-start | bytes 1572868
  7.1 16.7 %collective-permute-start = (bf16[128,256]{1,0:T(8,128)(2,1)S(1)}, bf16[128,256]{1,0:T(8,128)(2,1)S(1)}, u32[]{:S(2)}, u32[]{:S(2)}) collective-permute-start(bf16[128,256]{1,0:T(8,128)(2,1)S(1)} %get-tuple-element.42.last_ref), channel_id=1, source_target_pairs={{0,1},{1,2},{2,3},{3,4},{4,5},{5,6},{6,7},{7,8},{8,9},{9,10},{10,1... | collective-permute-start | bytes 196616 | tf_op jit(solution)/shard_map/ppermute | solution.py:337
  11.9 11.9 %collective-permute-start.1 = (bf16[128,256]{1,0:T(8,128)(2,1)S(1)}, bf16[128,256]{1,0:T(8,128)(2,1)S(1)}, u32[]{:S(2)}, u32[]{:S(2)}) collective-permute-start(bf16[128,256]{1,0:T(8,128)(2,1)S(1)} %get-tuple-element.41.first_ref), channel_id=1, source_target_pairs={{1,0},{2,1},{3,2},{4,3},{5,4},{6,5},{7,6},{8,7},{9,8},{10,9},{11,1... | collective-permute-start | bytes 196616 | tf_op jit(solution)/shard_map/ppermute | solution.py:337
  24.7 1.0 copy-start.4
  25.6 0.8 copy-start.5
  26.4 21.2 %copy-start.7 = (s32[2,16]{1,0:T(2,128)S(1)}, s32[2,16]{1,0:T(2,128)}, u32[]{:S(2)}) copy-start(s32[2,16]{1,0:T(2,128)} %parts_ref.3) | copy-start | bytes 388
  75.1 26.9 %copy-start.6 = (bf16[6,128,256]{2,1,0:T(8,128)(2,1)S(1)}, bf16[6,128,256]{2,1,0:T(8,128)(2,1)}, u32[]{:S(2)}) copy-start(bf16[6,128,256]{2,1,0:T(8,128)(2,1)} %copy-done.5) | copy-start | bytes 1179652
  94.6 12.2 %collective-permute-start.2 = (bf16[128,256]{1,0:T(8,128)(2,1)S(1)}, bf16[128,256]{1,0:T(8,128)(2,1)S(1)}, u32[]{:S(2)}, u32[]{:S(2)}) collective-permute-start(bf16[128,256]{1,0:T(8,128)(2,1)S(1)} %get-tuple-element.55), channel_id=1, source_target_pairs={{0,1},{1,2},{2,3},{3,4},{4,5},{5,6},{6,7},{7,8},{8,9},{9,10},{10,1... | collective-permute-start | bytes 196616 | tf_op jit(solution)/shard_map/ppermute | solution.py:337
  99.8 8.6 %collective-permute-start.3 = (bf16[128,256]{1,0:T(8,128)(2,1)S(1)}, bf16[128,256]{1,0:T(8,128)(2,1)S(1)}, u32[]{:S(2)}, u32[]{:S(2)}) collective-permute-start(bf16[128,256]{1,0:T(8,128)(2,1)S(1)} %get-tuple-element.56), channel_id=1, source_target_pairs={{1,0},{2,1},{3,2},{4,3},{5,4},{6,5},{7,6},{8,7},{9,8},{10,9},{11,1... | collective-permute-start | bytes 196616 | tf_op jit(solution)/shard_map/ppermute | solution.py:337
  103.5 11.2 %collective-permute-start.5 = (bf16[208,256]{1,0:T(8,128)(2,1)S(1)}, bf16[208,256]{1,0:T(8,128)(2,1)S(1)}, u32[]{:S(2)}, u32[]{:S(2)}) collective-permute-start(bf16[208,256]{1,0:T(8,128)(2,1)S(1)} %get-tuple-element.61), channel_id=1, source_target_pairs={{0,2},{1,3},{2,4},{3,5},{4,6},{5,7},{6,8},{7,9},{8,10},{9,11},{10,... | collective-permute-start | bytes 319496 | tf_op jit(solution)/shard_map/ppermute | solution.py:351
  104.4 10.3 %collective-permute-start.6 = (bf16[208,256]{1,0:T(8,128)(2,1)S(1)}, bf16[208,256]{1,0:T(8,128)(2,1)S(1)}, u32[]{:S(2)}, u32[]{:S(2)}) collective-permute-start(bf16[208,256]{1,0:T(8,128)(2,1)S(1)} %get-tuple-element.62), channel_id=1, source_target_pairs={{0,14},{1,15},{2,0},{3,1},{4,2},{5,3},{6,4},{7,5},{8,6},{9,7},{10,... | collective-permute-start | bytes 319496 | tf_op jit(solution)/shard_map/ppermute | solution.py:351
  109.5 5.2 %collective-permute-start.7 = (bf16[64,256]{1,0:T(8,128)(2,1)S(1)}, bf16[64,256]{1,0:T(8,128)(2,1)S(1)}, u32[]{:S(2)}, u32[]{:S(2)}) collective-permute-start(bf16[64,256]{1,0:T(8,128)(2,1)S(1)} %get-tuple-element.63), channel_id=1, source_target_pairs={{0,2},{1,3},{2,4},{3,5},{4,6},{5,7},{6,8},{7,9},{8,10},{9,11},{10,... | collective-permute-start | bytes 98312 | tf_op jit(solution)/shard_map/ppermute | solution.py:351
  109.9 4.7 %collective-permute-start.8 = (bf16[64,256]{1,0:T(8,128)(2,1)S(1)}, bf16[64,256]{1,0:T(8,128)(2,1)S(1)}, u32[]{:S(2)}, u32[]{:S(2)}) collective-permute-start(bf16[64,256]{1,0:T(8,128)(2,1)S(1)} %get-tuple-element.64), channel_id=1, source_target_pairs={{0,14},{1,15},{2,0},{3,1},{4,2},{5,3},{6,4},{7,5},{8,6},{9,7},{10,... | collective-permute-start | bytes 98312 | tf_op jit(solution)/shard_map/ppermute | solution.py:351
  114.8 8.0 %collective-permute-start.10 = (bf16[2,272,256]{2,1,0:T(8,128)(2,1)S(1)}, bf16[2,272,256]{2,1,0:T(8,128)(2,1)S(1)}, u32[]{:S(2)}, u32[]{:S(2)}) collective-permute-start(bf16[2,272,256]{2,1,0:T(8,128)(2,1)S(1)} %get-tuple-element.66), channel_id=1, source_target_pairs={{0,2},{1,3},{2,4},{3,5},{4,6},{5,7},{6,8},{7,9},{8,10},{9,11},{10,... | collective-permute-start | bytes 835592 | tf_op jit(solution)/shard_map/ppermute | solution.py:351
  115.1 7.7 %collective-permute-start.11 = (bf16[2,272,256]{2,1,0:T(8,128)(2,1)S(1)}, bf16[2,272,256]{2,1,0:T(8,128)(2,1)S(1)}, u32[]{:S(2)}, u32[]{:S(2)}) collective-permute-start(bf16[2,272,256]{2,1,0:T(8,128)(2,1)S(1)} %get-tuple-element.67), channel_id=1, source_target_pairs={{0,14},{1,15},{2,0},{3,1},{4,2},{5,3},{6,4},{7,5},{8,6},{9,7},{10,... | collective-permute-start | bytes 835592 | tf_op jit(solution)/shard_map/ppermute | solution.py:351
  118.4 14.5 %collective-permute-start.4 = (bf16[3,208,256]{2,1,0:T(8,128)(2,1)S(1)}, bf16[3,208,256]{2,1,0:T(8,128)(2,1)S(1)}, u32[]{:S(2)}, u32[]{:S(2)}) collective-permute-start(bf16[3,208,256]{2,1,0:T(8,128)(2,1)S(1)} %get-tuple-element.60), channel_id=1, source_target_pairs={{0,1},{1,0},{2,3},{3,2},{4,5},{5,4},{6,7},{7,6},{8,9},{9,8},{10,11... | collective-permute-start | bytes 958472 | tf_op jit(solution)/shard_map/ppermute | solution.py:351
  119.0 13.9 %collective-permute-start.9 = (bf16[3,64,256]{2,1,0:T(8,128)(2,1)S(1)}, bf16[3,64,256]{2,1,0:T(8,128)(2,1)S(1)}, u32[]{:S(2)}, u32[]{:S(2)}) collective-permute-start(bf16[3,64,256]{2,1,0:T(8,128)(2,1)S(1)} %get-tuple-element.65), channel_id=1, source_target_pairs={{0,1},{1,0},{2,3},{3,2},{4,5},{5,4},{6,7},{7,6},{8,9},{9,8},{10,11... | collective-permute-start | bytes 294920 | tf_op jit(solution)/shard_map/ppermute | solution.py:351
  122.9 9.9 %collective-permute-start.12 = (bf16[272,256]{1,0:T(8,128)(2,1)S(1)}, bf16[272,256]{1,0:T(8,128)(2,1)S(1)}, u32[]{:S(2)}, u32[]{:S(2)}) collective-permute-start(bf16[272,256]{1,0:T(8,128)(2,1)S(1)} %get-tuple-element.68), channel_id=1, source_target_pairs={{0,2},{1,3},{2,4},{3,5},{4,6},{5,7},{6,8},{7,9},{8,10},{9,11},{10,... | collective-permute-start | bytes 417800 | tf_op jit(solution)/shard_map/ppermute | solution.py:351
  123.5 9.4 %collective-permute-start.13 = (bf16[272,256]{1,0:T(8,128)(2,1)S(1)}, bf16[272,256]{1,0:T(8,128)(2,1)S(1)}, u32[]{:S(2)}, u32[]{:S(2)}) collective-permute-start(bf16[272,256]{1,0:T(8,128)(2,1)S(1)} %get-tuple-element.69), channel_id=1, source_target_pairs={{0,3},{1,2},{2,5},{3,4},{4,7},{5,6},{6,9},{7,8},{8,11},{9,10},{10,... | collective-permute-start | bytes 417800 | tf_op jit(solution)/shard_map/ppermute | solution.py:351
  127.3 5.6 %collective-permute-start.14 = (bf16[272,256]{1,0:T(8,128)(2,1)S(1)}, bf16[272,256]{1,0:T(8,128)(2,1)S(1)}, u32[]{:S(2)}, u32[]{:S(2)}) collective-permute-start(bf16[272,256]{1,0:T(8,128)(2,1)S(1)} %get-tuple-element.70), channel_id=1, source_target_pairs={{0,14},{1,15},{2,0},{3,1},{4,2},{5,3},{6,4},{7,5},{8,6},{9,7},{10,... | collective-permute-start | bytes 417800 | tf_op jit(solution)/shard_map/ppermute | solution.py:351
  132.9 7.5 %collective-permute-start.15 = (bf16[272,256]{1,0:T(8,128)(2,1)S(1)}, bf16[272,256]{1,0:T(8,128)(2,1)S(1)}, u32[]{:S(2)}, u32[]{:S(2)}) collective-permute-start(bf16[272,256]{1,0:T(8,128)(2,1)S(1)} %get-tuple-element.71), channel_id=1, source_target_pairs={{0,15},{1,14},{2,1},{3,0},{4,3},{5,2},{6,5},{7,4},{8,7},{9,6},{10,... | collective-permute-start | bytes 417800 | tf_op jit(solution)/shard_map/ppermute | solution.py:351
  140.5 6.3 %collective-permute-start.16 = (bf16[272,256]{1,0:T(8,128)(2,1)S(1)}, bf16[272,256]{1,0:T(8,128)(2,1)S(1)}, u32[]{:S(2)}, u32[]{:S(2)}) collective-permute-start(bf16[272,256]{1,0:T(8,128)(2,1)S(1)} %get-tuple-element.72), channel_id=1, source_target_pairs={{0,2},{1,3},{2,4},{3,5},{4,6},{5,7},{6,8},{7,9},{8,10},{9,11},{10,... | collective-permute-start | bytes 417800 | tf_op jit(solution)/shard_map/ppermute | solution.py:351
  140.6 6.3 %collective-permute-start.17 = (bf16[272,256]{1,0:T(8,128)(2,1)S(1)}, bf16[272,256]{1,0:T(8,128)(2,1)S(1)}, u32[]{:S(2)}, u32[]{:S(2)}) collective-permute-start(bf16[272,256]{1,0:T(8,128)(2,1)S(1)} %get-tuple-element.73), channel_id=1, source_target_pairs={{0,14},{1,15},{2,0},{3,1},{4,2},{5,3},{6,4},{7,5},{8,6},{9,7},{10,... | collective-permute-start | bytes 417800 | tf_op jit(solution)/shard_map/ppermute | solution.py:351

commit v6 on v5

--- a/solution.py
+++ b/solution.py
@@ -181,7 +181,7 @@
 
 def window_kernel(
     place_ref, g_ref, h2_ref, g2_ref, hp_ref, ws_ref,
-    out_ref, g1_ref, up_ref, down_ref, near_ref,
+    out_ref, g1_ref, up_ref, down_ref,
 ):
     rows, cols, mid = g2_ref.shape
     chunks = out_ref.shape[0]
@@ -201,7 +201,6 @@
             grad = dot(moved[b], source, FIRST_DOT).astype(BF16)
             out_ref[:, start : start + width] = grad.reshape(chunks, width, mid)
     farthest(place_ref, out_ref, up_ref, down_ref)
-    near_others(place_ref, out_ref, near_ref)
     sums = taps([flat(g2_ref[2 - a : rows - a]) for a in range(3)], ws_ref, LAST_DOT)
     total = narrowed(sums, cols)
     g1_ref[...] = jnp.where(flat(hp_ref[2:rows]) > 0, total, 0.0).astype(BF16)
@@ -236,11 +235,14 @@
     out_ref[0, 1 : rows - 1] = inner.reshape(rows - 2, cols, -1)
 
 
-def near_others(place_ref, local_ref, out_ref):
-    depth = local_ref.shape[0] // 2
+def near_others(place_ref, early_ref, late_ref, out_ref):
+    rows = early_ref.shape[1]
+    depth = early_ref.shape[0] // 2
     z, half = place_ref[0] // 2, place_ref[0] % 2
     for index in range(3):
-        out_ref[index] = local_ref[2 * ((z + index - 1 + depth) % depth) + 1 - half]
+        block = 2 * ((z + index - 1 + depth) % depth) + 1 - half
+        out_ref[index, :rows] = early_ref[block]
+        out_ref[index, rows:] = late_ref[block]
 
 
 def join_kernel(
@@ -248,7 +250,7 @@
 ):
     rows = early_ref.shape[1]
     depth = early_ref.shape[0] // 2
-    near_others(place_ref, late_ref, near_ref)
+    near_others(place_ref, early_ref, late_ref, near_ref)
     for way, (sign, got, out_ref) in enumerate(((1, (eu, lu), up_ref), (-1, (ed, ld), down_ref))):
         block = 2 * ((place_ref[0] // 2 + sign * offset + depth) % depth)
         for side in range(2):
@@ -274,20 +276,21 @@
             target[rows:] = late.astype(BF16)
 
 
-def own_terms(place_ref, early_ref, late_ref, ne_ref, nl_ref, offset):
+def own_terms(place_ref, early_ref, late_ref, near_ref, offset):
+    rows = early_ref.shape[1]
     depth = early_ref.shape[0] // 2
     z, half = place_ref[0] // 2, place_ref[0] % 2
     block = 2 * ((z + offset + depth) % depth) + half
-    early = early_ref[block].astype(F32) + ne_ref[1 + offset].astype(F32)
-    return early, late_ref[block].astype(F32) + nl_ref[1 + offset].astype(F32)
+    early = early_ref[block].astype(F32) + near_ref[1 + offset, :rows].astype(F32)
+    return early, late_ref[block].astype(F32) + near_ref[1 + offset, rows:].astype(F32)
 
 
 def side_kernel(
-    place_ref, early_ref, late_ref, ne_ref, nl_ref, us, uc, ds, dc, up_ref, down_ref
+    place_ref, early_ref, late_ref, near_ref, us, uc, ds, dc, up_ref, down_ref
 ):
     rows = early_ref.shape[1]
     for offset, got, out_ref in ((1, (us, uc), up_ref), (-1, (ds, dc), down_ref)):
-        early, late = own_terms(place_ref, early_ref, late_ref, ne_ref, nl_ref, offset)
+        early, late = own_terms(place_ref, early_ref, late_ref, near_ref, offset)
         for ref in got:
             early = early + ref[:rows].astype(F32)
             late = late + ref[rows:].astype(F32)
@@ -296,11 +299,11 @@
 
 
 def last_kernel(
-    place_ref, early_ref, late_ref, ne_ref, nl_ref, gu_ref, gd_ref,
+    place_ref, early_ref, late_ref, near_ref, gu_ref, gd_ref,
     expand_ref, spatial_ref, reduce_ref,
 ):
     rows = early_ref.shape[1]
-    early, late = own_terms(place_ref, early_ref, late_ref, ne_ref, nl_ref, 0)
+    early, late = own_terms(place_ref, early_ref, late_ref, near_ref, 0)
     for ref in (gu_ref, gd_ref):
         early = early + ref[:rows].astype(F32)
         late = late + ref[rows:].astype(F32)
@@ -337,7 +340,7 @@
     return lax.ppermute(last, "space", up), lax.ppermute(first, "space", down)
 
 
-def scattered(early, late, early_sends, late_sends, near_early, place):
+def scattered(early, late, early_sends, late_sends, place):
     peers = lax.axis_size("space")
     far = peers // 4
     ups = [(i, (i + 2) % peers) for i in range(peers)]
@@ -353,14 +356,14 @@
     def moved(up, down):
         return sent(up, ups), sent(down, downs)
 
-    got = moved(*early_sends)
-    near_early = sent(near_early, swap)
-    got = got + moved(*late_sends)
-    near = ((3, *late.shape[1:]), BF16)
+    got = moved(*early_sends) + moved(*late_sends)
+    near = ((3, rows, mid), BF16)
     join = functools.partial(join_kernel, far - 1)
-    up, down, near_late = call(join, pair + [near], rows * mid, smem=1)(place, early, late, *got)
+    up, down, near = call(join, pair + [near], rows * mid, smem=1)(
+        place, early, late, *got
+    )
     up, down = moved(up, down)
-    near_late = sent(near_late, swap)
+    near = sent(near, swap)
     for step in range(3, far):
         split = step == far - 1
         kernel = functools.partial(pass_kernel, far + 1 - step, split)
@@ -371,7 +374,7 @@
     uc = sent(got[1], [(i, j ^ 1) for i, j in ups])
     dc = sent(got[3], [(i, j ^ 1) for i, j in downs])
     us, ds = moved(got[0], got[2])
-    terms = (place, early, late, near_early, near_late)
+    terms = (place, early, late, near)
     up, down = call(side_kernel, [side] * 2, rows * mid, smem=1)(*terms, us, uc, ds, dc)
     return *terms, *moved(up, down)
 
@@ -440,11 +443,10 @@
     )(grads, h_two, w_expand)
     over, under = exchanged(first, last)
     part, width = channels // n_space, mid // n_space
-    early, g1_in, *early_sends, near_early = call(
+    early, g1_in, *early_sends = call(
         window_kernel,
         [((n_space, part + 9 * width, mid), BF16), ((inside, mid), BF16)]
-        + [((part + 9 * width, mid), BF16)] * 2
-        + [((3, part + 9 * width, mid), BF16)],
+        + [((part + 9 * width, mid), BF16)] * 2,
         70 * mac,
         smem=1,
     )(place, grads, h_two, g_two, h_pad, w_spatial)
@@ -462,7 +464,7 @@
         [((part, mid), F32), ((3, 3, width, mid), F32), ((part, mid), F32)],
         mac,
         smem=1,
-    )(*scattered(early, late, early_sends, late_sends, near_early, place))
+    )(*scattered(early, late, early_sends, late_sends, place))
     return (
         loss[0, 0],
         g_images,

time: 148 us -> 145 us (0.980)
  waiting for transfers between devices: 25.9 us -> 22.4 us
    ppermute x14 -> x13, waiting for transfers between devices: 16.2 us -> 13.5 us  [sent(): return lax.ppermute(value, 'space', path)]
    ppermute x14 -> x13, starting transfers between devices: 22.6 us -> 22 us  [sent(): return lax.ppermute(value, 'space', path)]
  transfers between devices with their start and end apart: 19 -> 18, of which waited for: 7 -> 8; matrix products, arithmetic and copies ran while one was open for 0% -> 0% of each run, Pallas kernels for 4% -> 4%
where the time goes in v6:
time: 145 us; the launch traced here: 144 us
  blocking collectives  63.9 us (44%)
  starting transfers between devices  43.8 us (30%)
  waiting for transfers between devices  22.4 us (15%)
  Pallas kernels  11.7 us (8%)
  local copies, waits for them, and re-layouts  1.74 us (1%)
    all_to_all x1, blocking collectives, step(): message = lax.all_to_all(message, ('dp', 'space'), 0, 0, tiled=True)  23.6 us
    ppermute x13, starting transfers between devices, sent(): return lax.ppermute(value, 'space', path)  22 us
    all_to_all x1, blocking collectives, step(): s_all = lax.all_to_all(s_all, 'dp', 0, 0, tiled=True)  21.2 us
    all_to_all x1, blocking collectives, step(): grads = lax.all_to_all(grads, 'dp', 0, 0, tiled=True)  19.1 us
    ppermute x4, starting transfers between devices, exchanged(): return (lax.ppermute(last, 'space', up), lax.ppermute(first, 'space', down))  15.7 us
    ppermute x13, waiting for transfers between devices, sent(): return lax.ppermute(value, 'space', path)  13.5 us
    pallas_call x12, Pallas kernels, run(): pl.pallas_call(kernel, out_shape=[jax.ShapeDtypeStruct(s, d) for s, d in...  11.4 us
    ppermute x4, waiting for transfers between devices, exchanged(): return (lax.ppermute(last, 'space', up), lax.ppermute(first, 'space', down))  8.81 us
  transfers between devices with their start and end apart: 18, of which 8 were waited for; matrix products, arithmetic and copies ran while one was open for 0% of the time, Pallas kernels for 4%

profile of v6, /device:TPU:6, one launch (start us, length us, event | category | flops | bytes accessed | tf_op | source)
XLA Modules:
  0.0 144.3 jit_solution(188312365475802538)
XLA Ops:
  0.6 0.0 copy-start.2
  0.6 0.0 copy-start
  0.7 6.1 %all-to-all-start.1 = ((bf16[16,32,1024]{2,1,0:T(8,128)(2,1)}), bf16[16,32,1024]{2,1,0:T(8,128)(2,1)}, u32[]{:S(2)}, u32[]{:S(2)}) async-start(bf16[16,32,1024]{2,1,0:T(8,128)(2,1)} %bitcast.22), calls=%async_computation.1 | async-start | bytes 2097152 | tf_op jit(solution)/shard_map/all_to_all | solution.py:396
  6.8 0.0 copy-start.3
  6.8 0.0 copy-done.2
  6.8 0.0 copy-done
  6.8 0.3 edge.1
  7.1 3.8 %collective-permute-start.1 = (bf16[128,256]{1,0:T(8,128)(2,1)S(1)}, bf16[128,256]{1,0:T(8,128)(2,1)S(1)}, u32[]{:S(2)}, u32[]{:S(2)}) collective-permute-start(bf16[128,256]{1,0:T(8,128)(2,1)S(1)} %get-tuple-element.40.first_ref), channel_id=1, source_target_pairs={{1,0},{2,1},{3,2},{4,3},{5,4},{6,5},{7,6},{8,7},{9,8},{10,9},{11,1... | collective-permute-start | bytes 196616 | tf_op jit(solution)/shard_map/ppermute | solution.py:340
  10.9 4.6 %collective-permute-start = (bf16[128,256]{1,0:T(8,128)(2,1)S(1)}, bf16[128,256]{1,0:T(8,128)(2,1)S(1)}, u32[]{:S(2)}, u32[]{:S(2)}) collective-permute-start(bf16[128,256]{1,0:T(8,128)(2,1)S(1)} %get-tuple-element.41.last_ref), channel_id=1, source_target_pairs={{0,1},{1,2},{2,3},{3,4},{4,5},{5,6},{6,7},{7,8},{8,9},{9,10},{10,1... | collective-permute-start | bytes 196616 | tf_op jit(solution)/shard_map/ppermute | solution.py:340
  15.5 0.0 copy-done.1
  15.5 0.0 copy-done.3
  15.5 1.1 shard_map.101
  16.6 3.5 %collective-permute-done.1.below_ref = bf16[128,256]{1,0:T(8,128)(2,1)S(1)} collective-permute-done((bf16[128,256]{1,0:T(8,128)(2,1)S(1)}, bf16[128,256]{1,0:T(8,128)(2,1)S(1)}, u32[]{:S(2)}, u32[]{:S(2)}) %collective-permute-start.1) | collective-permute-done | bytes 65568 | tf_op jit(solution)/shard_map/ppermute | solution.py:340
  20.1 3.6 %collective-permute-done.above_ref = bf16[128,256]{1,0:T(8,128)(2,1)S(1)} collective-permute-done((bf16[128,256]{1,0:T(8,128)(2,1)S(1)}, bf16[128,256]{1,0:T(8,128)(2,1)S(1)}, u32[]{:S(2)}, u32[]{:S(2)}) %collective-permute-start) | collective-permute-done | bytes 65568 | tf_op jit(solution)/shard_map/ppermute | solution.py:340
  23.8 0.9 shard_map.102
  24.7 0.0 copy-start.4
  24.7 1.0 copy-done.4
  25.6 0.7 copy-done.5
  26.4 0.0 all-to-all-done.1.t_ref
  26.4 21.2 %all_to_all.26.s_ref = bf16[16,32,1024]{2,1,0:T(8,128)(2,1)S(1)} all-to-all(bf16[16,32,1024]{2,1,0:T(8,128)(2,1)} %copy-done.4), channel_id=1, replica_groups=mesh['dp'=16,'space'=16] {'dp'}, dimensions={0} | all-to-all | bytes 2097152 | tf_op jit(solution)/shard_map/all_to_all | solution.py:430
  47.6 2.1 %shard_map.103 = f32[256,128]{1,0:T(8,128)S(1)} custom-call(s32[2,16]{1,0:T(2,128)S(1)} %copy-done.7, bf16[16,32,1024]{2,1,0:T(8,128)(2,1)S(1)} %all_to_all.26.s_ref, bf16[16,32,1024]{2,1,0:T(8,128)(2,1)} %all-to-all-done.1.t_ref), custom_call_target="tpu_custom_call" | custom-call | flops 536870912 | bytes 2097280 | tf_op jit(solution)/shard_map/pallas_call | solution.py:323
  49.7 23.6 %all_to_all.27 = f32[256,1,128]{2,1,0:T(1,128)S(1)} all-to-all(f32[256,1,128]{2,1,0:T(1,128)S(1)} %bitcast.20), channel_id=1, replica_groups=mesh['dp'=16,'space'=16] {'dp','space'}, dimensions={0} | all-to-all | bytes 262144 | tf_op jit(solution)/shard_map/all_to_all | solution.py:433
  73.3 1.8 %shard_map.104 = (bf16[16,32,1024]{2,1,0:T(8,128)(2,1)S(1)}, f32[1,1]{1,0:T(1,128)}) custom-call(s32[2,16]{1,0:T(2,128)S(1)} %copy-done.7, f32[256,128]{1,0:T(8,128)S(1)} %bitcast.21, bf16[16,32,1024]{2,1,0:T(8,128)(2,1)S(1)} %all_to_all.26.s_ref), custom_call_target="tpu_custom_call" | custom-call | flops 16777216 | bytes 1179776 | tf_op jit(solution)/shard_map/pallas_call | solution.py:323
  75.1 0.0 copy-start.6
  75.1 19.1 %all_to_all.28.g_ref = bf16[16,32,1024]{2,1,0:T(8,128)(2,1)S(1)} all-to-all(bf16[16,32,1024]{2,1,0:T(8,128)(2,1)S(1)} %get-tuple-element.48), channel_id=1, replica_groups=mesh['dp'=16,'space'=16] {'dp'}, dimensions={0} | all-to-all | bytes 2097152 | tf_op jit(solution)/shard_map/all_to_all | solution.py:440
  94.1 0.5 shard_map.105
  94.6 5.2 %collective-permute-start.2 = (bf16[128,256]{1,0:T(8,128)(2,1)S(1)}, bf16[128,256]{1,0:T(8,128)(2,1)S(1)}, u32[]{:S(2)}, u32[]{:S(2)}) collective-permute-start(bf16[128,256]{1,0:T(8,128)(2,1)S(1)} %get-tuple-element.54), channel_id=1, source_target_pairs={{0,1},{1,2},{2,3},{3,4},{4,5},{5,6},{6,7},{7,8},{8,9},{9,10},{10,1... | collective-permute-start | bytes 196616 | tf_op jit(solution)/shard_map/ppermute | solution.py:340
  99.8 2.2 %collective-permute-start.3 = (bf16[128,256]{1,0:T(8,128)(2,1)S(1)}, bf16[128,256]{1,0:T(8,128)(2,1)S(1)}, u32[]{:S(2)}, u32[]{:S(2)}) collective-permute-start(bf16[128,256]{1,0:T(8,128)(2,1)S(1)} %get-tuple-element.55), channel_id=1, source_target_pairs={{1,0},{2,1},{3,2},{4,3},{5,4},{6,5},{7,6},{8,7},{9,8},{10,9},{11,1... | collective-permute-start | bytes 196616 | tf_op jit(solution)/shard_map/ppermute | solution.py:340
  102.0 0.0 copy-done.6
  102.0 1.4 shard_map.106
  103.4 0.9 collective-permute-start.4
  104.3 2.4 %collective-permute-start.5 = (bf16[208,256]{1,0:T(8,128)(2,1)S(1)}, bf16[208,256]{1,0:T(8,128)(2,1)S(1)}, u32[]{:S(2)}, u32[]{:S(2)}) collective-permute-start(bf16[208,256]{1,0:T(8,128)(2,1)S(1)} %get-tuple-element.60), channel_id=1, source_target_pairs={{0,14},{1,15},{2,0},{3,1},{4,2},{5,3},{6,4},{7,5},{8,6},{9,7},{10,... | collective-permute-start | bytes 319496 | tf_op jit(solution)/shard_map/ppermute | solution.py:354
  106.8 0.0 collective-permute-done.2.above_ref
  106.8 1.6 %collective-permute-done.3.below_ref = bf16[128,256]{1,0:T(8,128)(2,1)S(1)} collective-permute-done((bf16[128,256]{1,0:T(8,128)(2,1)S(1)}, bf16[128,256]{1,0:T(8,128)(2,1)S(1)}, u32[]{:S(2)}, u32[]{:S(2)}) %collective-permute-start.3) | collective-permute-done | bytes 65568 | tf_op jit(solution)/shard_map/ppermute | solution.py:340
  108.4 1.1 shard_map.107
  109.5 0.4 collective-permute-start.6
  109.9 2.9 %collective-permute-start.7 = (bf16[64,256]{1,0:T(8,128)(2,1)S(1)}, bf16[64,256]{1,0:T(8,128)(2,1)S(1)}, u32[]{:S(2)}, u32[]{:S(2)}) collective-permute-start(bf16[64,256]{1,0:T(8,128)(2,1)S(1)} %get-tuple-element.62), channel_id=1, source_target_pairs={{0,14},{1,15},{2,0},{3,1},{4,2},{5,3},{6,4},{7,5},{8,6},{9,7},{10,... | collective-permute-start | bytes 98312 | tf_op jit(solution)/shard_map/ppermute | solution.py:354
  112.8 1.9 %collective-permute-done.6.lu = bf16[64,256]{1,0:T(8,128)(2,1)S(1)} collective-permute-done((bf16[64,256]{1,0:T(8,128)(2,1)S(1)}, bf16[64,256]{1,0:T(8,128)(2,1)S(1)}, u32[]{:S(2)}, u32[]{:S(2)}) %collective-permute-start.6) | collective-permute-done | bytes 32800 | tf_op jit(solution)/shard_map/ppermute | solution.py:354
  114.7 0.0 collective-permute-done.7.ld
  114.7 0.0 collective-permute-done.4.eu
  114.7 0.0 collective-permute-done.5.ed
  114.7 0.1 shard_map.109
  114.8 0.3 collective-permute-start.9
  115.1 3.3 %collective-permute-start.10 = (bf16[2,272,256]{2,1,0:T(8,128)(2,1)S(1)}, bf16[2,272,256]{2,1,0:T(8,128)(2,1)S(1)}, u32[]{:S(2)}, u32[]{:S(2)}) collective-permute-start(bf16[2,272,256]{2,1,0:T(8,128)(2,1)S(1)} %get-tuple-element.65), channel_id=1, source_target_pairs={{0,14},{1,15},{2,0},{3,1},{4,2},{5,3},{6,4},{7,5},{8,6},{9,7},{10,... | collective-permute-start | bytes 835592 | tf_op jit(solution)/shard_map/ppermute | solution.py:354
  118.4 0.6 collective-permute-start.8
  119.0 3.9 %collective-permute-done.9.gu_ref = bf16[2,272,256]{2,1,0:T(8,128)(2,1)S(1)} collective-permute-done((bf16[2,272,256]{2,1,0:T(8,128)(2,1)S(1)}, bf16[2,272,256]{2,1,0:T(8,128)(2,1)S(1)}, u32[]{:S(2)}, u32[]{:S(2)}) %collective-permute-start.9) | collective-permute-done | bytes 278560 | tf_op jit(solution)/shard_map/ppermute | solution.py:354
  122.8 0.0 collective-permute-done.10.gd_ref
  122.8 0.1 shard_map.110
  123.0 0.5 collective-permute-start.11
  123.5 3.8 %collective-permute-start.12 = (bf16[272,256]{1,0:T(8,128)(2,1)S(1)}, bf16[272,256]{1,0:T(8,128)(2,1)S(1)}, u32[]{:S(2)}, u32[]{:S(2)}) collective-permute-start(bf16[272,256]{1,0:T(8,128)(2,1)S(1)} %get-tuple-element.67), channel_id=1, source_target_pairs={{0,3},{1,2},{2,5},{3,4},{4,7},{5,6},{6,9},{7,8},{8,11},{9,10},{10,... | collective-permute-start | bytes 417800 | tf_op jit(solution)/shard_map/ppermute | solution.py:354
  127.2 1.2 collective-permute-start.13
  128.5 2.4 %collective-permute-start.14 = (bf16[272,256]{1,0:T(8,128)(2,1)S(1)}, bf16[272,256]{1,0:T(8,128)(2,1)S(1)}, u32[]{:S(2)}, u32[]{:S(2)}) collective-permute-start(bf16[272,256]{1,0:T(8,128)(2,1)S(1)} %get-tuple-element.69), channel_id=1, source_target_pairs={{0,15},{1,14},{2,1},{3,0},{4,3},{5,2},{6,5},{7,4},{8,7},{9,6},{10,... | collective-permute-start | bytes 417800 | tf_op jit(solution)/shard_map/ppermute | solution.py:354
  130.9 0.0 collective-permute-done.11.us
  130.9 1.5 %collective-permute-done.12.uc = bf16[272,256]{1,0:T(8,128)(2,1)S(1)} collective-permute-done((bf16[272,256]{1,0:T(8,128)(2,1)S(1)}, bf16[272,256]{1,0:T(8,128)(2,1)S(1)}, u32[]{:S(2)}, u32[]{:S(2)}) %collective-permute-start.12) | collective-permute-done | bytes 139296 | tf_op jit(solution)/shard_map/ppermute | solution.py:354
  132.4 0.0 collective-permute-done.13.ds
  132.4 4.7 %collective-permute-done.14.dc = bf16[272,256]{1,0:T(8,128)(2,1)S(1)} collective-permute-done((bf16[272,256]{1,0:T(8,128)(2,1)S(1)}, bf16[272,256]{1,0:T(8,128)(2,1)S(1)}, u32[]{:S(2)}, u32[]{:S(2)}) %collective-permute-start.14) | collective-permute-done | bytes 139296 | tf_op jit(solution)/shard_map/ppermute | solution.py:354
  137.1 0.0 collective-permute-done.8.near_ref
  137.1 0.2 shard_map.111
  137.2 0.2 collective-permute-start.15
  137.4 3.1 %collective-permute-start.16 = (bf16[272,256]{1,0:T(8,128)(2,1)S(1)}, bf16[272,256]{1,0:T(8,128)(2,1)S(1)}, u32[]{:S(2)}, u32[]{:S(2)}) collective-permute-start(bf16[272,256]{1,0:T(8,128)(2,1)S(1)} %get-tuple-element.71), channel_id=1, source_target_pairs={{0,14},{1,15},{2,0},{3,1},{4,2},{5,3},{6,4},{7,5},{8,6},{9,7},{10,... | collective-permute-start | bytes 417800 | tf_op jit(solution)/shard_map/ppermute | solution.py:354
  140.6 1.4 %shard_map.108 = bf16[1,4,128,1024]{3,2,1,0:T(8,128)(2,1)} custom-call(bf16[16,32,1024]{2,1,0:T(8,128)(2,1)S(1)} %all_to_all.28.g_ref, bf16[256,256]{1,0:T(8,128)(2,1)S(1)} %get-tuple-element.53.g1i_ref, bf16[256,256]{1,0:T(8,128)(2,1)S(1)} %get-tuple-element.56.g1o_ref, bf16[1024,256]{1,0:T(8,128)(2,1)S(1)} %copy-done.2), custom_call_target="tpu_custom_call" | custom-call | flops 268435456 | bytes 1835008 | tf_op jit(solution)/shard_map/pallas_call | solution.py:323
  142.0 1.6 %collective-permute-done.15.gu_ref = bf16[272,256]{1,0:T(8,128)(2,1)S(1)} collective-permute-done((bf16[272,256]{1,0:T(8,128)(2,1)S(1)}, bf16[272,256]{1,0:T(8,128)(2,1)S(1)}, u32[]{:S(2)}, u32[]{:S(2)}) %collective-permute-start.15) | collective-permute-done | bytes 139296 | tf_op jit(solution)/shard_map/ppermute | solution.py:354
  143.6 0.0 collective-permute-done.16.gd_ref
  143.6 0.8 shard_map.112
  (4 shorter events, 0.0 us)
Async XLA Ops:
  0.6 6.1 %copy-start.2 = (bf16[1024,256]{1,0:T(8,128)(2,1)S(1)}, bf16[1024,256]{1,0:T(8,128)(2,1)}, u32[]{:S(2)}) copy-start(bf16[1024,256]{1,0:T(8,128)(2,1)} %wr_ref.3) | copy-start | bytes 1572868
  0.6 6.1 %copy-start = (bf16[1,4,128,1024]{3,2,1,0:T(8,128)(2,1)S(1)}, bf16[1,4,128,1024]{3,2,1,0:T(8,128)(2,1)}, u32[]{:S(2)}) copy-start(bf16[1,4,128,1024]{3,2,1,0:T(8,128)(2,1)} %param.6) | copy-start | bytes 3145732
  0.7 25.7 %all-to-all-start.1 = ((bf16[16,32,1024]{2,1,0:T(8,128)(2,1)}), bf16[16,32,1024]{2,1,0:T(8,128)(2,1)}, u32[]{:S(2)}, u32[]{:S(2)}) async-start(bf16[16,32,1024]{2,1,0:T(8,128)(2,1)} %bitcast.22), calls=%async_computation.1 | async-start | bytes 2097152 | tf_op jit(solution)/shard_map/all_to_all | solution.py:396
  6.7 8.8 %copy-start.1 = (bf16[3,3,256,256]{3,2,1,0:T(8,128)(2,1)S(1)}, bf16[3,3,256,256]{3,2,1,0:T(8,128)(2,1)}, u32[]{:S(2)}) copy-start(bf16[3,3,256,256]{3,2,1,0:T(8,128)(2,1)} %ws_ref.7) | copy-start | bytes 3538948
  6.8 8.8 %copy-start.3 = (bf16[256,1024]{1,0:T(8,128)(2,1)S(1)}, bf16[256,1024]{1,0:T(8,128)(2,1)}, u32[]{:S(2)}) copy-start(bf16[256,1024]{1,0:T(8,128)(2,1)} %we_ref.5) | copy-start | bytes 1572868
  7.1 13.0 %collective-permute-start.1 = (bf16[128,256]{1,0:T(8,128)(2,1)S(1)}, bf16[128,256]{1,0:T(8,128)(2,1)S(1)}, u32[]{:S(2)}, u32[]{:S(2)}) collective-permute-start(bf16[128,256]{1,0:T(8,128)(2,1)S(1)} %get-tuple-element.40.first_ref), channel_id=1, source_target_pairs={{1,0},{2,1},{3,2},{4,3},{5,4},{6,5},{7,6},{8,7},{9,8},{10,9},{11,1... | collective-permute-start | bytes 196616 | tf_op jit(solution)/shard_map/ppermute | solution.py:340
  10.9 12.9 %collective-permute-start = (bf16[128,256]{1,0:T(8,128)(2,1)S(1)}, bf16[128,256]{1,0:T(8,128)(2,1)S(1)}, u32[]{:S(2)}, u32[]{:S(2)}) collective-permute-start(bf16[128,256]{1,0:T(8,128)(2,1)S(1)} %get-tuple-element.41.last_ref), channel_id=1, source_target_pairs={{0,1},{1,2},{2,3},{3,4},{4,5},{5,6},{6,7},{7,8},{8,9},{9,10},{10,1... | collective-permute-start | bytes 196616 | tf_op jit(solution)/shard_map/ppermute | solution.py:340
  24.7 1.0 copy-start.4
  25.6 0.7 copy-start.5
  26.4 21.2 %copy-start.7 = (s32[2,16]{1,0:T(2,128)S(1)}, s32[2,16]{1,0:T(2,128)}, u32[]{:S(2)}) copy-start(s32[2,16]{1,0:T(2,128)} %parts_ref.3) | copy-start | bytes 388
  75.1 27.0 %copy-start.6 = (bf16[6,128,256]{2,1,0:T(8,128)(2,1)S(1)}, bf16[6,128,256]{2,1,0:T(8,128)(2,1)}, u32[]{:S(2)}) copy-start(bf16[6,128,256]{2,1,0:T(8,128)(2,1)} %copy-done.5) | copy-start | bytes 1179652
  94.6 12.1 %collective-permute-start.2 = (bf16[128,256]{1,0:T(8,128)(2,1)S(1)}, bf16[128,256]{1,0:T(8,128)(2,1)S(1)}, u32[]{:S(2)}, u32[]{:S(2)}) collective-permute-start(bf16[128,256]{1,0:T(8,128)(2,1)S(1)} %get-tuple-element.54), channel_id=1, source_target_pairs={{0,1},{1,2},{2,3},{3,4},{4,5},{5,6},{6,7},{7,8},{8,9},{9,10},{10,1... | collective-permute-start | bytes 196616 | tf_op jit(solution)/shard_map/ppermute | solution.py:340
  99.8 8.6 %collective-permute-start.3 = (bf16[128,256]{1,0:T(8,128)(2,1)S(1)}, bf16[128,256]{1,0:T(8,128)(2,1)S(1)}, u32[]{:S(2)}, u32[]{:S(2)}) collective-permute-start(bf16[128,256]{1,0:T(8,128)(2,1)S(1)} %get-tuple-element.55), channel_id=1, source_target_pairs={{1,0},{2,1},{3,2},{4,3},{5,4},{6,5},{7,6},{8,7},{9,8},{10,9},{11,1... | collective-permute-start | bytes 196616 | tf_op jit(solution)/shard_map/ppermute | solution.py:340
  103.4 11.2 %collective-permute-start.4 = (bf16[208,256]{1,0:T(8,128)(2,1)S(1)}, bf16[208,256]{1,0:T(8,128)(2,1)S(1)}, u32[]{:S(2)}, u32[]{:S(2)}) collective-permute-start(bf16[208,256]{1,0:T(8,128)(2,1)S(1)} %get-tuple-element.59), channel_id=1, source_target_pairs={{0,2},{1,3},{2,4},{3,5},{4,6},{5,7},{6,8},{7,9},{8,10},{9,11},{10,... | collective-permute-start | bytes 319496 | tf_op jit(solution)/shard_map/ppermute | solution.py:354
  104.3 10.3 %collective-permute-start.5 = (bf16[208,256]{1,0:T(8,128)(2,1)S(1)}, bf16[208,256]{1,0:T(8,128)(2,1)S(1)}, u32[]{:S(2)}, u32[]{:S(2)}) collective-permute-start(bf16[208,256]{1,0:T(8,128)(2,1)S(1)} %get-tuple-element.60), channel_id=1, source_target_pairs={{0,14},{1,15},{2,0},{3,1},{4,2},{5,3},{6,4},{7,5},{8,6},{9,7},{10,... | collective-permute-start | bytes 319496 | tf_op jit(solution)/shard_map/ppermute | solution.py:354
  109.5 5.2 %collective-permute-start.6 = (bf16[64,256]{1,0:T(8,128)(2,1)S(1)}, bf16[64,256]{1,0:T(8,128)(2,1)S(1)}, u32[]{:S(2)}, u32[]{:S(2)}) collective-permute-start(bf16[64,256]{1,0:T(8,128)(2,1)S(1)} %get-tuple-element.61), channel_id=1, source_target_pairs={{0,2},{1,3},{2,4},{3,5},{4,6},{5,7},{6,8},{7,9},{8,10},{9,11},{10,... | collective-permute-start | bytes 98312 | tf_op jit(solution)/shard_map/ppermute | solution.py:354
  109.9 4.8 %collective-permute-start.7 = (bf16[64,256]{1,0:T(8,128)(2,1)S(1)}, bf16[64,256]{1,0:T(8,128)(2,1)S(1)}, u32[]{:S(2)}, u32[]{:S(2)}) collective-permute-start(bf16[64,256]{1,0:T(8,128)(2,1)S(1)} %get-tuple-element.62), channel_id=1, source_target_pairs={{0,14},{1,15},{2,0},{3,1},{4,2},{5,3},{6,4},{7,5},{8,6},{9,7},{10,... | collective-permute-start | bytes 98312 | tf_op jit(solution)/shard_map/ppermute | solution.py:354
  114.8 8.0 %collective-permute-start.9 = (bf16[2,272,256]{2,1,0:T(8,128)(2,1)S(1)}, bf16[2,272,256]{2,1,0:T(8,128)(2,1)S(1)}, u32[]{:S(2)}, u32[]{:S(2)}) collective-permute-start(bf16[2,272,256]{2,1,0:T(8,128)(2,1)S(1)} %get-tuple-element.64), channel_id=1, source_target_pairs={{0,2},{1,3},{2,4},{3,5},{4,6},{5,7},{6,8},{7,9},{8,10},{9,11},{10,... | collective-permute-start | bytes 835592 | tf_op jit(solution)/shard_map/ppermute | solution.py:354
  115.1 7.7 %collective-permute-start.10 = (bf16[2,272,256]{2,1,0:T(8,128)(2,1)S(1)}, bf16[2,272,256]{2,1,0:T(8,128)(2,1)S(1)}, u32[]{:S(2)}, u32[]{:S(2)}) collective-permute-start(bf16[2,272,256]{2,1,0:T(8,128)(2,1)S(1)} %get-tuple-element.65), channel_id=1, source_target_pairs={{0,14},{1,15},{2,0},{3,1},{4,2},{5,3},{6,4},{7,5},{8,6},{9,7},{10,... | collective-permute-start | bytes 835592 | tf_op jit(solution)/shard_map/ppermute | solution.py:354
  118.4 18.7 %collective-permute-start.8 = (bf16[3,272,256]{2,1,0:T(8,128)(2,1)S(1)}, bf16[3,272,256]{2,1,0:T(8,128)(2,1)S(1)}, u32[]{:S(2)}, u32[]{:S(2)}) collective-permute-start(bf16[3,272,256]{2,1,0:T(8,128)(2,1)S(1)} %get-tuple-element.63), channel_id=1, source_target_pairs={{0,1},{1,0},{2,3},{3,2},{4,5},{5,4},{6,7},{7,6},{8,9},{9,8},{10,11... | collective-permute-start | bytes 1253384 | tf_op jit(solution)/shard_map/ppermute | solution.py:354
  123.0 7.9 %collective-permute-start.11 = (bf16[272,256]{1,0:T(8,128)(2,1)S(1)}, bf16[272,256]{1,0:T(8,128)(2,1)S(1)}, u32[]{:S(2)}, u32[]{:S(2)}) collective-permute-start(bf16[272,256]{1,0:T(8,128)(2,1)S(1)} %get-tuple-element.66), channel_id=1, source_target_pairs={{0,2},{1,3},{2,4},{3,5},{4,6},{5,7},{6,8},{7,9},{8,10},{9,11},{10,... | collective-permute-start | bytes 417800 | tf_op jit(solution)/shard_map/ppermute | solution.py:354
  123.5 8.9 %collective-permute-start.12 = (bf16[272,256]{1,0:T(8,128)(2,1)S(1)}, bf16[272,256]{1,0:T(8,128)(2,1)S(1)}, u32[]{:S(2)}, u32[]{:S(2)}) collective-permute-start(bf16[272,256]{1,0:T(8,128)(2,1)S(1)} %get-tuple-element.67), channel_id=1, source_target_pairs={{0,3},{1,2},{2,5},{3,4},{4,7},{5,6},{6,9},{7,8},{8,11},{9,10},{10,... | collective-permute-start | bytes 417800 | tf_op jit(solution)/shard_map/ppermute | solution.py:354
  127.2 5.2 %collective-permute-start.13 = (bf16[272,256]{1,0:T(8,128)(2,1)S(1)}, bf16[272,256]{1,0:T(8,128)(2,1)S(1)}, u32[]{:S(2)}, u32[]{:S(2)}) collective-permute-start(bf16[272,256]{1,0:T(8,128)(2,1)S(1)} %get-tuple-element.68), channel_id=1, source_target_pairs={{0,14},{1,15},{2,0},{3,1},{4,2},{5,3},{6,4},{7,5},{8,6},{9,7},{10,... | collective-permute-start | bytes 417800 | tf_op jit(solution)/shard_map/ppermute | solution.py:354
  128.5 8.6 %collective-permute-start.14 = (bf16[272,256]{1,0:T(8,128)(2,1)S(1)}, bf16[272,256]{1,0:T(8,128)(2,1)S(1)}, u32[]{:S(2)}, u32[]{:S(2)}) collective-permute-start(bf16[272,256]{1,0:T(8,128)(2,1)S(1)} %get-tuple-element.69), channel_id=1, source_target_pairs={{0,15},{1,14},{2,1},{3,0},{4,3},{5,2},{6,5},{7,4},{8,7},{9,6},{10,... | collective-permute-start | bytes 417800 | tf_op jit(solution)/shard_map/ppermute | solution.py:354
  137.2 6.3 %collective-permute-start.15 = (bf16[272,256]{1,0:T(8,128)(2,1)S(1)}, bf16[272,256]{1,0:T(8,128)(2,1)S(1)}, u32[]{:S(2)}, u32[]{:S(2)}) collective-permute-start(bf16[272,256]{1,0:T(8,128)(2,1)S(1)} %get-tuple-element.70), channel_id=1, source_target_pairs={{0,2},{1,3},{2,4},{3,5},{4,6},{5,7},{6,8},{7,9},{8,10},{9,11},{10,... | collective-permute-start | bytes 417800 | tf_op jit(solution)/shard_map/ppermute | solution.py:354
  137.4 6.1 %collective-permute-start.16 = (bf16[272,256]{1,0:T(8,128)(2,1)S(1)}, bf16[272,256]{1,0:T(8,128)(2,1)S(1)}, u32[]{:S(2)}, u32[]{:S(2)}) collective-permute-start(bf16[272,256]{1,0:T(8,128)(2,1)S(1)} %get-tuple-element.71), channel_id=1, source_target_pairs={{0,14},{1,15},{2,0},{3,1},{4,2},{5,3},{6,4},{7,5},{8,6},{9,7},{10,... | collective-permute-start | bytes 417800 | tf_op jit(solution)/shard_map/ppermute | solution.py:354

commit v7 on v6

--- a/solution.py
+++ b/solution.py
@@ -245,33 +245,33 @@
         out_ref[index, rows:] = late_ref[block]
 
 
-def join_kernel(
-    offset, place_ref, early_ref, late_ref, eu, ed, lu, ld, up_ref, down_ref, near_ref
-):
-    rows = early_ref.shape[1]
-    depth = early_ref.shape[0] // 2
+def join_kernel(offset, place_ref, local_ref, gu_ref, gd_ref, up_ref, down_ref):
+    depth = local_ref.shape[0] // 2
+    for way, (sign, got_ref, out_ref) in enumerate(((1, gu_ref, up_ref), (-1, gd_ref, down_ref))):
+        block = 2 * ((place_ref[0] // 2 + sign * offset + depth) % depth)
+        out_ref[1 - way] = local_ref[block + 1 - way]
+        total = local_ref[block + way].astype(F32) + got_ref[...].astype(F32)
+        out_ref[way] = total.astype(BF16)
+
+
+def late_kernel(
+    offset, place_ref, early_ref, late_ref, gu_ref, gd_ref, up_ref, down_ref, near_ref
+):
+    join_kernel(offset, place_ref, late_ref, gu_ref, gd_ref, up_ref, down_ref)
     near_others(place_ref, early_ref, late_ref, near_ref)
-    for way, (sign, got, out_ref) in enumerate(((1, (eu, lu), up_ref), (-1, (ed, ld), down_ref))):
-        block = 2 * ((place_ref[0] // 2 + sign * offset + depth) % depth)
-        for side in range(2):
-            early, late = early_ref[block + side], late_ref[block + side]
-            if side == way:
-                early = (early.astype(F32) + got[0][...].astype(F32)).astype(BF16)
-                late = (late.astype(F32) + got[1][...].astype(F32)).astype(BF16)
-            out_ref[side, :rows] = early
-            out_ref[side, rows:] = late
-
-
-def pass_kernel(offset, split, place_ref, early_ref, late_ref, gu_ref, gd_ref, *outs):
+
+
+def cross_kernel(
+    offset, place_ref, early_ref, late_ref, eu_ref, ed_ref, lu_ref, ld_ref, us, uc, ds, dc
+):
     rows = early_ref.shape[1]
     depth = early_ref.shape[0] // 2
     z, half = place_ref[0] // 2, place_ref[0] % 2
-    for way, (sign, got_ref) in enumerate(((1, gu_ref), (-1, gd_ref))):
+    for sign, e_ref, l_ref, outs in ((1, eu_ref, lu_ref, (us, uc)), (-1, ed_ref, ld_ref, (ds, dc))):
         block = 2 * ((z + sign * offset + depth) % depth)
-        for index, side in enumerate((half, 1 - half) if split else (0, 1)):
-            early = early_ref[block + side].astype(F32) + got_ref[side, :rows].astype(F32)
-            late = late_ref[block + side].astype(F32) + got_ref[side, rows:].astype(F32)
-            target = outs[2 * way + index] if split else outs[way].at[side]
+        for side, target in zip((half, 1 - half), outs):
+            early = early_ref[block + side].astype(F32) + e_ref[side].astype(F32)
+            late = late_ref[block + side].astype(F32) + l_ref[side].astype(F32)
             target[:rows] = early.astype(BF16)
             target[rows:] = late.astype(BF16)
 
@@ -348,7 +348,9 @@
     swap = [(i, i ^ 1) for i in range(peers)]
     rows, mid = early.shape[1] + late.shape[1], early.shape[2]
     side = ((rows, mid), BF16)
-    pair = [((2, rows, mid), BF16)] * 2
+    near = ((3, rows, mid), BF16)
+    pairs = [[((2, *local.shape[1:]), BF16)] * 2 for local in (early, late)]
+    assert far == 4
 
     def sent(value, path):
         return lax.ppermute(value, "space", path)
@@ -356,21 +358,19 @@
     def moved(up, down):
         return sent(up, ups), sent(down, downs)
 
-    got = moved(*early_sends) + moved(*late_sends)
-    near = ((3, rows, mid), BF16)
+    early_got = moved(*early_sends)
+    late_got = moved(*late_sends)
     join = functools.partial(join_kernel, far - 1)
-    up, down, near = call(join, pair + [near], rows * mid, smem=1)(
-        place, early, late, *got
+    early_got = call(join, pairs[0], rows * mid, smem=1)(place, early, *early_got)
+    early_got = moved(*early_got)
+    join = functools.partial(late_kernel, far - 1)
+    *late_got, near = call(join, pairs[1] + [near], rows * mid, smem=1)(
+        place, early, late, *late_got
     )
-    up, down = moved(up, down)
+    late_got = moved(*late_got)
     near = sent(near, swap)
-    for step in range(3, far):
-        split = step == far - 1
-        kernel = functools.partial(pass_kernel, far + 1 - step, split)
-        outs = [side] * 4 if split else pair
-        got = call(kernel, outs, rows * mid, smem=1)(place, early, late, up, down)
-        if not split:
-            up, down = moved(*got)
+    cross = functools.partial(cross_kernel, far - 2)
+    got = call(cross, [side] * 4, rows * mid, smem=1)(place, early, late, *early_got, *late_got)
     uc = sent(got[1], [(i, j ^ 1) for i, j in ups])
     dc = sent(got[3], [(i, j ^ 1) for i, j in downs])
     us, ds = moved(got[0], got[2])

time: 145 us -> 148 us (1.021)
  the two profiles are of different devices: /device:TPU:6 before, /device:TPU:64 now
where the time goes in v7:
time: 148 us; the launch traced here: 147 us
  blocking collectives  62.6 us (42%)
  starting transfers between devices  42.3 us (29%)
  waiting for transfers between devices  28.2 us (19%)
  Pallas kernels  11.7 us (8%)
  local copies, waits for them, and re-layouts  1.74 us (1%)
    all_to_all x1, blocking collectives, step(): message = lax.all_to_all(message, ('dp', 'space'), 0, 0, tiled=True)  22.1 us
    all_to_all x1, blocking collectives, step(): s_all = lax.all_to_all(s_all, 'dp', 0, 0, tiled=True)  21.2 us
    ppermute x15, starting transfers between devices, sent(): return lax.ppermute(value, 'space', path)  20.9 us
    all_to_all x1, blocking collectives, step(): grads = lax.all_to_all(grads, 'dp', 0, 0, tiled=True)  19.2 us
    ppermute x15, waiting for transfers between devices, sent(): return lax.ppermute(value, 'space', path)  18.7 us
    ppermute x4, starting transfers between devices, exchanged(): return (lax.ppermute(last, 'space', up), lax.ppermute(first, 'space', down))  15.7 us
    pallas_call x13, Pallas kernels, run(): pl.pallas_call(kernel, out_shape=[jax.ShapeDtypeStruct(s, d) for s, d in...  11.4 us
    ppermute x4, waiting for transfers between devices, exchanged(): return (lax.ppermute(last, 'space', up), lax.ppermute(first, 'space', down))  9.43 us
  transfers between devices with their start and end apart: 20, of which 10 were waited for; matrix products, arithmetic and copies ran while one was open for 0% of the time, Pallas kernels for 4%

profile of v7, /device:TPU:64, one launch (start us, length us, event | category | flops | bytes accessed | tf_op | source)
XLA Modules:
  0.0 147.4 jit_solution(1529043402119219287)
XLA Ops:
  0.6 0.0 copy-start.2
  0.7 5.7 %all-to-all-start.1 = ((bf16[16,32,1024]{2,1,0:T(8,128)(2,1)}), bf16[16,32,1024]{2,1,0:T(8,128)(2,1)}, u32[]{:S(2)}, u32[]{:S(2)}) async-start(bf16[16,32,1024]{2,1,0:T(8,128)(2,1)} %bitcast.22), calls=%async_computation.1 | async-start | bytes 2097152 | tf_op jit(solution)/shard_map/all_to_all | solution.py:396
  6.4 0.0 copy-start.1
  6.4 0.0 copy-start.3
  6.4 0.3 edge.1
  6.7 4.3 %collective-permute-start.1 = (bf16[128,256]{1,0:T(8,128)(2,1)S(1)}, bf16[128,256]{1,0:T(8,128)(2,1)S(1)}, u32[]{:S(2)}, u32[]{:S(2)}) collective-permute-start(bf16[128,256]{1,0:T(8,128)(2,1)S(1)} %get-tuple-element.42.first_ref), channel_id=1, source_target_pairs={{1,0},{2,1},{3,2},{4,3},{5,4},{6,5},{7,6},{8,7},{9,8},{10,9},{11,1... | collective-permute-start | bytes 196616 | tf_op jit(solution)/shard_map/ppermute | solution.py:340
  11.0 3.2 %collective-permute-start = (bf16[128,256]{1,0:T(8,128)(2,1)S(1)}, bf16[128,256]{1,0:T(8,128)(2,1)S(1)}, u32[]{:S(2)}, u32[]{:S(2)}) collective-permute-start(bf16[128,256]{1,0:T(8,128)(2,1)S(1)} %get-tuple-element.43.last_ref), channel_id=1, source_target_pairs={{0,1},{1,2},{2,3},{3,4},{4,5},{5,6},{6,7},{7,8},{8,9},{9,10},{10,1... | collective-permute-start | bytes 196616 | tf_op jit(solution)/shard_map/ppermute | solution.py:340
  14.2 1.1 shard_map.101
  15.3 9.4 %collective-permute-done.1.below_ref = bf16[128,256]{1,0:T(8,128)(2,1)S(1)} collective-permute-done((bf16[128,256]{1,0:T(8,128)(2,1)S(1)}, bf16[128,256]{1,0:T(8,128)(2,1)S(1)}, u32[]{:S(2)}, u32[]{:S(2)}) %collective-permute-start.1) | collective-permute-done | bytes 65568 | tf_op jit(solution)/shard_map/ppermute | solution.py:340
  24.8 0.0 collective-permute-done.above_ref
  24.8 0.9 shard_map.102
  25.6 0.0 copy-start.4
  25.6 1.0 copy-done.4
  26.6 0.7 copy-done.5
  27.4 0.0 all-to-all-done.1.t_ref
  27.4 21.2 %all_to_all.26.s_ref = bf16[16,32,1024]{2,1,0:T(8,128)(2,1)S(1)} all-to-all(bf16[16,32,1024]{2,1,0:T(8,128)(2,1)} %copy-done.4), channel_id=1, replica_groups=mesh['dp'=16,'space'=16] {'dp'}, dimensions={0} | all-to-all | bytes 2097152 | tf_op jit(solution)/shard_map/all_to_all | solution.py:430
  48.6 0.0 copy-done.7
  48.6 2.1 %shard_map.103 = f32[256,128]{1,0:T(8,128)S(1)} custom-call(s32[2,16]{1,0:T(2,128)S(1)} %copy-done.7, bf16[16,32,1024]{2,1,0:T(8,128)(2,1)S(1)} %all_to_all.26.s_ref, bf16[16,32,1024]{2,1,0:T(8,128)(2,1)} %all-to-all-done.1.t_ref), custom_call_target="tpu_custom_call" | custom-call | flops 536870912 | bytes 2097280 | tf_op jit(solution)/shard_map/pallas_call | solution.py:323
  50.7 22.1 %all_to_all.27 = f32[256,1,128]{2,1,0:T(1,128)S(1)} all-to-all(f32[256,1,128]{2,1,0:T(1,128)S(1)} %bitcast.20), channel_id=1, replica_groups=mesh['dp'=16,'space'=16] {'dp','space'}, dimensions={0} | all-to-all | bytes 262144 | tf_op jit(solution)/shard_map/all_to_all | solution.py:433
  72.9 1.8 %shard_map.104 = (bf16[16,32,1024]{2,1,0:T(8,128)(2,1)S(1)}, f32[1,1]{1,0:T(1,128)}) custom-call(s32[2,16]{1,0:T(2,128)S(1)} %copy-done.7, f32[256,128]{1,0:T(8,128)S(1)} %bitcast.21, bf16[16,32,1024]{2,1,0:T(8,128)(2,1)S(1)} %all_to_all.26.s_ref), custom_call_target="tpu_custom_call" | custom-call | flops 16777216 | bytes 1179776 | tf_op jit(solution)/shard_map/pallas_call | solution.py:323
  74.6 19.2 %all_to_all.28.g_ref = bf16[16,32,1024]{2,1,0:T(8,128)(2,1)S(1)} all-to-all(bf16[16,32,1024]{2,1,0:T(8,128)(2,1)S(1)} %get-tuple-element.50), channel_id=1, replica_groups=mesh['dp'=16,'space'=16] {'dp'}, dimensions={0} | all-to-all | bytes 2097152 | tf_op jit(solution)/shard_map/all_to_all | solution.py:440
  93.8 0.5 shard_map.105
  94.3 3.2 %collective-permute-start.2 = (bf16[128,256]{1,0:T(8,128)(2,1)S(1)}, bf16[128,256]{1,0:T(8,128)(2,1)S(1)}, u32[]{:S(2)}, u32[]{:S(2)}) collective-permute-start(bf16[128,256]{1,0:T(8,128)(2,1)S(1)} %get-tuple-element.56), channel_id=1, source_target_pairs={{0,1},{1,2},{2,3},{3,4},{4,5},{5,6},{6,7},{7,8},{8,9},{9,10},{10,1... | collective-permute-start | bytes 196616 | tf_op jit(solution)/shard_map/ppermute | solution.py:340
  97.6 5.0 %collective-permute-start.3 = (bf16[128,256]{1,0:T(8,128)(2,1)S(1)}, bf16[128,256]{1,0:T(8,128)(2,1)S(1)}, u32[]{:S(2)}, u32[]{:S(2)}) collective-permute-start(bf16[128,256]{1,0:T(8,128)(2,1)S(1)} %get-tuple-element.57), channel_id=1, source_target_pairs={{1,0},{2,1},{3,2},{4,3},{5,4},{6,5},{7,6},{8,7},{9,8},{10,9},{11,1... | collective-permute-start | bytes 196616 | tf_op jit(solution)/shard_map/ppermute | solution.py:340
  102.6 0.0 copy-done.6
  102.6 1.4 shard_map.106
  104.0 0.7 collective-permute-start.7
  104.7 1.4 collective-permute-start.8
  106.1 0.0 collective-permute-done.2.above_ref
  106.1 0.0 collective-permute-done.3.below_ref
  106.1 1.1 shard_map.107
  107.2 0.7 collective-permute-start.4
  107.9 1.4 collective-permute-start.5
  109.3 1.9 %collective-permute-done.4.gu_ref = bf16[64,256]{1,0:T(8,128)(2,1)S(1)} collective-permute-done((bf16[64,256]{1,0:T(8,128)(2,1)S(1)}, bf16[64,256]{1,0:T(8,128)(2,1)S(1)}, u32[]{:S(2)}, u32[]{:S(2)}) %collective-permute-start.4) | collective-permute-done | bytes 32800 | tf_op jit(solution)/shard_map/ppermute | solution.py:356
  111.2 1.7 %collective-permute-done.5.gd_ref = bf16[64,256]{1,0:T(8,128)(2,1)S(1)} collective-permute-done((bf16[64,256]{1,0:T(8,128)(2,1)S(1)}, bf16[64,256]{1,0:T(8,128)(2,1)S(1)}, u32[]{:S(2)}, u32[]{:S(2)}) %collective-permute-start.5) | collective-permute-done | bytes 32800 | tf_op jit(solution)/shard_map/ppermute | solution.py:356
  112.9 2.7 %collective-permute-start.6 = (bf16[3,272,256]{2,1,0:T(8,128)(2,1)S(1)}, bf16[3,272,256]{2,1,0:T(8,128)(2,1)S(1)}, u32[]{:S(2)}, u32[]{:S(2)}) collective-permute-start(bf16[3,272,256]{2,1,0:T(8,128)(2,1)S(1)} %get-tuple-element.63), channel_id=1, source_target_pairs={{0,1},{1,0},{2,3},{3,2},{4,5},{5,4},{6,7},{7,6},{8,9},{9,8},{10,11... | collective-permute-start | bytes 1253384 | tf_op jit(solution)/shard_map/ppermute | solution.py:356
  115.6 0.0 collective-permute-done.7.gu_ref
  115.6 0.0 collective-permute-done.8.gd_ref
  115.6 0.1 shard_map.110
  115.7 1.4 collective-permute-start.9
  117.1 0.7 collective-permute-start.10
  117.8 1.3 collective-permute-start.11
  119.1 0.7 collective-permute-start.12
  119.9 3.1 %collective-permute-done.11.lu_ref = bf16[2,64,256]{2,1,0:T(8,128)(2,1)S(1)} collective-permute-done((bf16[2,64,256]{2,1,0:T(8,128)(2,1)S(1)}, bf16[2,64,256]{2,1,0:T(8,128)(2,1)S(1)}, u32[]{:S(2)}, u32[]{:S(2)}) %collective-permute-start.11) | collective-permute-done | bytes 65568 | tf_op jit(solution)/shard_map/ppermute | solution.py:356
  123.0 0.7 collective-permute-done.12.ld_ref
  123.6 0.0 collective-permute-done.9.eu_ref
  123.6 0.0 collective-permute-done.10.ed_ref
  123.7 0.1 shard_map.111
  123.8 2.3 %collective-permute-start.13 = (bf16[272,256]{1,0:T(8,128)(2,1)S(1)}, bf16[272,256]{1,0:T(8,128)(2,1)S(1)}, u32[]{:S(2)}, u32[]{:S(2)}) collective-permute-start(bf16[272,256]{1,0:T(8,128)(2,1)S(1)} %get-tuple-element.70), channel_id=1, source_target_pairs={{0,2},{1,3},{2,4},{3,5},{4,6},{5,7},{6,8},{7,9},{8,10},{9,11},{10,... | collective-permute-start | bytes 417800 | tf_op jit(solution)/shard_map/ppermute | solution.py:356
  126.1 3.2 %collective-permute-start.14 = (bf16[272,256]{1,0:T(8,128)(2,1)S(1)}, bf16[272,256]{1,0:T(8,128)(2,1)S(1)}, u32[]{:S(2)}, u32[]{:S(2)}) collective-permute-start(bf16[272,256]{1,0:T(8,128)(2,1)S(1)} %get-tuple-element.71), channel_id=1, source_target_pairs={{0,3},{1,2},{2,5},{3,4},{4,7},{5,6},{6,9},{7,8},{8,11},{9,10},{10,... | collective-permute-start | bytes 417800 | tf_op jit(solution)/shard_map/ppermute | solution.py:356
  129.3 1.3 collective-permute-start.15
  130.6 0.0 collective-permute-start.16
  130.6 0.0 collective-permute-done.13.us
  130.6 3.0 %collective-permute-done.14.uc = bf16[272,256]{1,0:T(8,128)(2,1)S(1)} collective-permute-done((bf16[272,256]{1,0:T(8,128)(2,1)S(1)}, bf16[272,256]{1,0:T(8,128)(2,1)S(1)}, u32[]{:S(2)}, u32[]{:S(2)}) %collective-permute-start.14) | collective-permute-done | bytes 139296 | tf_op jit(solution)/shard_map/ppermute | solution.py:356
  133.6 0.8 collective-permute-done.15.ds
  134.4 4.0 %collective-permute-done.16.dc = bf16[272,256]{1,0:T(8,128)(2,1)S(1)} collective-permute-done((bf16[272,256]{1,0:T(8,128)(2,1)S(1)}, bf16[272,256]{1,0:T(8,128)(2,1)S(1)}, u32[]{:S(2)}, u32[]{:S(2)}) %collective-permute-start.16) | collective-permute-done | bytes 139296 | tf_op jit(solution)/shard_map/ppermute | solution.py:356
  138.4 0.0 collective-permute-done.6.near_ref
  138.4 0.2 shard_map.112
  138.5 3.0 %collective-permute-start.17 = (bf16[272,256]{1,0:T(8,128)(2,1)S(1)}, bf16[272,256]{1,0:T(8,128)(2,1)S(1)}, u32[]{:S(2)}, u32[]{:S(2)}) collective-permute-start(bf16[272,256]{1,0:T(8,128)(2,1)S(1)} %get-tuple-element.74), channel_id=1, source_target_pairs={{0,2},{1,3},{2,4},{3,5},{4,6},{5,7},{6,8},{7,9},{8,10},{9,11},{10,... | collective-permute-start | bytes 417800 | tf_op jit(solution)/shard_map/ppermute | solution.py:356
  141.5 0.0 collective-permute-start.18
  141.6 1.4 shard_map.108
  143.0 1.2 collective-permute-done.17.gu_ref
  144.1 2.5 %collective-permute-done.18.gd_ref = bf16[272,256]{1,0:T(8,128)(2,1)S(1)} collective-permute-done((bf16[272,256]{1,0:T(8,128)(2,1)S(1)}, bf16[272,256]{1,0:T(8,128)(2,1)S(1)}, u32[]{:S(2)}, u32[]{:S(2)}) %collective-permute-start.18) | collective-permute-done | bytes 139296 | tf_op jit(solution)/shard_map/ppermute | solution.py:356
  146.6 0.8 shard_map.113
  (9 shorter events, 0.1 us)
Async XLA Ops:
  0.6 5.8 %copy-start.2 = (bf16[1024,256]{1,0:T(8,128)(2,1)S(1)}, bf16[1024,256]{1,0:T(8,128)(2,1)}, u32[]{:S(2)}) copy-start(bf16[1024,256]{1,0:T(8,128)(2,1)} %wr_ref.3) | copy-start | bytes 1572868
  0.6 5.8 %copy-start = (bf16[1,4,128,1024]{3,2,1,0:T(8,128)(2,1)S(1)}, bf16[1,4,128,1024]{3,2,1,0:T(8,128)(2,1)}, u32[]{:S(2)}) copy-start(bf16[1,4,128,1024]{3,2,1,0:T(8,128)(2,1)} %param.6) | copy-start | bytes 3145732
  0.7 26.7 %all-to-all-start.1 = ((bf16[16,32,1024]{2,1,0:T(8,128)(2,1)}), bf16[16,32,1024]{2,1,0:T(8,128)(2,1)}, u32[]{:S(2)}, u32[]{:S(2)}) async-start(bf16[16,32,1024]{2,1,0:T(8,128)(2,1)} %bitcast.22), calls=%async_computation.1 | async-start | bytes 2097152 | tf_op jit(solution)/shard_map/all_to_all | solution.py:396
  6.4 7.9 %copy-start.1 = (bf16[3,3,256,256]{3,2,1,0:T(8,128)(2,1)S(1)}, bf16[3,3,256,256]{3,2,1,0:T(8,128)(2,1)}, u32[]{:S(2)}) copy-start(bf16[3,3,256,256]{3,2,1,0:T(8,128)(2,1)} %ws_ref.7) | copy-start | bytes 3538948
  6.4 7.9 %copy-start.3 = (bf16[256,1024]{1,0:T(8,128)(2,1)S(1)}, bf16[256,1024]{1,0:T(8,128)(2,1)}, u32[]{:S(2)}) copy-start(bf16[256,1024]{1,0:T(8,128)(2,1)} %we_ref.5) | copy-start | bytes 1572868
  6.7 18.0 %collective-permute-start.1 = (bf16[128,256]{1,0:T(8,128)(2,1)S(1)}, bf16[128,256]{1,0:T(8,128)(2,1)S(1)}, u32[]{:S(2)}, u32[]{:S(2)}) collective-permute-start(bf16[128,256]{1,0:T(8,128)(2,1)S(1)} %get-tuple-element.42.first_ref), channel_id=1, source_target_pairs={{1,0},{2,1},{3,2},{4,3},{5,4},{6,5},{7,6},{8,7},{9,8},{10,9},{11,1... | collective-permute-start | bytes 196616 | tf_op jit(solution)/shard_map/ppermute | solution.py:340
  11.0 13.7 %collective-permute-start = (bf16[128,256]{1,0:T(8,128)(2,1)S(1)}, bf16[128,256]{1,0:T(8,128)(2,1)S(1)}, u32[]{:S(2)}, u32[]{:S(2)}) collective-permute-start(bf16[128,256]{1,0:T(8,128)(2,1)S(1)} %get-tuple-element.43.last_ref), channel_id=1, source_target_pairs={{0,1},{1,2},{2,3},{3,4},{4,5},{5,6},{6,7},{7,8},{8,9},{9,10},{10,1... | collective-permute-start | bytes 196616 | tf_op jit(solution)/shard_map/ppermute | solution.py:340
  25.6 1.0 copy-start.4
  26.6 0.8 copy-start.5
  27.4 21.2 %copy-start.7 = (s32[2,16]{1,0:T(2,128)S(1)}, s32[2,16]{1,0:T(2,128)}, u32[]{:S(2)}) copy-start(s32[2,16]{1,0:T(2,128)} %parts_ref.3) | copy-start | bytes 388
  74.6 28.0 %copy-start.6 = (bf16[6,128,256]{2,1,0:T(8,128)(2,1)S(1)}, bf16[6,128,256]{2,1,0:T(8,128)(2,1)}, u32[]{:S(2)}) copy-start(bf16[6,128,256]{2,1,0:T(8,128)(2,1)} %copy-done.5) | copy-start | bytes 1179652
  94.3 11.8 %collective-permute-start.2 = (bf16[128,256]{1,0:T(8,128)(2,1)S(1)}, bf16[128,256]{1,0:T(8,128)(2,1)S(1)}, u32[]{:S(2)}, u32[]{:S(2)}) collective-permute-start(bf16[128,256]{1,0:T(8,128)(2,1)S(1)} %get-tuple-element.56), channel_id=1, source_target_pairs={{0,1},{1,2},{2,3},{3,4},{4,5},{5,6},{6,7},{7,8},{8,9},{9,10},{10,1... | collective-permute-start | bytes 196616 | tf_op jit(solution)/shard_map/ppermute | solution.py:340
  97.6 8.6 %collective-permute-start.3 = (bf16[128,256]{1,0:T(8,128)(2,1)S(1)}, bf16[128,256]{1,0:T(8,128)(2,1)S(1)}, u32[]{:S(2)}, u32[]{:S(2)}) collective-permute-start(bf16[128,256]{1,0:T(8,128)(2,1)S(1)} %get-tuple-element.57), channel_id=1, source_target_pairs={{1,0},{2,1},{3,2},{4,3},{5,4},{6,5},{7,6},{8,7},{9,8},{10,9},{11,1... | collective-permute-start | bytes 196616 | tf_op jit(solution)/shard_map/ppermute | solution.py:340
  104.0 11.6 %collective-permute-start.7 = (bf16[208,256]{1,0:T(8,128)(2,1)S(1)}, bf16[208,256]{1,0:T(8,128)(2,1)S(1)}, u32[]{:S(2)}, u32[]{:S(2)}) collective-permute-start(bf16[208,256]{1,0:T(8,128)(2,1)S(1)} %get-tuple-element.64), channel_id=1, source_target_pairs={{0,2},{1,3},{2,4},{3,5},{4,6},{5,7},{6,8},{7,9},{8,10},{9,11},{10,... | collective-permute-start | bytes 319496 | tf_op jit(solution)/shard_map/ppermute | solution.py:356
  104.7 10.9 %collective-permute-start.8 = (bf16[208,256]{1,0:T(8,128)(2,1)S(1)}, bf16[208,256]{1,0:T(8,128)(2,1)S(1)}, u32[]{:S(2)}, u32[]{:S(2)}) collective-permute-start(bf16[208,256]{1,0:T(8,128)(2,1)S(1)} %get-tuple-element.65), channel_id=1, source_target_pairs={{0,14},{1,15},{2,0},{3,1},{4,2},{5,3},{6,4},{7,5},{8,6},{9,7},{10,... | collective-permute-start | bytes 319496 | tf_op jit(solution)/shard_map/ppermute | solution.py:356
  107.2 4.0 %collective-permute-start.4 = (bf16[64,256]{1,0:T(8,128)(2,1)S(1)}, bf16[64,256]{1,0:T(8,128)(2,1)S(1)}, u32[]{:S(2)}, u32[]{:S(2)}) collective-permute-start(bf16[64,256]{1,0:T(8,128)(2,1)S(1)} %get-tuple-element.61), channel_id=1, source_target_pairs={{0,2},{1,3},{2,4},{3,5},{4,6},{5,7},{6,8},{7,9},{8,10},{9,11},{10,... | collective-permute-start | bytes 98312 | tf_op jit(solution)/shard_map/ppermute | solution.py:356
  107.9 5.0 %collective-permute-start.5 = (bf16[64,256]{1,0:T(8,128)(2,1)S(1)}, bf16[64,256]{1,0:T(8,128)(2,1)S(1)}, u32[]{:S(2)}, u32[]{:S(2)}) collective-permute-start(bf16[64,256]{1,0:T(8,128)(2,1)S(1)} %get-tuple-element.62), channel_id=1, source_target_pairs={{0,14},{1,15},{2,0},{3,1},{4,2},{5,3},{6,4},{7,5},{8,6},{9,7},{10,... | collective-permute-start | bytes 98312 | tf_op jit(solution)/shard_map/ppermute | solution.py:356
  112.9 25.4 %collective-permute-start.6 = (bf16[3,272,256]{2,1,0:T(8,128)(2,1)S(1)}, bf16[3,272,256]{2,1,0:T(8,128)(2,1)S(1)}, u32[]{:S(2)}, u32[]{:S(2)}) collective-permute-start(bf16[3,272,256]{2,1,0:T(8,128)(2,1)S(1)} %get-tuple-element.63), channel_id=1, source_target_pairs={{0,1},{1,0},{2,3},{3,2},{4,5},{5,4},{6,7},{7,6},{8,9},{9,8},{10,11... | collective-permute-start | bytes 1253384 | tf_op jit(solution)/shard_map/ppermute | solution.py:356
  115.7 7.9 %collective-permute-start.9 = (bf16[2,208,256]{2,1,0:T(8,128)(2,1)S(1)}, bf16[2,208,256]{2,1,0:T(8,128)(2,1)S(1)}, u32[]{:S(2)}, u32[]{:S(2)}) collective-permute-start(bf16[2,208,256]{2,1,0:T(8,128)(2,1)S(1)} %get-tuple-element.66), channel_id=1, source_target_pairs={{0,2},{1,3},{2,4},{3,5},{4,6},{5,7},{6,8},{7,9},{8,10},{9,11},{10,... | collective-permute-start | bytes 638984 | tf_op jit(solution)/shard_map/ppermute | solution.py:356
  117.1 6.6 %collective-permute-start.10 = (bf16[2,208,256]{2,1,0:T(8,128)(2,1)S(1)}, bf16[2,208,256]{2,1,0:T(8,128)(2,1)S(1)}, u32[]{:S(2)}, u32[]{:S(2)}) collective-permute-start(bf16[2,208,256]{2,1,0:T(8,128)(2,1)S(1)} %get-tuple-element.67), channel_id=1, source_target_pairs={{0,14},{1,15},{2,0},{3,1},{4,2},{5,3},{6,4},{7,5},{8,6},{9,7},{10,... | collective-permute-start | bytes 638984 | tf_op jit(solution)/shard_map/ppermute | solution.py:356
  117.8 5.1 %collective-permute-start.11 = (bf16[2,64,256]{2,1,0:T(8,128)(2,1)S(1)}, bf16[2,64,256]{2,1,0:T(8,128)(2,1)S(1)}, u32[]{:S(2)}, u32[]{:S(2)}) collective-permute-start(bf16[2,64,256]{2,1,0:T(8,128)(2,1)S(1)} %get-tuple-element.68), channel_id=1, source_target_pairs={{0,2},{1,3},{2,4},{3,5},{4,6},{5,7},{6,8},{7,9},{8,10},{9,11},{10,... | collective-permute-start | bytes 196616 | tf_op jit(solution)/shard_map/ppermute | solution.py:356
  119.1 4.5 %collective-permute-start.12 = (bf16[2,64,256]{2,1,0:T(8,128)(2,1)S(1)}, bf16[2,64,256]{2,1,0:T(8,128)(2,1)S(1)}, u32[]{:S(2)}, u32[]{:S(2)}) collective-permute-start(bf16[2,64,256]{2,1,0:T(8,128)(2,1)S(1)} %get-tuple-element.69), channel_id=1, source_target_pairs={{0,14},{1,15},{2,0},{3,1},{4,2},{5,3},{6,4},{7,5},{8,6},{9,7},{10,... | collective-permute-start | bytes 196616 | tf_op jit(solution)/shard_map/ppermute | solution.py:356
  123.8 6.8 %collective-permute-start.13 = (bf16[272,256]{1,0:T(8,128)(2,1)S(1)}, bf16[272,256]{1,0:T(8,128)(2,1)S(1)}, u32[]{:S(2)}, u32[]{:S(2)}) collective-permute-start(bf16[272,256]{1,0:T(8,128)(2,1)S(1)} %get-tuple-element.70), channel_id=1, source_target_pairs={{0,2},{1,3},{2,4},{3,5},{4,6},{5,7},{6,8},{7,9},{8,10},{9,11},{10,... | collective-permute-start | bytes 417800 | tf_op jit(solution)/shard_map/ppermute | solution.py:356
  126.1 7.5 %collective-permute-start.14 = (bf16[272,256]{1,0:T(8,128)(2,1)S(1)}, bf16[272,256]{1,0:T(8,128)(2,1)S(1)}, u32[]{:S(2)}, u32[]{:S(2)}) collective-permute-start(bf16[272,256]{1,0:T(8,128)(2,1)S(1)} %get-tuple-element.71), channel_id=1, source_target_pairs={{0,3},{1,2},{2,5},{3,4},{4,7},{5,6},{6,9},{7,8},{8,11},{9,10},{10,... | collective-permute-start | bytes 417800 | tf_op jit(solution)/shard_map/ppermute | solution.py:356
  129.3 5.1 %collective-permute-start.15 = (bf16[272,256]{1,0:T(8,128)(2,1)S(1)}, bf16[272,256]{1,0:T(8,128)(2,1)S(1)}, u32[]{:S(2)}, u32[]{:S(2)}) collective-permute-start(bf16[272,256]{1,0:T(8,128)(2,1)S(1)} %get-tuple-element.72), channel_id=1, source_target_pairs={{0,14},{1,15},{2,0},{3,1},{4,2},{5,3},{6,4},{7,5},{8,6},{9,7},{10,... | collective-permute-start | bytes 417800 | tf_op jit(solution)/shard_map/ppermute | solution.py:356
  130.6 7.8 %collective-permute-start.16 = (bf16[272,256]{1,0:T(8,128)(2,1)S(1)}, bf16[272,256]{1,0:T(8,128)(2,1)S(1)}, u32[]{:S(2)}, u32[]{:S(2)}) collective-permute-start(bf16[272,256]{1,0:T(8,128)(2,1)S(1)} %get-tuple-element.73), channel_id=1, source_target_pairs={{0,15},{1,14},{2,1},{3,0},{4,3},{5,2},{6,5},{7,4},{8,7},{9,6},{10,... | collective-permute-start | bytes 417800 | tf_op jit(solution)/shard_map/ppermute | solution.py:356
  138.5 5.6 %collective-permute-start.17 = (bf16[272,256]{1,0:T(8,128)(2,1)S(1)}, bf16[272,256]{1,0:T(8,128)(2,1)S(1)}, u32[]{:S(2)}, u32[]{:S(2)}) collective-permute-start(bf16[272,256]{1,0:T(8,128)(2,1)S(1)} %get-tuple-element.74), channel_id=1, source_target_pairs={{0,2},{1,3},{2,4},{3,5},{4,6},{5,7},{6,8},{7,9},{8,10},{9,11},{10,... | collective-permute-start | bytes 417800 | tf_op jit(solution)/shard_map/ppermute | solution.py:356
  141.5 5.1 %collective-permute-start.18 = (bf16[272,256]{1,0:T(8,128)(2,1)S(1)}, bf16[272,256]{1,0:T(8,128)(2,1)S(1)}, u32[]{:S(2)}, u32[]{:S(2)}) collective-permute-start(bf16[272,256]{1,0:T(8,128)(2,1)S(1)} %get-tuple-element.75), channel_id=1, source_target_pairs={{0,14},{1,15},{2,0},{3,1},{4,2},{5,3},{6,4},{7,5},{8,6},{9,7},{10,... | collective-permute-start | bytes 417800 | tf_op jit(solution)/shard_map/ppermute | solution.py:356
